TPU v7x, 32 devices: a whole 2x2x4 slice. The times are simulated.
32 devices in a mesh: view: 4 (over x, core), samp: 8 (over z, y).
Axes of the slice: x: 2, y: 2, z: 4, core: 2. Of those that a mesh axis runs over, the one named last changes fastest.
Arguments:
- view_data: bfloat16 [8, 4096, 2048], P('view', 'samp'), may hold values from -10 to 10
- init_coeffs: float32 [8, 2048, 128], P('view'), may hold values from -0.125 to 0.125
Outputs:
- shared_scores: float32 [4096, 128], P('samp')
- final_coeffs: float32 [8, 2048, 128], P('view', 'samp')
All inputs are finite; a program needn't handle non-finite values.
Results may differ from a plain program's by a relative error of at most 0.005.
Values may be sent and summed in bfloat16 or wider, within the bound.
No kernel may reach another device: no remote copies, remote signals or barrier semaphores. Data moves between devices by JAX's collectives and lax.ppermute only.
A program may use at most 128 MiB of HBM per device.

v0:
```python
import jax
import jax.numpy as jnp
from jax import lax
from jax.sharding import PartitionSpec as P

OUTER = 2
INNER = 2
NS_ITERS = 12


HIGH = lax.Precision.HIGHEST
ridge_weight = 0.1
step_size = 0.5


def newton_inverse(gram):
    size_k = gram.shape[0]
    eye_mat = jnp.eye(size_k, dtype=jnp.float32)
    shrunk = gram + jnp.trace(gram) / size_k * eye_mat
    scale = jnp.sqrt(jnp.sum(shrunk * shrunk))
    approx = shrunk / scale
    inverse = eye_mat
    for turn in range(NS_ITERS):
        factor = 0.5 * (3.0 * eye_mat - jnp.dot(inverse, approx, precision=HIGH))
        approx = jnp.dot(approx, factor, precision=HIGH)
        inverse = jnp.dot(factor, inverse, precision=HIGH)
    return (inverse, scale)


def make_scores(view_data, coeffs_low, total):
    local_sum = jnp.zeros((view_data.shape[1], coeffs_low.shape[2]), jnp.float32)
    for member in range(view_data.shape[0]):
        local_sum = local_sum + jnp.dot(
            view_data[member], coeffs_low[member], preferred_element_type=jnp.float32
        )
    summed = lax.psum(local_sum, "view")
    gram = lax.psum(jnp.dot(summed.T, summed, precision=HIGH), "samp")
    inverse, scale = newton_inverse(gram)
    return jnp.dot(summed, inverse, precision=HIGH) * jnp.sqrt(total / scale)


def grad_term(samples, weights_low, scores):
    resid = (jnp.dot(samples, weights_low, preferred_element_type=jnp.float32) - scores).astype(
        jnp.bfloat16
    )
    return lax.dot_general(
        samples, resid, (((0,), (0,)), ((), ())), preferred_element_type=jnp.float32
    )


def body(view_data, init_coeffs):
    total = view_data.shape[1] * lax.axis_size("samp")
    row_count = init_coeffs.shape[1] // lax.axis_size("samp")
    row_start = lax.axis_index("samp") * row_count
    own_coeffs = lax.dynamic_slice_in_dim(init_coeffs, row_start, row_count, 1)
    coeffs_low = init_coeffs.astype(jnp.bfloat16)
    scores = make_scores(view_data, coeffs_low, total)
    for outer_step in range(OUTER):
        for inner_step in range(INNER):
            terms = jnp.stack(
                [
                    grad_term(view_data[member], coeffs_low[member], scores)
                    for member in range(view_data.shape[0])
                ]
            )
            summed_grad = lax.psum_scatter(terms, "samp", scatter_dimension=1, tiled=True)
            own_coeffs = own_coeffs - step_size * (summed_grad / total + ridge_weight * own_coeffs)
            coeffs_low = lax.all_gather(own_coeffs.astype(jnp.bfloat16), "samp", axis=1, tiled=True)
        scores = make_scores(view_data, coeffs_low, total)
    return (scores, own_coeffs)


def solution(mesh):
    in_specs = (P("view", "samp", None), P("view", None, None))
    out_specs = (P("samp", None), P("view", "samp", None))
    return jax.shard_map(body, mesh=mesh, in_specs=in_specs, out_specs=out_specs, check_vma=False)
```

profile of v0, /device:TPU:0, one launch (start us, length us, event | category | flops | bytes accessed | tf_op | source)
XLA Modules:
  0.0 856.1 jit_solution(11644975215844309981)
XLA Ops:
  9.1 2.3 fusion.12
  12.9 35.1 %all-reduce.7.cloned.1.call-done = f32[512,128]{1,0:T(8,128)} async-done(((f32[512,128]{1,0:T(8,128)}), f32[512,128]{1,0:T(8,128)}) %all-reduce.7.cloned.1.call-update) | async-done | bytes 262160 | tf_op jit(solution)/shard_map/psum | solution.py:36
  50.4 70.9 %all-reduce.9.cloned.1.call-done = f32[128,128]{1,0:T(8,128)} async-done(((f32[128,128]{1,0:T(8,128)}), f32[128,128]{1,0:T(8,128)}) %all-reduce.9.cloned.1.call-update) | async-done | bytes 65552 | tf_op jit(solution)/shard_map/psum | solution.py:37
  135.1 2.3 convolution_bitcast_fusion.6
  140.7 67.8 %reduce-scatter.5.cloned.1.call-done = f32[2,256,128]{1,2,0:T(8,128)} async-done(((f32[2,2048,128]{1,2,0:T(8,128)}), f32[2,256,128]{1,2,0:T(8,128)}) %reduce-scatter.5.cloned.1.call-update) | async-done | bytes 262160 | tf_op jit(solution)/shard_map/reduce_scatter | solution.py:66
  210.3 39.2 %all-gather.5.cloned.1.call-done = bf16[2,2048,128]{1,2,0:T(8,128)(2,1)} async-done(((bf16[2,256,128]{1,2,0:T(8,128)(2,1)}), bf16[2,2048,128]{1,2,0:T(8,128)(2,1)}) %all-gather.5.cloned.1.call-update) | async-done | bytes 1048592 | tf_op jit(solution)/shard_map/all_gather | solution.py:68
  249.5 4.0 convolution_bitcast_fusion.4
  253.4 4.0 convolution_bitcast_fusion.5
  259.0 68.0 %reduce-scatter.7.cloned.1.call-done = f32[2,256,128]{1,2,0:T(8,128)} async-done(((f32[2,2048,128]{1,2,0:T(8,128)}), f32[2,256,128]{1,2,0:T(8,128)}) %reduce-scatter.7.cloned.1.call-update) | async-done | bytes 262160 | tf_op jit(solution)/shard_map/reduce_scatter | solution.py:66
  328.7 39.1 %all-gather.7.cloned.1.call-done = bf16[2,2048,128]{1,2,0:T(8,128)(2,1)} async-done(((bf16[2,256,128]{1,2,0:T(8,128)(2,1)}), bf16[2,2048,128]{1,2,0:T(8,128)(2,1)}) %all-gather.7.cloned.1.call-update) | async-done | bytes 1048592 | tf_op jit(solution)/shard_map/all_gather | solution.py:68
  367.9 2.7 fusion.55
  370.6 3.1 fusion.164
  374.0 31.2 %all-reduce.11.cloned.1.call-done = f32[512,128]{0,1:T(8,128)} async-done(((f32[512,128]{0,1:T(8,128)}), f32[512,128]{0,1:T(8,128)}) %all-reduce.11.cloned.1.call-update) | async-done | bytes 262160 | tf_op jit(solution)/shard_map/psum | solution.py:36
  407.3 71.1 %all-reduce.13.cloned.1.call-done = f32[128,128]{1,0:T(8,128)} async-done(((f32[128,128]{1,0:T(8,128)}), f32[128,128]{1,0:T(8,128)}) %all-reduce.13.cloned.1.call-update) | async-done | bytes 65552 | tf_op jit(solution)/shard_map/psum | solution.py:37
  496.7 69.1 %reduce-scatter.9.cloned.1.call-done = f32[2,256,128]{1,2,0:T(8,128)} async-done(((f32[2,2048,128]{1,2,0:T(8,128)}), f32[2,256,128]{1,2,0:T(8,128)}) %reduce-scatter.9.cloned.1.call-update) | async-done | bytes 262160 | tf_op jit(solution)/shard_map/reduce_scatter | solution.py:66
  567.5 39.2 %all-gather.9.cloned.1.call-done = bf16[2,2048,128]{1,2,0:T(8,128)(2,1)} async-done(((bf16[2,256,128]{1,2,0:T(8,128)(2,1)}), bf16[2,2048,128]{1,2,0:T(8,128)(2,1)}) %all-gather.9.cloned.1.call-update) | async-done | bytes 1048592 | tf_op jit(solution)/shard_map/all_gather | solution.py:68
  606.7 3.6 convolution_bitcast_fusion
  610.3 3.6 convolution_bitcast_fusion.1
  615.5 68.0 %reduce-scatter.11.cloned.1.call-done = f32[2,256,128]{1,2,0:T(8,128)} async-done(((f32[2,2048,128]{1,2,0:T(8,128)}), f32[2,256,128]{1,2,0:T(8,128)}) %reduce-scatter.11.cloned.1.call-update) | async-done | bytes 262160 | tf_op jit(solution)/shard_map/reduce_scatter | solution.py:66
  685.3 39.1 %all-gather.11.cloned.1.call-done = bf16[2,2048,128]{1,2,0:T(8,128)(2,1)} async-done(((bf16[2,256,128]{1,2,0:T(8,128)(2,1)}), bf16[2,2048,128]{1,2,0:T(8,128)(2,1)}) %all-gather.11.cloned.1.call-update) | async-done | bytes 1048592 | tf_op jit(solution)/shard_map/all_gather | solution.py:68
  724.4 2.7 fusion
  727.1 3.1 fusion.46
  730.5 31.2 %all-reduce.15.cloned.1.call-done = f32[512,128]{0,1:T(8,128)} async-done(((f32[512,128]{0,1:T(8,128)}), f32[512,128]{0,1:T(8,128)}) %all-reduce.15.cloned.1.call-update) | async-done | bytes 262160 | tf_op jit(solution)/shard_map/psum | solution.py:36
  764.6 70.2 %all-reduce.17.cloned.1.call-done = f32[128,128]{1,0:T(8,128)} async-done(((f32[128,128]{1,0:T(8,128)}), f32[128,128]{1,0:T(8,128)}) %all-reduce.17.cloned.1.call-update) | async-done | bytes 65552 | tf_op jit(solution)/shard_map/psum | solution.py:37
  (181 shorter events, 66.2 us)
Async XLA Ops:
  7.2 40.9 %all-reduce.7.cloned.1.call-start = ((), (), s32[]{:S(2)}) async-start(), calls=%async_computation.4 | async-start | bytes 524288 | tf_op jit(solution)/shard_map/psum | solution.py:36
  7.2 4.2 copy-start
  12.9 108.4 %all-reduce.9.cloned.1.call-start = ((), (), s32[]{:S(2)}) async-start(), calls=%async_computation.5 | async-start | bytes 131072 | tf_op jit(solution)/shard_map/psum | solution.py:37
  50.3 158.2 %reduce-scatter.5.cloned.1.call-start = ((), (), s32[]{:S(2)}) async-start(), calls=%async_computation.6 | async-start | bytes 2359296 | tf_op jit(solution)/shard_map/reduce_scatter | solution.py:66
  130.2 4.5 copy-start.4
  134.7 2.8 copy-start.1
  139.6 109.9 %all-gather.5.cloned.1.call-start = ((), (), s32[]{:S(2)}) async-start(), calls=%async_computation.7 | async-start | bytes 1179648 | tf_op jit(solution)/shard_map/all_gather | solution.py:68
  210.2 116.8 %reduce-scatter.7.cloned.1.call-start = ((), (), s32[]{:S(2)}) async-start(), calls=%async_computation.8 | async-start | bytes 2359296 | tf_op jit(solution)/shard_map/reduce_scatter | solution.py:66
  258.9 68.1 %copy-start.6 = (f32[2,256,128]{1,2,0:T(8,128)S(1)}, f32[2,256,128]{1,2,0:T(8,128)}, u32[]{:S(2)}) copy-start(f32[2,256,128]{1,2,0:T(8,128)} %reduce-scatter.5.cloned.1.call-done) | copy-start | bytes 786436
  258.9 109.0 %all-gather.7.cloned.1.call-start = ((), (), s32[]{:S(2)}) async-start(), calls=%async_computation.9 | async-start | bytes 1179648 | tf_op jit(solution)/shard_map/all_gather | solution.py:68
  328.7 76.5 %all-reduce.11.cloned.1.call-start = ((), (), s32[]{:S(2)}) async-start(), calls=%async_computation.10 | async-start | bytes 524288 | tf_op jit(solution)/shard_map/psum | solution.py:36
  367.9 2.7 copy-start.8
  373.7 104.7 %all-reduce.13.cloned.1.call-start = ((), (), s32[]{:S(2)}) async-start(), calls=%async_computation.11 | async-start | bytes 131072 | tf_op jit(solution)/shard_map/psum | solution.py:37
  407.3 158.5 %reduce-scatter.9.cloned.1.call-start = ((), (), s32[]{:S(2)}) async-start(), calls=%async_computation.12 | async-start | bytes 2359296 | tf_op jit(solution)/shard_map/reduce_scatter | solution.py:66
  487.4 4.5 copy-start.5
  491.9 2.8 copy-start.2
  496.7 110.0 %all-gather.9.cloned.1.call-start = ((), (), s32[]{:S(2)}) async-start(), calls=%async_computation.13 | async-start | bytes 1179648 | tf_op jit(solution)/shard_map/all_gather | solution.py:68
  567.5 116.0 %reduce-scatter.11.cloned.1.call-start = ((), (), s32[]{:S(2)}) async-start(), calls=%async_computation.14 | async-start | bytes 2359296 | tf_op jit(solution)/shard_map/reduce_scatter | solution.py:66
  615.4 68.1 %copy-start.7 = (f32[2,256,128]{1,2,0:T(8,128)S(1)}, f32[2,256,128]{1,2,0:T(8,128)}, u32[]{:S(2)}) copy-start(f32[2,256,128]{1,2,0:T(8,128)} %reduce-scatter.9.cloned.1.call-done) | copy-start | bytes 786436
  615.4 109.0 %all-gather.11.cloned.1.call-start = ((), (), s32[]{:S(2)}) async-start(), calls=%async_computation.15 | async-start | bytes 1179648 | tf_op jit(solution)/shard_map/all_gather | solution.py:68
  685.2 76.5 %all-reduce.15.cloned.1.call-start = ((), (), s32[]{:S(2)}) async-start(), calls=%async_computation.16 | async-start | bytes 524288 | tf_op jit(solution)/shard_map/psum | solution.py:36
  724.4 2.7 copy-start.9
  730.3 104.6 %all-reduce.17.cloned.1.call-start = ((), (), s32[]{:S(2)}) async-start(), calls=%async_computation.17 | async-start | bytes 131072 | tf_op jit(solution)/shard_map/psum | solution.py:37
  843.8 4.5 copy-start.3
Sparse Core Ops, SparseCore 0:
  13.0 35.0 all-reduce.6
  52.0 69.2 all-reduce.8
  139.7 68.8 reduce-scatter.4
  211.0 38.3 all-gather.4
  259.0 67.8 reduce-scatter.6
  329.4 38.4 all-gather.6
  373.9 31.2 all-reduce.10
  409.2 69.2 all-reduce.12
  496.8 68.9 reduce-scatter.8
  568.2 38.3 all-gather.8
  615.6 67.9 reduce-scatter.10
  686.0 38.3 all-gather.10
  730.4 31.2 all-reduce.14
  765.6 69.2 all-reduce.16
where the time goes:
time: 857 us; the launch traced here: 856 us
  waiting for transfers between devices  740 us (86%)
  matrix products  70.7 us (8%)
  other arithmetic  23.3 us (3%)
  between operations  19.3 us (2%)
    reduce_scatter x4, waiting for transfers between devices, body(): lax.psum_scatter(terms, 'samp', scatter_dimension=1, tiled=True)  273 us
    psum x3, waiting for transfers between devices, make_scores(): gram = lax.psum(jnp.dot(summed.T, summed, precision=HIGH), 'samp')  212 us
    all_gather x4, waiting for transfers between devices, body(): lax.all_gather(own_coeffs.astype(jnp.bfloat16), 'samp', axis=1, tiled=True)  157 us
    psum x3, waiting for transfers between devices, make_scores(): summed = lax.psum(local_sum, 'view')  97.5 us
    dot_general x8, matrix products, grad_term(): lax.dot_general(samples, resid, (((0,), (0,)), ((), ())), preferred_eleme...  20.6 us
  transfers between devices with their start and end apart: 14, of which 14 were waited for; matrix products, arithmetic and copies ran while one was open for 0% of the time, Pallas kernels for 0%

commit v1 on v0

v1 whole, which is shorter than its diff:
```python
import jax
import jax.numpy as jnp
from jax import lax
from jax.sharding import PartitionSpec as P

OUTER = 2
INNER = 2
NS_ITERS = 12

HIGH = lax.Precision.HIGHEST
ridge_weight = 0.1
step_size = 0.5
AXES = ("view", "samp")
GROUP = 4


def newton_inverse(gram):
    size_k = gram.shape[0]
    eye_mat = jnp.eye(size_k, dtype=jnp.float32)
    shrunk = gram + jnp.trace(gram) / size_k * eye_mat
    scale = jnp.sqrt(jnp.sum(shrunk * shrunk))
    approx = shrunk / scale
    inverse = eye_mat
    for turn in range(NS_ITERS):
        factor = 0.5 * (3.0 * eye_mat - jnp.dot(inverse, approx, precision=HIGH))
        approx = jnp.dot(approx, factor, precision=HIGH)
        inverse = jnp.dot(factor, inverse, precision=HIGH)
    return (inverse, scale)


class Grid:
    def __init__(self, n_view, n_samp):
        self.planes, self.squares = n_view // 2, n_samp // GROUP
        self.n_samp = n_samp

    def encode(self, plane, core, square, corner):
        return (plane * 2 + core) * self.n_samp + square * GROUP + corner

    def each(self):
        for plane in range(self.planes):
            for core in range(2):
                for square in range(self.squares):
                    for corner in range(GROUP):
                        yield plane, core, square, corner

    def permute(self, value, target):
        pairs = [(self.encode(*at), self.encode(*target(*at))) for at in self.each()]
        return lax.ppermute(value, AXES, pairs)

    def swap_core(self, value):
        return self.permute(value, lambda a, c, q, p: (a, 1 - c, q, p))

    def sum_squares(self, value, wire):
        bit = 1
        while bit < self.squares:
            low = value.astype(wire)
            other = self.permute(low, lambda a, c, q, p, bit=bit: (a, c, q ^ bit, p))
            value = low.astype(jnp.float32) + other.astype(jnp.float32)
            bit *= 2
        return value

    def sum_planes(self, value):
        bit = 1
        while bit < self.planes:
            value = value + self.permute(value, lambda a, c, q, p, bit=bit: (a ^ bit, c, q, p))
            bit *= 2
        return value


def pick(parts, index):
    return lax.dynamic_index_in_dim(parts, index, 0, keepdims=False)


def body(view_data, init_coeffs):
    low = jnp.bfloat16
    grid = Grid(lax.axis_size("view"), lax.axis_size("samp"))
    rows, feats = view_data.shape[1:]
    comps = init_coeffs.shape[2]
    half_k, half_rows = comps // 2, rows // 2
    pooled = rows * GROUP
    total = rows * lax.axis_size("samp")
    view_at, samp_at = lax.axis_index("view"), lax.axis_index("samp")
    core = view_at % 2
    square, corner = samp_at // GROUP, samp_at % GROUP

    slots = []
    for k in range(GROUP):
        m = corner ^ k
        piece = lax.dynamic_slice(
            view_data, (m % 2, (m // 2) * half_rows, 0), (1, half_rows, feats)
        )[0]
        slots.append(
            grid.permute(
                piece,
                lambda a, c, q, p, k=k: (a, (p ^ k) // 2, q, 2 * c + (p ^ k) % 2),
            )
        )
    data = jnp.zeros((pooled, feats), low)
    for k in range(GROUP):
        source = (2 * core + corner % 2) ^ k
        other = grid.swap_core(slots[k])
        data = lax.dynamic_update_slice(data, slots[k], ((2 * source + core) * half_rows, 0))
        data = lax.dynamic_update_slice(
            data, other, ((2 * (source ^ 2) + 1 - core) * half_rows, 0)
        )

    local = jnp.transpose(pick(init_coeffs, corner % 2)).reshape(2, half_k, feats)
    from_core = grid.swap_core(pick(local, 1 - core))
    coeffs = jnp.where(core == corner // 2, pick(local, core), from_core)

    def whiten(pooled_sums):
        part = lax.dot_general(
            pooled_sums, pooled_sums, (((1,), (1,)), ((), ())), preferred_element_type=jnp.float32
        )
        gram = grid.sum_squares(part, jnp.float32)
        inverse, scale = newton_inverse(gram)
        return inverse * jnp.sqrt(total / scale)

    def half_scores(mixing, pooled_sums):
        own = lax.dynamic_slice_in_dim(mixing, core * half_k, half_k, 1)
        return lax.dot_general(
            own, pooled_sums.astype(jnp.float32), (((0,), (0,)), ((), ())), precision=HIGH
        )

    coeffs_low = init_coeffs.astype(low)
    part = jnp.zeros((comps, rows), jnp.float32)
    for member in range(view_data.shape[0]):
        part = part + lax.dot_general(
            coeffs_low[member],
            view_data[member],
            (((0,), (1,)), ((), ())),
            preferred_element_type=jnp.float32,
        )
    mine = lax.dynamic_slice_in_dim(part, core * half_rows, half_rows, 1)
    theirs = lax.dynamic_slice_in_dim(part, (1 - core) * half_rows, half_rows, 1)
    mine = grid.sum_planes(mine + grid.swap_core(theirs))
    square_groups = [
        [grid.encode(a, c, q, p) for p in range(GROUP) for c in range(2)]
        for a in range(grid.planes)
        for q in range(grid.squares)
    ]
    gathered = lax.all_to_all(
        jnp.broadcast_to(mine.astype(low), (2 * GROUP, comps, half_rows)),
        AXES, 0, 0, axis_index_groups=square_groups,
    )
    sums = jnp.transpose(gathered, (1, 0, 2)).reshape(comps, pooled)
    mixing = whiten(sums)
    scores = half_scores(mixing, sums)

    n_sub = GROUP * grid.planes
    sub = pooled // n_sub
    reduce_groups = [
        [grid.encode(a, c, q, p) for a in range(grid.planes) for p in range(GROUP)]
        for c in range(2)
        for q in range(grid.squares)
    ]
    gather_groups = [
        [
            grid.encode(a, c, q, p)
            for c in range(2)
            for a in range(grid.planes)
            for p in range(GROUP)
        ]
        for q in range(grid.squares)
    ]

    def product(weights):
        return lax.dot_general(
            weights.astype(low), data, (((1,), (1,)), ((), ())), preferred_element_type=jnp.float32
        )

    values = product(coeffs)
    for outer_step in range(OUTER):
        for inner_step in range(INNER):
            if inner_step > 0:
                values = product(coeffs)
            resid = (values - scores).astype(low)
            term = jnp.dot(resid, data, preferred_element_type=jnp.float32)
            grad = grid.sum_squares(term, low)
            coeffs = coeffs - step_size * (grad / total + ridge_weight * coeffs)
        values = product(coeffs)
        parts = jnp.transpose(values.astype(low).reshape(half_k, n_sub, sub), (1, 0, 2))
        parts = lax.all_to_all(parts, AXES, 0, 0, axis_index_groups=reduce_groups)
        own = jnp.sum(parts.astype(jnp.float32), axis=0).astype(low)
        gathered = lax.all_to_all(
            jnp.broadcast_to(own, (2 * n_sub, half_k, sub)),
            AXES, 0, 0, axis_index_groups=gather_groups,
        )
        sums = jnp.transpose(gathered.reshape(2, n_sub, half_k, sub), (0, 2, 1, 3)).reshape(
            comps, pooled
        )
        mixing = whiten(sums)
        if outer_step < OUTER - 1:
            scores = half_scores(mixing, sums)
    block = lax.dynamic_slice_in_dim(sums, corner * rows, rows, 1).astype(jnp.float32)
    shared = lax.dot_general(block, mixing, (((0,), (0,)), ((), ())), precision=HIGH)

    out_rows = feats // lax.axis_size("samp")
    pieces = []
    for k in range(GROUP):
        corner_to = (2 * core + corner % 2) ^ k
        piece = lax.dynamic_slice_in_dim(
            coeffs, (square * GROUP + corner_to) * out_rows, out_rows, 1
        )
        pieces.append(
            grid.permute(
                piece,
                lambda a, c, q, p, k=k: (a, p // 2, q, (2 * c + p % 2) ^ k),
            )
        )
    pieces = jnp.stack(pieces)
    ordered = [pick(pieces, corner ^ r) for r in range(GROUP)]
    final = jnp.stack(
        [jnp.concatenate([ordered[member], ordered[2 + member]], axis=0).T for member in range(2)]
    )
    return (shared, final)


def solution(mesh):
    in_specs = (P("view", "samp", None), P("view", None, None))
    out_specs = (P("samp", None), P("view", "samp", None))
    return jax.shard_map(body, mesh=mesh, in_specs=in_specs, out_specs=out_specs, check_vma=False)
```

time: 857 us -> 300 us (0.35)
  waiting for transfers between devices: 740 us -> 105 us
  starting transfers between devices: 0.98 us -> 37.6 us
  blocking collectives: 0 us -> 33 us
  local copies, waits for them, and re-layouts: 2.29 us -> 32.5 us
  other arithmetic: 23.3 us -> 6.19 us
  between operations: 19.3 us -> 6.28 us
    psum x6 -> x0, waiting for transfers between devices: 310 us -> none  [the longest x3 212 us: make_scores(): gram = lax.psum(jnp.dot(summed.T, summed, precision=HIGH), 'samp')]
    reduce_scatter x4 -> x0, waiting for transfers between devices: 273 us -> none  [body(): lax.psum_scatter(terms, 'samp', scatter_dimension=1, tiled=True)]
    all_gather x4 -> x0, waiting for transfers between devices: 157 us -> none  [body(): lax.all_gather(own_coeffs.astype(jnp.bfloat16), 'samp', axis=1, tiled=True)]
    ppermute x0 -> x22, waiting for transfers between devices: none -> 105 us  [permute(): return lax.ppermute(value, AXES, pairs)]
    all_to_all x0 -> x3, blocking collectives: none -> 33 us  [the longest x2 20.3 us: body(): parts = lax.all_to_all(parts, AXES, 0, 0, axis_index_groups=reduce_groups)]
    ppermute x0 -> x22, starting transfers between devices: none -> 29.6 us  [permute(): return lax.ppermute(value, AXES, pairs)]
    dynamic_update_slice x0 -> x8, local copies, waits for them, and re-layouts: none -> 18.6 us  [the longest x4 9.36 us: body(): lax.dynamic_update_slice(data, other, ((2 * (source ^ 2) + 1 - core) * ha...]
    dot_general x20 -> x14, matrix products: 44.3 us -> 56 us  [the longest x4 34.8 us: body(): term = jnp.dot(resid, data, preferred_element_type=jnp.float32)]
  transfers between devices with their start and end apart: 14 -> 24, of which waited for: 14 -> 14; matrix products, arithmetic and copies ran while one was open for 0% -> 14% of each run, Pallas kernels for 0% -> 0%
where the time goes in v1:
time: 300 us; the launch traced here: 298 us
  waiting for transfers between devices  105 us (35%)
  matrix products  77.5 us (26%)
  starting transfers between devices  37.6 us (13%)
  blocking collectives  33 us (11%)
  local copies, waits for them, and re-layouts  32.5 us (11%)
  between operations  6.28 us (2%)
  other arithmetic  6.19 us (2%)
    ppermute x22, waiting for transfers between devices, permute(): return lax.ppermute(value, AXES, pairs)  105 us
    dot_general x4, matrix products, body(): term = jnp.dot(resid, data, preferred_element_type=jnp.float32)  34.8 us
    ppermute x22, starting transfers between devices, permute(): return lax.ppermute(value, AXES, pairs)  29.6 us
    all_to_all x2, blocking collectives, body(): parts = lax.all_to_all(parts, AXES, 0, 0, axis_index_groups=reduce_groups)  20.3 us
    all_to_all x1, blocking collectives, body(): lax.all_to_all(jnp.broadcast_to(own, (2 * n_sub, half_k, sub)), AXES, 0,...  12.6 us
    dot_general x2, matrix products, product(): lax.dot_general(weights.astype(low), data, (((1,), (1,)), ((), ())), pref...  12.1 us
    dynamic_update_slice x4, local copies, waits for them, and re-layouts, body(): lax.dynamic_update_slice(data, other, ((2 * (source ^ 2) + 1 - core) * ha...  9.36 us
    dynamic_update_slice x4, local copies, waits for them, and re-layouts, body(): lax.dynamic_update_slice(data, slots[k], ((2 * source + core) * half_rows...  9.26 us
  transfers between devices with their start and end apart: 24, of which 14 were waited for; matrix products, arithmetic and copies ran while one was open for 14% of the time, Pallas kernels for 0%

profile of v1, /device:TPU:0, one launch (start us, length us, event | category | flops | bytes accessed | tf_op | source)
XLA Modules:
  0.0 298.5 jit_solution(13139701067191949190)
XLA Ops:
  16.6 4.1 %all-to-all-start = ((bf16[8,128,256]{2,1,0:T(8,128)(2,1)}), bf16[8,128,256]{2,1,0:T(8,128)(2,1)}, u32[]{:S(2)}, u32[]{:S(2)}) async-start(bf16[8,128,256]{2,1,0:T(8,128)(2,1)} %broadcast_in_dim.17), calls=%async_computation | async-start | bytes 1048576 | tf_op jit(solution)/shard_map/all_to_all | solution.py:142
  20.7 4.4 %dynamic-slice_bitcast_fusion = (bf16[256,2048]{1,0:T(8,128)(2,1)}, bf16[256,2048]{1,0:T(8,128)(2,1)}, bf16[256,2048]{1,0:T(8,128)(2,1)}, bf16[256,2048]{1,0:T(8,128)(2,1)}) fusion(bf16[2,512,2048]{2,1,0:T(8,128)(2,1)} %param.2, s32[]{:T(128)S(6)} %select_n.201, s32[]{:T(128)S(6)} %select_n.203, s32[]{:T(128)S(6)} %select_n.195, s32[]{:T(128)S(6)} %select_n.197, ...), kind=kLoop, calls=%fused_computation.92 | loop fusion | bytes 8388640 | tf_op jit(solution)/shard_map/squeeze | solution.py:89
  25.1 9.5 %collective-permute-start.1 = (bf16[256,2048]{1,0:T(8,128)(2,1)}, bf16[256,2048]{1,0:T(8,128)(2,1)}, u32[]{:S(2)}, u32[]{:S(2)}) collective-permute-start(bf16[256,2048]{1,0:T(8,128)(2,1)} %get-tuple-element.17), channel_id=1, source_target_pairs={{0,0},{1,1},{2,8},{3,9},{4,4},{5,5},{6,12},{7,13},{8,2},{9,3},{10,... | collective-permute-start | bytes 3145736 | tf_op jit(solution)/shard_map/ppermute | solution.py:48
  42.7 4.3 %broadcast_in_dim.16 = bf16[2048,2048]{1,0:T(8,128)(2,1)} broadcast(bf16[]{:T(256)} %constant.166.clone.1), dimensions={} | broadcast | bytes 8388610 | tf_op jit(solution)/shard_map/broadcast_in_dim | solution.py:98
  50.6 10.3 %collective-permute-done.3 = bf16[256,2048]{1,0:T(8,128)(2,1)} collective-permute-done((bf16[256,2048]{1,0:T(8,128)(2,1)}, bf16[256,2048]{1,0:T(8,128)(2,1)}, u32[]{:S(2)}, u32[]{:S(2)}) %collective-permute-start.3) | collective-permute-done | bytes 1048608 | tf_op jit(solution)/shard_map/ppermute | solution.py:48
  60.9 5.2 %collective-permute-done.5 = bf16[256,2048]{1,0:T(8,128)(2,1)} collective-permute-done((bf16[256,2048]{1,0:T(8,128)(2,1)}, bf16[256,2048]{1,0:T(8,128)(2,1)}, u32[]{:S(2)}, u32[]{:S(2)}) %collective-permute-start.5) | collective-permute-done | bytes 1048608 | tf_op jit(solution)/shard_map/ppermute | solution.py:48
  66.1 16.7 %collective-permute-done.7 = bf16[256,2048]{1,0:T(8,128)(2,1)} collective-permute-done((bf16[256,2048]{1,0:T(8,128)(2,1)}, bf16[256,2048]{1,0:T(8,128)(2,1)}, u32[]{:S(2)}, u32[]{:S(2)}) %collective-permute-start.7) | collective-permute-done | bytes 1048608 | tf_op jit(solution)/shard_map/ppermute | solution.py:48
  110.5 9.9 %convolution_convert_fusion.4 = bf16[64,2048]{1,0:T(8,128)(2,1)S(1)} fusion(bf16[2048,2048]{1,0:T(8,128)(2,1)} %constant_dynamic-update-slice_fusion, f32[64,2048]{1,0:T(8,128)S(1)} %fusion.66, f32[64,2048]{1,0:T(8,128)S(1)} %collective-permute-done, f32[2,64,2048]{2,1,0:T(8,128)S(1)} %bitcast.308, s32[]{:T(128)S(6)} %select_n.182, pred[]{:T(512)S(6)} %eq.122), kind=kOutput, calls=%fused_computation.10 | convolution fusion | flops 1074266112 | bytes 18350084 | tf_op jit(solution)/shard_map/dot_general | solution.py:178
  123.2 12.5 %collective-permute-done.12 = bf16[64,2048]{1,0:T(8,128)(2,1)S(1)} collective-permute-done((bf16[64,2048]{1,0:T(8,128)(2,1)S(1)}, bf16[64,2048]{1,0:T(8,128)(2,1)S(1)}, u32[]{:S(2)}, u32[]{:S(2)}) %collective-permute-start.12) | collective-permute-done | bytes 262176 | tf_op jit(solution)/shard_map/ppermute | solution.py:48
  135.9 10.1 %convolution_convert_fusion.3 = bf16[64,2048]{1,0:T(8,128)(2,1)S(1)} fusion(bf16[2048,2048]{1,0:T(8,128)(2,1)} %constant_dynamic-update-slice_fusion, f32[64,2048]{1,0:T(8,128)S(1)} %fusion.66, f32[64,2048]{1,0:T(8,128)S(1)} %multiply_subtract_fusion.3), kind=kOutput, calls=%fused_computation.9 | convolution fusion | flops 1074266112 | bytes 9699328 | tf_op jit(solution)/shard_map/dot_general | solution.py:178
  146.0 14.4 %collective-permute-done.13 = bf16[64,2048]{1,0:T(8,128)(2,1)S(1)} collective-permute-done((bf16[64,2048]{1,0:T(8,128)(2,1)S(1)}, bf16[64,2048]{1,0:T(8,128)(2,1)S(1)}, u32[]{:S(2)}, u32[]{:S(2)}) %collective-permute-start.13) | collective-permute-done | bytes 262176 | tf_op jit(solution)/shard_map/ppermute | solution.py:48
  160.4 6.0 %fusion.93 = (bf16[64,2048]{1,0:T(8,128)(2,1)S(1)}, f32[64,2048]{1,0:T(8,128)S(1)}) fusion(bf16[2048,2048]{1,0:T(8,128)(2,1)} %constant_dynamic-update-slice_fusion, f32[64,2048]{1,0:T(8,128)S(1)} %multiply_subtract_fusion.3, bf16[64,2048]{1,0:T(8,128)(2,1)S(1)} %collective-permute-done.13, bf16[64,2048]{1,0:T(8,128)(2,1)S(1)} %convolution_convert_fusion.3), kind=kOutput, calls=%fused_computation.178 | convolution fusion | flops 538181632 | bytes 10223616 | tf_op jit(solution)/shard_map/dot_general | solution.py:168
  166.5 10.9 %all_to_all.25 = bf16[8,64,256]{2,1,0:T(8,128)(2,1)S(1)} all-to-all(bf16[8,64,256]{2,1,0:T(8,128)(2,1)S(1)} %bitcast.317), channel_id=1, replica_groups={{0,1,2,3,16,17,18,19},{4,5,6,7,20,21,22,23},{8,9,10,11,24,25,26,27},{12..., dimensions={0} | all-to-all | bytes 524288 | tf_op jit(solution)/shard_map/all_to_all | solution.py:183
  177.5 12.6 %all_to_all.26 = bf16[16,64,256]{2,1,0:T(8,128)(2,1)S(1)} all-to-all(bf16[16,64,256]{2,1,0:T(8,128)(2,1)S(1)} %broadcast_in_dim.18), channel_id=1, replica_groups={{0,1,2,3,16,17,18,19,8,9,10,11,24,25,26,27},{4,5,6,7,20,21,22,23,12,13,..., dimensions={0} | all-to-all | bytes 1048576 | tf_op jit(solution)/shard_map/all_to_all | solution.py:185
  192.3 4.9 %collective-permute-done.14 = f32[128,128]{1,0:T(8,128)S(1)} collective-permute-done((f32[128,128]{1,0:T(8,128)S(1)}, f32[128,128]{1,0:T(8,128)S(1)}, u32[]{:S(2)}, u32[]{:S(2)}) %collective-permute-start.14) | collective-permute-done | bytes 65568 | tf_op jit(solution)/shard_map/ppermute | solution.py:48
  207.7 4.9 %convolution_convert_fusion.2 = bf16[64,2048]{1,0:T(8,128)(2,1)S(1)} fusion(bf16[2048,2048]{1,0:T(8,128)(2,1)} %constant_dynamic-update-slice_fusion, f32[64,2048]{1,0:T(8,128)S(1)} %get-tuple-element.27, f32[64,2048]{1,0:T(8,128)S(1)} %fusion.65), kind=kOutput, calls=%fused_computation.8 | convolution fusion | flops 537264128 | bytes 9699328 | tf_op jit(solution)/shard_map/dot_general | solution.py:178
  213.1 11.8 %collective-permute-done.15 = bf16[64,2048]{1,0:T(8,128)(2,1)S(1)} collective-permute-done((bf16[64,2048]{1,0:T(8,128)(2,1)S(1)}, bf16[64,2048]{1,0:T(8,128)(2,1)S(1)}, u32[]{:S(2)}, u32[]{:S(2)}) %collective-permute-start.15) | collective-permute-done | bytes 262176 | tf_op jit(solution)/shard_map/ppermute | solution.py:48
  224.9 9.9 %convolution_convert_fusion.1 = bf16[64,2048]{1,0:T(8,128)(2,1)S(1)} fusion(bf16[2048,2048]{1,0:T(8,128)(2,1)} %constant_dynamic-update-slice_fusion, f32[64,2048]{1,0:T(8,128)S(1)} %fusion.65, bf16[64,2048]{1,0:T(8,128)(2,1)S(1)} %collective-permute-done.15, bf16[64,2048]{1,0:T(8,128)(2,1)S(1)} %convolution_convert_fusion.2, ...), kind=kOutput, calls=%fused_computation.7 | convolution fusion | flops 1076363264 | bytes 10747904 | tf_op jit(solution)/shard_map/dot_general | solution.py:178
  234.9 13.1 %collective-permute-done.16 = bf16[64,2048]{1,0:T(8,128)(2,1)S(1)} collective-permute-done((bf16[64,2048]{1,0:T(8,128)(2,1)S(1)}, bf16[64,2048]{1,0:T(8,128)(2,1)S(1)}, u32[]{:S(2)}, u32[]{:S(2)}) %collective-permute-start.16) | collective-permute-done | bytes 262176 | tf_op jit(solution)/shard_map/ppermute | solution.py:48
  248.5 6.0 %convolution_convert_fusion = bf16[64,2048]{1,0:T(8,128)(2,1)S(1)} fusion(bf16[2048,2048]{1,0:T(8,128)(2,1)} %constant_dynamic-update-slice_fusion, f32[64,2048]{1,0:T(8,128)S(1)} %multiply_subtract_fusion), kind=kOutput, calls=%fused_computation.6 | convolution fusion | flops 537133056 | bytes 9175040 | tf_op jit(solution)/shard_map/dot_general | solution.py:168
  254.5 9.4 %all_to_all.27 = bf16[8,64,256]{2,1,0:T(8,128)(2,1)S(1)} all-to-all(bf16[8,64,256]{2,1,0:T(8,128)(2,1)S(1)} %bitcast.318), channel_id=1, replica_groups={{0,1,2,3,16,17,18,19},{4,5,6,7,20,21,22,23},{8,9,10,11,24,25,26,27},{12..., dimensions={0} | all-to-all | bytes 524288 | tf_op jit(solution)/shard_map/all_to_all | solution.py:183
  264.8 3.8 %all-to-all-start.4 = ((bf16[16,64,256]{2,1,0:T(8,128)(2,1)}), bf16[16,64,256]{2,1,0:T(8,128)(2,1)S(1)}, u32[]{:S(2)}, u32[]{:S(2)}) async-start(bf16[16,64,256]{2,1,0:T(8,128)(2,1)} %broadcast_in_dim.19), calls=%async_computation.4 | async-start | bytes 1048576 | tf_op jit(solution)/shard_map/all_to_all | solution.py:185
  272.8 4.0 %collective-permute-done.21 = f32[64,256]{1,0:T(8,128)S(1)} collective-permute-done((f32[64,256]{1,0:T(8,128)S(1)}, f32[64,256]{1,0:T(8,128)S(1)}, u32[]{:S(2)}, u32[]{:S(2)}) %collective-permute-start.21) | collective-permute-done | bytes 65568 | tf_op jit(solution)/shard_map/ppermute | solution.py:48
  283.4 4.0 %collective-permute-done.17 = f32[128,128]{1,0:T(8,128)S(1)} collective-permute-done((f32[128,128]{1,0:T(8,128)S(1)}, f32[128,128]{1,0:T(8,128)S(1)}, u32[]{:S(2)}, u32[]{:S(2)}) %collective-permute-start.17) | collective-permute-done | bytes 65568 | tf_op jit(solution)/shard_map/ppermute | solution.py:48
  (191 shorter events, 89.3 us)
Async XLA Ops:
  7.4 1.5 collective-permute-start.9
  9.0 6.7 %collective-permute-start.10 = (f32[128,256]{1,0:T(8,128)S(1)}, f32[128,256]{1,0:T(8,128)S(1)}, u32[]{:S(2)}, u32[]{:S(2)}) collective-permute-start(f32[128,256]{1,0:T(8,128)S(1)} %dynamic-slice_add_fusion), channel_id=1, source_target_pairs={{0,16},{1,17},{2,18},{3,19},{4,20},{5,21},{6,22},{7,23},{8,24},{9,... | collective-permute-start | bytes 393224 | tf_op jit(solution)/shard_map/ppermute | solution.py:48
  16.6 21.7 %all-to-all-start = ((bf16[8,128,256]{2,1,0:T(8,128)(2,1)}), bf16[8,128,256]{2,1,0:T(8,128)(2,1)}, u32[]{:S(2)}, u32[]{:S(2)}) async-start(bf16[8,128,256]{2,1,0:T(8,128)(2,1)} %broadcast_in_dim.17), calls=%async_computation | async-start | bytes 1048576 | tf_op jit(solution)/shard_map/all_to_all | solution.py:142
  25.1 14.7 %collective-permute-start.1 = (bf16[256,2048]{1,0:T(8,128)(2,1)}, bf16[256,2048]{1,0:T(8,128)(2,1)}, u32[]{:S(2)}, u32[]{:S(2)}) collective-permute-start(bf16[256,2048]{1,0:T(8,128)(2,1)} %get-tuple-element.17), channel_id=1, source_target_pairs={{0,0},{1,1},{2,8},{3,9},{4,4},{5,5},{6,12},{7,13},{8,2},{9,3},{10,... | collective-permute-start | bytes 3145736 | tf_op jit(solution)/shard_map/ppermute | solution.py:48
  34.6 26.4 %collective-permute-start.3 = (bf16[256,2048]{1,0:T(8,128)(2,1)}, bf16[256,2048]{1,0:T(8,128)(2,1)}, u32[]{:S(2)}, u32[]{:S(2)}) collective-permute-start(bf16[256,2048]{1,0:T(8,128)(2,1)} %get-tuple-element.16), channel_id=1, source_target_pairs={{0,1},{1,0},{2,9},{3,8},{4,5},{5,4},{6,13},{7,12},{8,3},{9,2},{10,... | collective-permute-start | bytes 3145736 | tf_op jit(solution)/shard_map/ppermute | solution.py:48
  36.5 29.6 %collective-permute-start.5 = (bf16[256,2048]{1,0:T(8,128)(2,1)}, bf16[256,2048]{1,0:T(8,128)(2,1)}, u32[]{:S(2)}, u32[]{:S(2)}) collective-permute-start(bf16[256,2048]{1,0:T(8,128)(2,1)} %get-tuple-element.15), channel_id=1, source_target_pairs={{0,8},{1,9},{2,0},{3,1},{4,12},{5,13},{6,4},{7,5},{8,10},{9,11},{1... | collective-permute-start | bytes 3145736 | tf_op jit(solution)/shard_map/ppermute | solution.py:48
  36.5 46.3 %collective-permute-start.7 = (bf16[256,2048]{1,0:T(8,128)(2,1)}, bf16[256,2048]{1,0:T(8,128)(2,1)}, u32[]{:S(2)}, u32[]{:S(2)}) collective-permute-start(bf16[256,2048]{1,0:T(8,128)(2,1)} %get-tuple-element.14), channel_id=1, source_target_pairs={{0,9},{1,8},{2,1},{3,0},{4,13},{5,12},{6,5},{7,4},{8,11},{9,10},{1... | collective-permute-start | bytes 3145736 | tf_op jit(solution)/shard_map/ppermute | solution.py:48
  38.2 72.3 %collective-permute-start = (f32[64,2048]{1,0:T(8,128)S(1)}, f32[64,2048]{1,0:T(8,128)S(1)}, u32[]{:S(2)}, u32[]{:S(2)}) collective-permute-start(f32[64,2048]{1,0:T(8,128)S(1)} %dynamic-slice_bitcast_fusion.5), channel_id=1, source_target_pairs={{0,8},{1,9},{2,10},{3,11},{4,12},{5,13},{6,14},{7,15},{8,0},{9,1},... | collective-permute-start | bytes 1572872 | tf_op jit(solution)/shard_map/ppermute | solution.py:48
  39.8 43.4 %collective-permute-start.11 = (f32[128,128]{1,0:T(8,128)S(1)}, f32[128,128]{1,0:T(8,128)S(1)}, u32[]{:S(2)}, u32[]{:S(2)}) collective-permute-start(f32[128,128]{1,0:T(8,128)S(1)} %convolution_bitcast_fusion), channel_id=1, source_target_pairs={{0,4},{1,5},{2,6},{3,7},{4,0},{5,1},{6,2},{7,3},{8,12},{9,13},{10,... | collective-permute-start | bytes 196616 | tf_op jit(solution)/shard_map/ppermute | solution.py:48
  60.9 33.2 %collective-permute-start.2 = (bf16[256,2048]{1,0:T(8,128)(2,1)}, bf16[256,2048]{1,0:T(8,128)(2,1)}, u32[]{:S(2)}, u32[]{:S(2)}) collective-permute-start(bf16[256,2048]{1,0:T(8,128)(2,1)} %collective-permute-done.1), channel_id=1, source_target_pairs={{0,8},{1,9},{2,10},{3,11},{4,12},{5,13},{6,14},{7,15},{8,0},{9,1},... | collective-permute-start | bytes 3145736 | tf_op jit(solution)/shard_map/ppermute | solution.py:48
  66.1 32.7 %collective-permute-start.4 = (bf16[256,2048]{1,0:T(8,128)(2,1)}, bf16[256,2048]{1,0:T(8,128)(2,1)}, u32[]{:S(2)}, u32[]{:S(2)}) collective-permute-start(bf16[256,2048]{1,0:T(8,128)(2,1)} %collective-permute-done.3), channel_id=1, source_target_pairs={{0,8},{1,9},{2,10},{3,11},{4,12},{5,13},{6,14},{7,15},{8,0},{9,1},... | collective-permute-start | bytes 3145736 | tf_op jit(solution)/shard_map/ppermute | solution.py:48
  82.8 20.6 %collective-permute-start.6 = (bf16[256,2048]{1,0:T(8,128)(2,1)}, bf16[256,2048]{1,0:T(8,128)(2,1)}, u32[]{:S(2)}, u32[]{:S(2)}) collective-permute-start(bf16[256,2048]{1,0:T(8,128)(2,1)} %collective-permute-done.5), channel_id=1, source_target_pairs={{0,8},{1,9},{2,10},{3,11},{4,12},{5,13},{6,14},{7,15},{8,0},{9,1},... | collective-permute-start | bytes 3145736 | tf_op jit(solution)/shard_map/ppermute | solution.py:48
  83.2 24.9 %collective-permute-start.8 = (bf16[256,2048]{1,0:T(8,128)(2,1)}, bf16[256,2048]{1,0:T(8,128)(2,1)}, u32[]{:S(2)}, u32[]{:S(2)}) collective-permute-start(bf16[256,2048]{1,0:T(8,128)(2,1)} %collective-permute-done.7), channel_id=1, source_target_pairs={{0,8},{1,9},{2,10},{3,11},{4,12},{5,13},{6,14},{7,15},{8,0},{9,1},... | collective-permute-start | bytes 3145736 | tf_op jit(solution)/shard_map/ppermute | solution.py:48
  120.3 15.3 %collective-permute-start.12 = (bf16[64,2048]{1,0:T(8,128)(2,1)S(1)}, bf16[64,2048]{1,0:T(8,128)(2,1)S(1)}, u32[]{:S(2)}, u32[]{:S(2)}) collective-permute-start(bf16[64,2048]{1,0:T(8,128)(2,1)S(1)} %convolution_convert_fusion.4), channel_id=1, source_target_pairs={{0,4},{1,5},{2,6},{3,7},{4,0},{5,1},{6,2},{7,3},{8,12},{9,13},{10,... | collective-permute-start | bytes 786440 | tf_op jit(solution)/shard_map/ppermute | solution.py:48
  145.9 14.5 %collective-permute-start.13 = (bf16[64,2048]{1,0:T(8,128)(2,1)S(1)}, bf16[64,2048]{1,0:T(8,128)(2,1)S(1)}, u32[]{:S(2)}, u32[]{:S(2)}) collective-permute-start(bf16[64,2048]{1,0:T(8,128)(2,1)S(1)} %convolution_convert_fusion.3), channel_id=1, source_target_pairs={{0,4},{1,5},{2,6},{3,7},{4,0},{5,1},{6,2},{7,3},{8,12},{9,13},{10,... | collective-permute-start | bytes 786440 | tf_op jit(solution)/shard_map/ppermute | solution.py:48
  190.9 6.3 %collective-permute-start.14 = (f32[128,128]{1,0:T(8,128)S(1)}, f32[128,128]{1,0:T(8,128)S(1)}, u32[]{:S(2)}, u32[]{:S(2)}) collective-permute-start(f32[128,128]{1,0:T(8,128)S(1)} %fusion.115), channel_id=1, source_target_pairs={{0,4},{1,5},{2,6},{3,7},{4,0},{5,1},{6,2},{7,3},{8,12},{9,13},{10,... | collective-permute-start | bytes 196616 | tf_op jit(solution)/shard_map/ppermute | solution.py:48
  212.6 12.3 %collective-permute-start.15 = (bf16[64,2048]{1,0:T(8,128)(2,1)S(1)}, bf16[64,2048]{1,0:T(8,128)(2,1)S(1)}, u32[]{:S(2)}, u32[]{:S(2)}) collective-permute-start(bf16[64,2048]{1,0:T(8,128)(2,1)S(1)} %convolution_convert_fusion.2), channel_id=1, source_target_pairs={{0,4},{1,5},{2,6},{3,7},{4,0},{5,1},{6,2},{7,3},{8,12},{9,13},{10,... | collective-permute-start | bytes 786440 | tf_op jit(solution)/shard_map/ppermute | solution.py:48
  234.8 13.2 %collective-permute-start.16 = (bf16[64,2048]{1,0:T(8,128)(2,1)S(1)}, bf16[64,2048]{1,0:T(8,128)(2,1)S(1)}, u32[]{:S(2)}, u32[]{:S(2)}) collective-permute-start(bf16[64,2048]{1,0:T(8,128)(2,1)S(1)} %convolution_convert_fusion.1), channel_id=1, source_target_pairs={{0,4},{1,5},{2,6},{3,7},{4,0},{5,1},{6,2},{7,3},{8,12},{9,13},{10,... | collective-permute-start | bytes 786440 | tf_op jit(solution)/shard_map/ppermute | solution.py:48
  264.8 15.8 %all-to-all-start.4 = ((bf16[16,64,256]{2,1,0:T(8,128)(2,1)}), bf16[16,64,256]{2,1,0:T(8,128)(2,1)S(1)}, u32[]{:S(2)}, u32[]{:S(2)}) async-start(bf16[16,64,256]{2,1,0:T(8,128)(2,1)} %broadcast_in_dim.19), calls=%async_computation.4 | async-start | bytes 1048576 | tf_op jit(solution)/shard_map/all_to_all | solution.py:185
  268.7 8.1 %collective-permute-start.21 = (f32[64,256]{1,0:T(8,128)S(1)}, f32[64,256]{1,0:T(8,128)S(1)}, u32[]{:S(2)}, u32[]{:S(2)}) collective-permute-start(f32[64,256]{1,0:T(8,128)S(1)} %get-tuple-element.19), channel_id=1, source_target_pairs={{0,3},{1,2},{2,11},{3,10},{4,7},{5,6},{6,15},{7,14},{8,1},{9,0},{1... | collective-permute-start | bytes 196616 | tf_op jit(solution)/shard_map/ppermute | solution.py:48
  271.2 6.5 %collective-permute-start.20 = (f32[64,256]{1,0:T(8,128)S(1)}, f32[64,256]{1,0:T(8,128)S(1)}, u32[]{:S(2)}, u32[]{:S(2)}) collective-permute-start(f32[64,256]{1,0:T(8,128)S(1)} %get-tuple-element.20), channel_id=1, source_target_pairs={{0,2},{1,3},{2,10},{3,11},{4,6},{5,7},{6,14},{7,15},{8,0},{9,1},{1... | collective-permute-start | bytes 196616 | tf_op jit(solution)/shard_map/ppermute | solution.py:48
  271.5 8.9 %collective-permute-start.19 = (f32[64,256]{1,0:T(8,128)S(1)}, f32[64,256]{1,0:T(8,128)S(1)}, u32[]{:S(2)}, u32[]{:S(2)}) collective-permute-start(f32[64,256]{1,0:T(8,128)S(1)} %get-tuple-element.21), channel_id=1, source_target_pairs={{0,1},{1,0},{2,9},{3,8},{4,5},{5,4},{6,13},{7,12},{8,3},{9,2},{10,... | collective-permute-start | bytes 196616 | tf_op jit(solution)/shard_map/ppermute | solution.py:48
  272.1 8.4 %collective-permute-start.18 = (f32[64,256]{1,0:T(8,128)S(1)}, f32[64,256]{1,0:T(8,128)S(1)}, u32[]{:S(2)}, u32[]{:S(2)}) collective-permute-start(f32[64,256]{1,0:T(8,128)S(1)} %get-tuple-element.18), channel_id=1, source_target_pairs={{0,0},{1,1},{2,8},{3,9},{4,4},{5,5},{6,12},{7,13},{8,2},{9,3},{10,... | collective-permute-start | bytes 196616 | tf_op jit(solution)/shard_map/ppermute | solution.py:48
  281.3 6.1 %collective-permute-start.17 = (f32[128,128]{1,0:T(8,128)S(1)}, f32[128,128]{1,0:T(8,128)S(1)}, u32[]{:S(2)}, u32[]{:S(2)}) collective-permute-start(f32[128,128]{1,0:T(8,128)S(1)} %fusion.137), channel_id=1, source_target_pairs={{0,4},{1,5},{2,6},{3,7},{4,0},{5,1},{6,2},{7,3},{8,12},{9,13},{10,... | collective-permute-start | bytes 196616 | tf_op jit(solution)/shard_map/ppermute | solution.py:48
  (1 other events, 35.3 us)

commit v2 on v1

v2 whole, which is shorter than its diff:
```python
import jax
import jax.numpy as jnp
from jax import lax
from jax.experimental import pallas as pl
from jax.experimental.pallas import tpu as pltpu
from jax.sharding import PartitionSpec as P


OUTER = 2
INNER = 2
NS_ITERS = 12

ridge_weight = 0.1
step_size = 0.5
AXES = ("view", "samp")
GROUP = 4


def split(value):
    top = value.astype(jnp.bfloat16)
    return top, (value - top.astype(jnp.float32)).astype(jnp.bfloat16)


def fine_dot(left, right):
    left_top, left_rest = split(left)
    right_top, right_rest = split(right)
    out = jnp.dot(left_top, right_rest, preferred_element_type=jnp.float32)
    out = out + jnp.dot(left_rest, right_top, preferred_element_type=jnp.float32)
    return out + jnp.dot(left_top, right_top, preferred_element_type=jnp.float32)


def tall_dot(left, right):
    return lax.dot_general(left, right, (((1,), (1,)), ((), ())), preferred_element_type=jnp.float32)


def mixed_dot(mixing, sums):
    top, rest = split(mixing)
    return jnp.dot(rest, sums, preferred_element_type=jnp.float32) + jnp.dot(
        top, sums, preferred_element_type=jnp.float32
    )


def newton(total, gram):
    size_k = gram.shape[0]
    row = lax.broadcasted_iota(jnp.int32, gram.shape, 0)
    col = lax.broadcasted_iota(jnp.int32, gram.shape, 1)
    eye_mat = jnp.where(row == col, 1.0, 0.0)

    def whole_sum(value):
        return jnp.sum(jnp.sum(value, axis=0, keepdims=True), axis=1, keepdims=True)

    shrunk = gram + whole_sum(gram * eye_mat) / size_k * eye_mat
    scale = jnp.sqrt(whole_sum(shrunk * shrunk))
    approx = shrunk / scale
    inverse = eye_mat
    for turn in range(NS_ITERS):
        both = approx if turn == 0 else fine_dot(inverse, approx)
        factor = 0.5 * (3.0 * eye_mat - both)
        if turn == 0:
            approx, inverse = fine_dot(approx, factor), factor
        elif turn < NS_ITERS - 1:
            stacked = fine_dot(jnp.concatenate([approx, inverse], axis=0), factor)
            approx, inverse = stacked[:size_k], stacked[size_k:]
        else:
            inverse = fine_dot(inverse, factor)
    return inverse * jnp.sqrt(total / scale)


def gathered_block(gathered_ref, index):
    half = gathered_ref.shape[0] // 2
    return jnp.concatenate([gathered_ref[index], gathered_ref[half + index]], axis=0)


def newton_mixing(total, pair):
    def kernel(part_ref, other_ref, mixing_ref):
        mixing_ref[...] = newton(total, part_ref[...] + other_ref[...])

    return pl.pallas_call(
        kernel, out_shape=jax.ShapeDtypeStruct(pair[0].shape, jnp.float32), name="newton"
    )(*pair)


def newton_scores(total, pair, gathered, first_block, n_blocks):
    comps, sub = pair[0].shape[0], gathered.shape[2]

    def kernel(first_ref, part_ref, other_ref, gathered_ref, out_ref):
        mixing = newton(total, part_ref[...] + other_ref[...])
        for n in range(n_blocks):
            sums = gathered_block(gathered_ref, first_ref[0] + n)
            out_ref[pl.ds(n * sub, sub), :] = mixed_dot(mixing, sums).T

    vmem = pl.BlockSpec(memory_space=pltpu.VMEM)
    return pl.pallas_call(
        kernel,
        in_specs=[pl.BlockSpec(memory_space=pltpu.SMEM), vmem, vmem, vmem],
        out_specs=vmem,
        out_shape=jax.ShapeDtypeStruct((n_blocks * sub, comps), jnp.float32),
        name="newton_scores",
    )(first_block, *pair, gathered)


def gram_part(gathered):
    half, half_k, _ = gathered.shape
    half = half // 2

    def kernel(gathered_ref, out_ref):
        acc = None
        for n in range(half):
            sums = gathered_block(gathered_ref, n)
            add = tall_dot(sums, sums)
            acc = add if acc is None else acc + add
        out_ref[...] = acc

    return pl.pallas_call(
        kernel, out_shape=jax.ShapeDtypeStruct((2 * half_k, 2 * half_k), jnp.float32), name="gram"
    )(gathered)


def sum_and_fan(parts):
    n, half_k, sub = parts.shape

    def kernel(parts_ref, out_ref):
        acc = parts_ref[0].astype(jnp.float32)
        for i in range(1, n):
            acc = acc + parts_ref[i].astype(jnp.float32)
        acc = acc.astype(jnp.bfloat16)
        for i in range(2 * n):
            out_ref[i] = acc

    return pl.pallas_call(
        kernel, out_shape=jax.ShapeDtypeStruct((2 * n, half_k, sub), jnp.bfloat16), name="fan"
    )(parts)


def step_call(
    total, where, data, coeffs=None, grads=None, values=None, mixing=None, gathered=None, n_sub=None
):
    piece_rows, feats = data[0].shape
    n_pieces = len(data)
    pooled = n_pieces * piece_rows
    half_k = (coeffs if coeffs is not None else values).shape[0]
    low = jnp.bfloat16
    vmem, smem = pl.BlockSpec(memory_space=pltpu.VMEM), pl.BlockSpec(memory_space=pltpu.SMEM)
    args, specs, shapes = [where, *data], [smem] + [pl.BlockSpec(memory_space=pl.ANY)] * n_pieces, []
    names = []

    def give(name, *arrays):
        for i, array in enumerate(arrays):
            names.append(f"{name}{i}")
            args.append(array)
            specs.append(vmem)

    if values is None:
        give("coeffs", coeffs)
        if grads is not None:
            give("grads", *grads)
            shapes.append(("new_coeffs", jax.ShapeDtypeStruct((half_k, feats), jnp.float32)))
    else:
        give("values", values)
    if n_sub is not None:
        sub = pooled // n_sub
        shapes.append(("out_values", jax.ShapeDtypeStruct((half_k, pooled), jnp.float32)))
        shapes.append(("parts", jax.ShapeDtypeStruct((n_sub, half_k, sub), low)))
    if mixing is not None:
        give("mixing", mixing)
        give("gathered", gathered)
        shapes.append(("term", jax.ShapeDtypeStruct((half_k, feats), low)))

    def kernel(where_ref, *refs):
        pieces = refs[:n_pieces]
        at = n_pieces
        ins = dict(zip(names, refs[at : at + len(names)], strict=True))
        at += len(names)
        outs = dict(zip([name for name, _ in shapes], refs[at : at + len(shapes)], strict=True))
        held, resid, sems = refs[at + len(shapes) :]
        base, core = where_ref[0], where_ref[1]

        def copy(i):
            return pltpu.make_async_copy(
                pieces[i], held.at[pl.ds(i * piece_rows, piece_rows), :], sems.at[i]
            )

        for i in range(n_pieces):
            copy(i).start()

        def block_at(i):
            own = core if i % 2 == 0 else 1 - core
            return 2 * lax.bitwise_xor(base, i // 2) + own

        if mixing is not None:
            mixing_rows = ins["mixing0"][pl.ds(pl.multiple_of(core * half_k, half_k), half_k), :]
            sub_in = gathered.shape[2]
            ratio = piece_rows // sub_in

            def set_resid(i, value):
                sums = [
                    gathered_block(ins["gathered0"], block_at(i) * ratio + r) for r in range(ratio)
                ]
                sums = sums[0] if ratio == 1 else jnp.concatenate(sums, axis=1)
                resid[:, pl.ds(i * piece_rows, piece_rows)] = (
                    value - mixed_dot(mixing_rows, sums)
                ).astype(low)

        if values is None:
            weights = ins["coeffs0"][...]
            if grads is not None:
                grad = ins["grads0"][...].astype(jnp.float32) + ins["grads1"][...].astype(jnp.float32)
                weights = weights - step_size * (grad / total + ridge_weight * weights)
                outs["new_coeffs"][...] = weights
            weights = weights.astype(low)
            for i in range(n_pieces):
                copy(i).wait()
                value = tall_dot(weights, held[pl.ds(i * piece_rows, piece_rows), :])
                if n_sub is not None:
                    outs["out_values"][:, pl.ds(i * piece_rows, piece_rows)] = value
                    ratio_out = piece_rows // sub
                    for r in range(ratio_out):
                        outs["parts"][block_at(i) * ratio_out + r] = value[
                            :, r * sub : (r + 1) * sub
                        ].astype(low)
                if mixing is not None:
                    set_resid(i, value)
        else:
            for i in range(n_pieces):
                set_resid(i, ins["values0"][:, pl.ds(i * piece_rows, piece_rows)])
            for i in range(n_pieces):
                copy(i).wait()
        if mixing is not None:
            outs["term"][...] = jnp.dot(
                resid[...], held[...], preferred_element_type=jnp.float32
            ).astype(low)

    return pl.pallas_call(
        kernel,
        in_specs=specs,
        out_specs=[vmem] * len(shapes),
        out_shape=[shape for _, shape in shapes],
        scratch_shapes=[
            pltpu.VMEM((pooled, feats), low),
            pltpu.VMEM((half_k, pooled), low),
            pltpu.SemaphoreType.DMA((n_pieces,)),
        ],
        name="step",
    )(*args)


class Grid:
    def __init__(self, n_view, n_samp):
        self.planes, self.squares = n_view // 2, n_samp // GROUP
        self.n_samp = n_samp

    def encode(self, plane, core, square, corner):
        return (plane * 2 + core) * self.n_samp + square * GROUP + corner

    def each(self):
        for plane in range(self.planes):
            for core in range(2):
                for square in range(self.squares):
                    for corner in range(GROUP):
                        yield plane, core, square, corner

    def permute(self, value, target):
        pairs = [(self.encode(*at), self.encode(*target(*at))) for at in self.each()]
        return lax.ppermute(value, AXES, pairs)

    def swap_core(self, value):
        return self.permute(value, lambda a, c, q, p: (a, 1 - c, q, p))

    def sum_squares(self, value, wire):
        low, other = value.astype(wire), jnp.zeros(value.shape, wire)
        bit = 1
        while bit < self.squares:
            if bit > 1:
                low = (low.astype(jnp.float32) + other.astype(jnp.float32)).astype(wire)
            other = self.permute(low, lambda a, c, q, p, bit=bit: (a, c, q ^ bit, p))
            bit *= 2
        return low, other

    def sum_planes(self, value):
        bit = 1
        while bit < self.planes:
            value = value + self.permute(value, lambda a, c, q, p, bit=bit: (a ^ bit, c, q, p))
            bit *= 2
        return value


def pick(parts, index, axis=0):
    return lax.dynamic_index_in_dim(parts, index, axis, keepdims=False)


def pick(parts, index, axis=0):
    return lax.dynamic_index_in_dim(parts, index, axis, keepdims=False)


def body(view_data, init_coeffs):
    low = jnp.bfloat16
    grid = Grid(lax.axis_size("view"), lax.axis_size("samp"))
    rows, feats = view_data.shape[1:]
    comps = init_coeffs.shape[2]
    half_k, half_rows = comps // 2, rows // 2
    total = rows * lax.axis_size("samp")
    view_at, samp_at = lax.axis_index("view"), lax.axis_index("samp")
    core = view_at % 2
    square, corner = samp_at // GROUP, samp_at % GROUP
    base = 2 * core + corner % 2
    where = jnp.stack([base, core]).astype(jnp.int32)
    n_sub = GROUP * grid.planes
    sub = rows // grid.planes

    slots = [None] * GROUP

    def pool(k):
        m = corner ^ k
        piece = lax.dynamic_slice(
            view_data, (m % 2, (m // 2) * half_rows, 0), (1, half_rows, feats)
        )[0]
        slots[k] = grid.permute(
            piece, lambda a, c, q, p, k=k: (a, (p ^ k) // 2, q, 2 * c + (p ^ k) % 2)
        )

    pool(1)
    pool(0)

    coeffs_low = init_coeffs.astype(low)
    part = jnp.zeros((comps, rows), jnp.float32)
    for member in range(view_data.shape[0]):
        part = part + lax.dot_general(
            coeffs_low[member],
            view_data[member],
            (((0,), (1,)), ((), ())),
            preferred_element_type=jnp.float32,
        )
    pool(3)
    pool(2)
    mine = lax.dynamic_slice_in_dim(part, core * half_rows, half_rows, 1)
    theirs = lax.dynamic_slice_in_dim(part, (1 - core) * half_rows, half_rows, 1)
    mine = mine + grid.swap_core(theirs)
    mine, init_later = lax.optimization_barrier((mine, init_coeffs))
    mine = grid.sum_planes(mine)
    square_groups = [
        [grid.encode(a, c, q, p) for p in range(GROUP) for c in range(2)]
        for a in range(grid.planes)
        for q in range(grid.squares)
    ]
    gathered = lax.all_to_all(
        jnp.broadcast_to(mine.astype(low), (2 * GROUP, comps, half_rows)),
        AXES, 0, 0, axis_index_groups=square_groups,
    )
    local = jnp.transpose(pick(init_later, corner % 2)).reshape(2, half_k, feats)
    from_core = grid.swap_core(pick(local, 1 - core))
    coeffs = jnp.where(core == corner // 2, pick(local, core), from_core)
    gathered, coeffs = lax.optimization_barrier((gathered, coeffs))
    gathered = jnp.transpose(
        gathered.reshape(2 * GROUP, 2, half_k, half_rows // sub, sub), (1, 0, 3, 2, 4)
    ).reshape(2 * n_sub, half_k, sub)

    data = []
    for k in range(GROUP):
        data += [slots[k], grid.swap_core(slots[k ^ 2])]

    def gram_pair(gathered):
        return grid.sum_squares(gram_part(gathered), jnp.float32)

    pair = gram_pair(gathered)
    mixing = newton_mixing(total, pair)

    reduce_groups = [
        [grid.encode(a, c, q, p) for p in range(GROUP) for a in range(grid.planes)]
        for c in range(2)
        for q in range(grid.squares)
    ]
    gather_groups = [
        [
            grid.encode(a, c, q, p)
            for c in range(2)
            for p in range(GROUP)
            for a in range(grid.planes)
        ]
        for q in range(grid.squares)
    ]
    values = grads = None
    for outer_step in range(OUTER):
        for inner_step in range(INNER):
            given = {"mixing": mixing, "gathered": gathered}
            if inner_step == 0 and outer_step > 0:
                (term,) = step_call(total, where, data, values=values, **given)
            elif grads is None:
                (term,) = step_call(total, where, data, coeffs=coeffs, **given)
            else:
                coeffs, term = step_call(total, where, data, coeffs=coeffs, grads=grads, **given)
            grads = grid.sum_squares(term, low)
        coeffs, values, parts = step_call(
            total, where, data, coeffs=coeffs, grads=grads, n_sub=n_sub
        )
        grads = None
        parts = lax.all_to_all(parts, AXES, 0, 0, axis_index_groups=reduce_groups)
        gathered = lax.all_to_all(
            sum_and_fan(parts), AXES, 0, 0, axis_index_groups=gather_groups
        )
        if outer_step < OUTER - 1:
            mixing = newton_mixing(total, gram_pair(gathered))
    gathered, coeffs = lax.optimization_barrier((gathered, coeffs))
    first_block = (corner * grid.planes).astype(jnp.int32).reshape(1)
    shared = newton_scores(total, gram_pair(gathered), gathered, first_block, grid.planes)

    out_rows = feats // lax.axis_size("samp")
    pieces = []
    for k in range(GROUP):
        start = (square * GROUP + (base ^ k)) * out_rows
        piece = lax.dynamic_slice_in_dim(coeffs, start, out_rows, 1)
        pieces.append(
            grid.permute(
                piece,
                lambda a, c, q, p, k=k: (a, p // 2, q, (2 * c + p % 2) ^ k),
            )
        )
    pieces = jnp.stack(pieces)
    ordered = [pick(pieces, corner ^ r) for r in range(GROUP)]
    final = jnp.stack(
        [jnp.concatenate([ordered[member], ordered[2 + member]], axis=0).T for member in range(2)]
    )
    return (shared, final)


def solution(mesh):
    in_specs = (P("view", "samp", None), P("view", None, None))
    out_specs = (P("samp", None), P("view", "samp", None))

    return jax.shard_map(body, mesh=mesh, in_specs=in_specs, out_specs=out_specs, check_vma=False)
```

time: 300 us -> 290 us (0.967)
  Pallas kernels: 0 us -> 82.5 us
  matrix products: 77.5 us -> 1.67 us
  local copies, waits for them, and re-layouts: 32.5 us -> 20.8 us
  between operations: 6.28 us -> 1.19 us
  blocking collectives: 33 us -> 37.2 us
  waiting for transfers between devices: 105 us -> 101 us
    pallas_call x0 -> x14, Pallas kernels: none -> 82.5 us  [the longest x6 54.3 us: step_call(): pl.pallas_call(kernel, in_specs=specs, out_specs=[vmem] * len(shapes), ou...]
    dot_general x117 -> x0, matrix products: 72.5 us -> none  [the longest x4 34.8 us: body(): term = jnp.dot(resid, data, preferred_element_type=jnp.float32)]
    ppermute x22, waiting for transfers between devices: 105 us -> 84.7 us  [permute(): return lax.ppermute(value, AXES, pairs)]
    dynamic_update_slice x8 -> x0, local copies, waits for them, and re-layouts: 18.6 us -> none  [the longest x4 9.36 us: body(): lax.dynamic_update_slice(data, other, ((2 * (source ^ 2) + 1 - core) * ha...]
    all_to_all x1, waiting for transfers between devices: 0.01 us -> 9.72 us  [body(): lax.all_to_all(sum_and_fan(parts), AXES, 0, 0, axis_index_groups=gather_g...]
    all_to_all x1, waiting for transfers between devices: 0.01 us -> 6.75 us  [body(): lax.all_to_all(jnp.broadcast_to(mine.astype(low), (2 * GROUP, comps, half...]
    broadcast_in_dim x3 -> x0, local copies, waits for them, and re-layouts: 5.17 us -> none  [the longest x1 4.28 us: body(): data = jnp.zeros((pooled, feats), low)]
    unnamed x5 -> x27, local copies, waits for them, and re-layouts: 1.06 us -> 5.56 us
  transfers between devices with their start and end apart: 24 -> 24, of which waited for: 14 -> 12; matrix products, arithmetic and copies ran while one was open for 14% -> 5% of each run, Pallas kernels for 0% -> 3%
where the time goes in v2:
time: 290 us; the launch traced here: 288 us
  waiting for transfers between devices  101 us (35%)
  Pallas kernels  82.5 us (28%)
  starting transfers between devices  39.4 us (14%)
  blocking collectives  37.2 us (13%)
  local copies, waits for them, and re-layouts  20.8 us (7%)
  other arithmetic  3.61 us (1%)
    ppermute x22, waiting for transfers between devices, permute(): return lax.ppermute(value, AXES, pairs)  84.7 us
    pallas_call x6, Pallas kernels, step_call(): pl.pallas_call(kernel, in_specs=specs, out_specs=[vmem] * len(shapes), ou...  54.3 us
    ppermute x22, starting transfers between devices, permute(): return lax.ppermute(value, AXES, pairs)  31.5 us
    all_to_all x2, blocking collectives, body(): parts = lax.all_to_all(parts, AXES, 0, 0, axis_index_groups=reduce_groups)  23.2 us
    all_to_all x1, blocking collectives, body(): lax.all_to_all(sum_and_fan(parts), AXES, 0, 0, axis_index_groups=gather_g...  14 us
    pallas_call x2, Pallas kernels, newton_mixing(): pl.pallas_call(kernel, out_shape=jax.ShapeDtypeStruct(pair[0].shape, jnp....  12 us
    all_to_all x1, waiting for transfers between devices, body(): lax.all_to_all(sum_and_fan(parts), AXES, 0, 0, axis_index_groups=gather_g...  9.72 us
    all_to_all x1, waiting for transfers between devices, body(): lax.all_to_all(jnp.broadcast_to(mine.astype(low), (2 * GROUP, comps, half...  6.75 us
  transfers between devices with their start and end apart: 24, of which 12 were waited for; matrix products, arithmetic and copies ran while one was open for 5% of the time, Pallas kernels for 3%

profile of v2, /device:TPU:0, one launch (start us, length us, event | category | flops | bytes accessed | tf_op | source)
XLA Modules:
  0.0 287.5 jit_solution(1957868700190471121)
XLA Ops:
  0.8 4.6 %dynamic-slice_bitcast_fusion.1 = (bf16[256,2048]{1,0:T(8,128)(2,1)}, bf16[256,2048]{1,0:T(8,128)(2,1)}, bf16[256,2048]{1,0:T(8,128)(2,1)}, bf16[256,2048]{1,0:T(8,128)(2,1)}) fusion(bf16[2,512,2048]{2,1,0:T(8,128)(2,1)} %param.2, s32[]{:T(128)S(6)} %select_n.135, s32[]{:T(128)S(6)} %select_n.137, s32[]{:T(128)S(6)} %select_n.131, s32[]{:T(128)S(6)} %select_n.133, ...), kind=kLoop, calls=%fused_computation.8 | loop fusion | bytes 8388640 | tf_op jit(solution)/shard_map/squeeze | solution.py:314
  9.5 9.5 %collective-permute-start = (bf16[256,2048]{1,0:T(8,128)(2,1)}, bf16[256,2048]{1,0:T(8,128)(2,1)}, u32[]{:S(2)}, u32[]{:S(2)}) collective-permute-start(bf16[256,2048]{1,0:T(8,128)(2,1)} %get-tuple-element.39), channel_id=1, source_target_pairs={{0,0},{1,1},{2,8},{3,9},{4,4},{5,5},{6,12},{7,13},{8,2},{9,3},{10,... | collective-permute-start | bytes 3145736 | tf_op jit(solution)/shard_map/ppermute | solution.py:264
  32.0 11.0 %collective-permute-done.4.refs_6_ = bf16[256,2048]{1,0:T(8,128)(2,1)S(1)} collective-permute-done((bf16[256,2048]{1,0:T(8,128)(2,1)}, bf16[256,2048]{1,0:T(8,128)(2,1)S(1)}, u32[]{:S(2)}, u32[]{:S(2)}) %collective-permute-start.4) | collective-permute-done | bytes 1048608 | tf_op jit(solution)/shard_map/ppermute | solution.py:264
  44.0 11.1 %collective-permute-done.3.refs_2_ = bf16[256,2048]{1,0:T(8,128)(2,1)S(1)} collective-permute-done((bf16[256,2048]{1,0:T(8,128)(2,1)}, bf16[256,2048]{1,0:T(8,128)(2,1)S(1)}, u32[]{:S(2)}, u32[]{:S(2)}) %collective-permute-start.3) | collective-permute-done | bytes 1048608 | tf_op jit(solution)/shard_map/ppermute | solution.py:264
  57.4 4.3 %all-to-all-start = ((bf16[8,128,256]{2,1,0:T(8,128)(2,1)}), bf16[8,128,256]{2,1,0:T(8,128)(2,1)}, u32[]{:S(2)}, u32[]{:S(2)}) async-start(bf16[8,128,256]{2,1,0:T(8,128)(2,1)} %broadcast_in_dim.3), calls=%async_computation | async-start | bytes 1048576 | tf_op jit(solution)/shard_map/all_to_all | solution.py:345
  63.7 6.7 %all-to-all-done = bf16[8,128,256]{2,1,0:T(8,128)(2,1)} async-done(((bf16[8,128,256]{2,1,0:T(8,128)(2,1)}), bf16[8,128,256]{2,1,0:T(8,128)(2,1)}, u32[]{:S(2)}, u32[]{:S(2)}) %all-to-all-start) | async-done | bytes 524320 | tf_op jit(solution)/shard_map/all_to_all | solution.py:345
  80.3 6.0 %newton.2.refs_9_.refs_11_ = f32[128,128]{1,0:T(8,128)} custom-call(f32[128,128]{1,0:T(8,128)} %gram.3.part_ref, f32[128,128]{1,0:T(8,128)} %copy-done.11), custom_call_target="tpu_custom_call" | custom-call | tf_op jit(solution)/shard_map/newton/pallas_call | solution.py:78
  86.4 9.8 %step.6.refs_9_ = bf16[64,2048]{1,0:T(8,128)(2,1)} custom-call(s32[2]{0:T(128)} %pad_add_fusion.where_ref, bf16[256,2048]{1,0:T(8,128)(2,1)} %collective-permute-done.refs_0_, bf16[256,2048]{1,0:T(8,128)(2,1)} %collective-permute-done.2.refs_1_, bf16[256,2048]{1,0:T(8,128)(2,1)} %copy-done.1, bf16[256,2048]{1,0:T(8,128)(2,1)} %collective-permute-done.5.refs_3_, ...), custom_call_target="tpu_custom_call" | custom-call | tf_op jit(solution)/shard_map/step/pallas_call | solution.py:233
  98.9 11.3 %collective-permute-done.12.refs_10_ = bf16[64,2048]{1,0:T(8,128)(2,1)S(1)} collective-permute-done((bf16[64,2048]{1,0:T(8,128)(2,1)}, bf16[64,2048]{1,0:T(8,128)(2,1)S(1)}, u32[]{:S(2)}, u32[]{:S(2)}) %collective-permute-start.12) | collective-permute-done | bytes 262176 | tf_op jit(solution)/shard_map/ppermute | solution.py:264
  111.0 10.0 %step.7 = (f32[64,2048]{1,0:T(8,128)}, bf16[64,2048]{1,0:T(8,128)(2,1)}) custom-call(s32[2]{0:T(128)} %pad_add_fusion.where_ref, bf16[256,2048]{1,0:T(8,128)(2,1)} %collective-permute-done.refs_0_, bf16[256,2048]{1,0:T(8,128)(2,1)} %collective-permute-done.2.refs_1_, bf16[256,2048]{1,0:T(8,128)(2,1)} %copy-done.1, ...), custom_call_target="tpu_custom_call" | custom-call | tf_op jit(solution)/shard_map/step/pallas_call | solution.py:233
  121.1 14.4 %collective-permute-done.13.refs_10_ = bf16[64,2048]{1,0:T(8,128)(2,1)S(1)} collective-permute-done((bf16[64,2048]{1,0:T(8,128)(2,1)}, bf16[64,2048]{1,0:T(8,128)(2,1)S(1)}, u32[]{:S(2)}, u32[]{:S(2)}) %collective-permute-start.13) | collective-permute-done | bytes 262176 | tf_op jit(solution)/shard_map/ppermute | solution.py:264
  136.2 8.8 %step.8 = (f32[64,2048]{1,0:T(8,128)}, f32[64,2048]{1,0:T(8,128)}, bf16[8,64,256]{2,1,0:T(8,128)(2,1)}) custom-call(s32[2]{0:T(128)} %pad_add_fusion.where_ref, bf16[256,2048]{1,0:T(8,128)(2,1)} %collective-permute-done.refs_0_, bf16[256,2048]{1,0:T(8,128)(2,1)} %collective-permute-done.2.refs_1_, bf16[256,2048]{1,0:T(8,128)(2,1)} %copy-done.1, ...), custom_call_target="tpu_custom_call" | custom-call | tf_op jit(solution)/shard_map/step/pallas_call | solution.py:233
  144.9 10.7 %all_to_all.25.parts_ref = bf16[8,64,256]{2,1,0:T(8,128)(2,1)} all-to-all(bf16[8,64,256]{2,1,0:T(8,128)(2,1)} %get-tuple-element.25), channel_id=1, replica_groups={{0,16,1,17,2,18,3,19},{4,20,5,21,6,22,7,23},{8,24,9,25,10,26,11,27},{12..., dimensions={0} | all-to-all | bytes 524288 | tf_op jit(solution)/shard_map/all_to_all | solution.py:396
  157.4 14.0 %all_to_all.26.gathered_ref.refs_10_.refs_12_ = bf16[16,64,256]{2,1,0:T(8,128)(2,1)} all-to-all(bf16[16,64,256]{2,1,0:T(8,128)(2,1)} %fan.2), channel_id=1, replica_groups={{0,16,1,17,2,18,3,19,8,24,9,25,10,26,11,27},{4,20,5,21,6,22,7,23,12,28,..., dimensions={0} | all-to-all | bytes 1048576 | tf_op jit(solution)/shard_map/all_to_all | solution.py:397
  174.4 5.5 %collective-permute-done.14.other_ref = f32[128,128]{1,0:T(8,128)S(1)} collective-permute-done((f32[128,128]{1,0:T(8,128)}, f32[128,128]{1,0:T(8,128)S(1)}, u32[]{:S(2)}, u32[]{:S(2)}) %collective-permute-start.14) | collective-permute-done | bytes 65568 | tf_op jit(solution)/shard_map/ppermute | solution.py:264
  180.5 6.0 %newton.3.refs_9_.refs_11_ = f32[128,128]{1,0:T(8,128)} custom-call(f32[128,128]{1,0:T(8,128)} %gram.4.part_ref, f32[128,128]{1,0:T(8,128)} %copy-done.12), custom_call_target="tpu_custom_call" | custom-call | tf_op jit(solution)/shard_map/newton/pallas_call | solution.py:78
  186.5 7.0 %step.9.refs_9_ = bf16[64,2048]{1,0:T(8,128)(2,1)} custom-call(s32[2]{0:T(128)} %pad_add_fusion.where_ref, bf16[256,2048]{1,0:T(8,128)(2,1)} %collective-permute-done.refs_0_, bf16[256,2048]{1,0:T(8,128)(2,1)} %collective-permute-done.2.refs_1_, bf16[256,2048]{1,0:T(8,128)(2,1)} %copy-done.1, bf16[256,2048]{1,0:T(8,128)(2,1)} %collective-permute-done.5.refs_3_, ...), custom_call_target="tpu_custom_call" | custom-call | tf_op jit(solution)/shard_map/step/pallas_call | solution.py:233
  193.6 12.7 %collective-permute-done.15.refs_10_ = bf16[64,2048]{1,0:T(8,128)(2,1)S(1)} collective-permute-done((bf16[64,2048]{1,0:T(8,128)(2,1)}, bf16[64,2048]{1,0:T(8,128)(2,1)S(1)}, u32[]{:S(2)}, u32[]{:S(2)}) %collective-permute-start.15) | collective-permute-done | bytes 262176 | tf_op jit(solution)/shard_map/ppermute | solution.py:264
  207.0 10.0 %step.10 = (f32[64,2048]{1,0:T(8,128)}, bf16[64,2048]{1,0:T(8,128)(2,1)}) custom-call(s32[2]{0:T(128)} %pad_add_fusion.where_ref, bf16[256,2048]{1,0:T(8,128)(2,1)} %collective-permute-done.refs_0_, bf16[256,2048]{1,0:T(8,128)(2,1)} %collective-permute-done.2.refs_1_, bf16[256,2048]{1,0:T(8,128)(2,1)} %copy-done.1, ...), custom_call_target="tpu_custom_call" | custom-call | tf_op jit(solution)/shard_map/step/pallas_call | solution.py:233
  217.1 11.1 %collective-permute-done.16.refs_10_ = bf16[64,2048]{1,0:T(8,128)(2,1)S(1)} collective-permute-done((bf16[64,2048]{1,0:T(8,128)(2,1)}, bf16[64,2048]{1,0:T(8,128)(2,1)S(1)}, u32[]{:S(2)}, u32[]{:S(2)}) %collective-permute-start.16) | collective-permute-done | bytes 262176 | tf_op jit(solution)/shard_map/ppermute | solution.py:264
  228.9 8.8 %step.11 = (f32[64,2048]{1,0:T(8,128)}, f32[64,2048]{1,0:T(8,128)}, bf16[8,64,256]{2,1,0:T(8,128)(2,1)}) custom-call(s32[2]{0:T(128)} %pad_add_fusion.where_ref, bf16[256,2048]{1,0:T(8,128)(2,1)} %collective-permute-done.refs_0_, bf16[256,2048]{1,0:T(8,128)(2,1)} %collective-permute-done.2.refs_1_, bf16[256,2048]{1,0:T(8,128)(2,1)} %copy-done.1, ...), custom_call_target="tpu_custom_call" | custom-call | tf_op jit(solution)/shard_map/step/pallas_call | solution.py:233
  237.6 12.5 %all_to_all.27.parts_ref = bf16[8,64,256]{2,1,0:T(8,128)(2,1)} all-to-all(bf16[8,64,256]{2,1,0:T(8,128)(2,1)} %get-tuple-element.28), channel_id=1, replica_groups={{0,16,1,17,2,18,3,19},{4,20,5,21,6,22,7,23},{8,24,9,25,10,26,11,27},{12..., dimensions={0} | all-to-all | bytes 524288 | tf_op jit(solution)/shard_map/all_to_all | solution.py:396
  255.6 9.7 %all-to-all-done.4.gathered_ref = bf16[16,64,256]{2,1,0:T(8,128)(2,1)S(1)} async-done(((bf16[16,64,256]{2,1,0:T(8,128)(2,1)}), bf16[16,64,256]{2,1,0:T(8,128)(2,1)S(1)}, u32[]{:S(2)}, u32[]{:S(2)}) %all-to-all-start.4) | async-done | bytes 524320 | tf_op jit(solution)/shard_map/all_to_all | solution.py:397
  280.9 6.6 %newton_scores.1 = f32[512,128]{1,0:T(8,128)} custom-call(s32[1]{0:T(128)} %bitcast.first_ref, f32[128,128]{1,0:T(8,128)} %gram.5.part_ref, f32[128,128]{1,0:T(8,128)} %copy-done.10, bf16[16,64,256]{2,1,0:T(8,128)(2,1)} %copy-done.4), custom_call_target="tpu_custom_call" | custom-call | tf_op jit(solution)/shard_map/newton_scores/pallas_call | solution.py:93
  (87 shorter events, 64.1 us)
Async XLA Ops:
  5.4 37.5 %collective-permute-start.4 = (bf16[256,2048]{1,0:T(8,128)(2,1)}, bf16[256,2048]{1,0:T(8,128)(2,1)S(1)}, u32[]{:S(2)}, u32[]{:S(2)}) collective-permute-start(bf16[256,2048]{1,0:T(8,128)(2,1)} %get-tuple-element.36), channel_id=1, source_target_pairs={{0,9},{1,8},{2,1},{3,0},{4,13},{5,12},{6,5},{7,4},{8,11},{9,10},{1... | collective-permute-start | bytes 3145736 | tf_op jit(solution)/shard_map/ppermute | solution.py:264
  7.9 47.3 %collective-permute-start.3 = (bf16[256,2048]{1,0:T(8,128)(2,1)}, bf16[256,2048]{1,0:T(8,128)(2,1)S(1)}, u32[]{:S(2)}, u32[]{:S(2)}) collective-permute-start(bf16[256,2048]{1,0:T(8,128)(2,1)} %get-tuple-element.37), channel_id=1, source_target_pairs={{0,1},{1,0},{2,9},{3,8},{4,5},{5,4},{6,13},{7,12},{8,3},{9,2},{10,... | collective-permute-start | bytes 3145736 | tf_op jit(solution)/shard_map/ppermute | solution.py:264
  8.4 46.7 %collective-permute-start.1 = (bf16[256,2048]{1,0:T(8,128)(2,1)}, bf16[256,2048]{1,0:T(8,128)(2,1)S(1)}, u32[]{:S(2)}, u32[]{:S(2)}) collective-permute-start(bf16[256,2048]{1,0:T(8,128)(2,1)} %get-tuple-element.38), channel_id=1, source_target_pairs={{0,8},{1,9},{2,0},{3,1},{4,12},{5,13},{6,4},{7,5},{8,10},{9,11},{1... | collective-permute-start | bytes 3145736 | tf_op jit(solution)/shard_map/ppermute | solution.py:264
  9.5 46.1 %collective-permute-start = (bf16[256,2048]{1,0:T(8,128)(2,1)}, bf16[256,2048]{1,0:T(8,128)(2,1)}, u32[]{:S(2)}, u32[]{:S(2)}) collective-permute-start(bf16[256,2048]{1,0:T(8,128)(2,1)} %get-tuple-element.39), channel_id=1, source_target_pairs={{0,0},{1,1},{2,8},{3,9},{4,4},{5,5},{6,12},{7,13},{8,2},{9,3},{10,... | collective-permute-start | bytes 3145736 | tf_op jit(solution)/shard_map/ppermute | solution.py:264
  20.9 1.5 collective-permute-start.8
  23.4 8.6 %collective-permute-start.9 = (f32[128,256]{1,0:T(8,128)S(1)}, f32[128,256]{1,0:T(8,128)S(1)}, u32[]{:S(2)}, u32[]{:S(2)}) collective-permute-start(f32[128,256]{1,0:T(8,128)S(1)} %dynamic-slice_add_fusion), channel_id=1, source_target_pairs={{0,16},{1,17},{2,18},{3,19},{4,20},{5,21},{6,22},{7,23},{8,24},{9,... | collective-permute-start | bytes 393224 | tf_op jit(solution)/shard_map/ppermute | solution.py:264
  32.0 29.7 %collective-permute-start.10 = (f32[64,2048]{1,0:T(8,128)}, f32[64,2048]{1,0:T(8,128)}, u32[]{:S(2)}, u32[]{:S(2)}) collective-permute-start(f32[64,2048]{1,0:T(8,128)} %dynamic-slice_bitcast_fusion.5), channel_id=1, source_target_pairs={{0,8},{1,9},{2,10},{3,11},{4,12},{5,13},{6,14},{7,15},{8,0},{9,1},... | collective-permute-start | bytes 1572872 | tf_op jit(solution)/shard_map/ppermute | solution.py:264
  43.0 43.4 %collective-permute-start.5 = (bf16[256,2048]{1,0:T(8,128)(2,1)S(1)}, bf16[256,2048]{1,0:T(8,128)(2,1)}, u32[]{:S(2)}, u32[]{:S(2)}) collective-permute-start(bf16[256,2048]{1,0:T(8,128)(2,1)S(1)} %collective-permute-done.4.refs_6_), channel_id=1, source_target_pairs={{0,8},{1,9},{2,10},{3,11},{4,12},{5,13},{6,14},{7,15},{8,0},{9,1},... | collective-permute-start | bytes 3145736 | tf_op jit(solution)/shard_map/ppermute | solution.py:264
  55.1 31.2 %collective-permute-start.7 = (bf16[256,2048]{1,0:T(8,128)(2,1)S(1)}, bf16[256,2048]{1,0:T(8,128)(2,1)}, u32[]{:S(2)}, u32[]{:S(2)}) collective-permute-start(bf16[256,2048]{1,0:T(8,128)(2,1)S(1)} %collective-permute-done.3.refs_2_), channel_id=1, source_target_pairs={{0,8},{1,9},{2,10},{3,11},{4,12},{5,13},{6,14},{7,15},{8,0},{9,1},... | collective-permute-start | bytes 3145736 | tf_op jit(solution)/shard_map/ppermute | solution.py:264
  55.1 31.2 %collective-permute-start.2 = (bf16[256,2048]{1,0:T(8,128)(2,1)S(1)}, bf16[256,2048]{1,0:T(8,128)(2,1)}, u32[]{:S(2)}, u32[]{:S(2)}) collective-permute-start(bf16[256,2048]{1,0:T(8,128)(2,1)S(1)} %collective-permute-done.1.refs_4_), channel_id=1, source_target_pairs={{0,8},{1,9},{2,10},{3,11},{4,12},{5,13},{6,14},{7,15},{8,0},{9,1},... | collective-permute-start | bytes 3145736 | tf_op jit(solution)/shard_map/ppermute | solution.py:264
  55.6 30.7 %collective-permute-start.6 = (bf16[256,2048]{1,0:T(8,128)(2,1)}, bf16[256,2048]{1,0:T(8,128)(2,1)}, u32[]{:S(2)}, u32[]{:S(2)}) collective-permute-start(bf16[256,2048]{1,0:T(8,128)(2,1)} %collective-permute-done.refs_0_), channel_id=1, source_target_pairs={{0,8},{1,9},{2,10},{3,11},{4,12},{5,13},{6,14},{7,15},{8,0},{9,1},... | collective-permute-start | bytes 3145736 | tf_op jit(solution)/shard_map/ppermute | solution.py:264
  57.4 13.0 %all-to-all-start = ((bf16[8,128,256]{2,1,0:T(8,128)(2,1)}), bf16[8,128,256]{2,1,0:T(8,128)(2,1)}, u32[]{:S(2)}, u32[]{:S(2)}) async-start(bf16[8,128,256]{2,1,0:T(8,128)(2,1)} %broadcast_in_dim.3), calls=%async_computation | async-start | bytes 1048576 | tf_op jit(solution)/shard_map/all_to_all | solution.py:345
  74.3 5.4 %collective-permute-start.11 = (f32[128,128]{1,0:T(8,128)}, f32[128,128]{1,0:T(8,128)S(1)}, u32[]{:S(2)}, u32[]{:S(2)}) collective-permute-start(f32[128,128]{1,0:T(8,128)} %gram.3.part_ref), channel_id=1, source_target_pairs={{0,4},{1,5},{2,6},{3,7},{4,0},{5,1},{6,2},{7,3},{8,12},{9,13},{10,... | collective-permute-start | bytes 196616 | tf_op jit(solution)/shard_map/ppermute | solution.py:264
  96.2 14.1 %collective-permute-start.12 = (bf16[64,2048]{1,0:T(8,128)(2,1)}, bf16[64,2048]{1,0:T(8,128)(2,1)S(1)}, u32[]{:S(2)}, u32[]{:S(2)}) collective-permute-start(bf16[64,2048]{1,0:T(8,128)(2,1)} %step.6.refs_9_), channel_id=1, source_target_pairs={{0,4},{1,5},{2,6},{3,7},{4,0},{5,1},{6,2},{7,3},{8,12},{9,13},{10,... | collective-permute-start | bytes 786440 | tf_op jit(solution)/shard_map/ppermute | solution.py:264
  121.0 14.5 %collective-permute-start.13 = (bf16[64,2048]{1,0:T(8,128)(2,1)}, bf16[64,2048]{1,0:T(8,128)(2,1)S(1)}, u32[]{:S(2)}, u32[]{:S(2)}) collective-permute-start(bf16[64,2048]{1,0:T(8,128)(2,1)} %get-tuple-element.22.refs_9_), channel_id=1, source_target_pairs={{0,4},{1,5},{2,6},{3,7},{4,0},{5,1},{6,2},{7,3},{8,12},{9,13},{10,... | collective-permute-start | bytes 786440 | tf_op jit(solution)/shard_map/ppermute | solution.py:264
  173.4 6.4 %collective-permute-start.14 = (f32[128,128]{1,0:T(8,128)}, f32[128,128]{1,0:T(8,128)S(1)}, u32[]{:S(2)}, u32[]{:S(2)}) collective-permute-start(f32[128,128]{1,0:T(8,128)} %gram.4.part_ref), channel_id=1, source_target_pairs={{0,4},{1,5},{2,6},{3,7},{4,0},{5,1},{6,2},{7,3},{8,12},{9,13},{10,... | collective-permute-start | bytes 196616 | tf_op jit(solution)/shard_map/ppermute | solution.py:264
  193.5 12.8 %collective-permute-start.15 = (bf16[64,2048]{1,0:T(8,128)(2,1)}, bf16[64,2048]{1,0:T(8,128)(2,1)S(1)}, u32[]{:S(2)}, u32[]{:S(2)}) collective-permute-start(bf16[64,2048]{1,0:T(8,128)(2,1)} %step.9.refs_9_), channel_id=1, source_target_pairs={{0,4},{1,5},{2,6},{3,7},{4,0},{5,1},{6,2},{7,3},{8,12},{9,13},{10,... | collective-permute-start | bytes 786440 | tf_op jit(solution)/shard_map/ppermute | solution.py:264
  217.0 11.1 %collective-permute-start.16 = (bf16[64,2048]{1,0:T(8,128)(2,1)}, bf16[64,2048]{1,0:T(8,128)(2,1)S(1)}, u32[]{:S(2)}, u32[]{:S(2)}) collective-permute-start(bf16[64,2048]{1,0:T(8,128)(2,1)} %get-tuple-element.27.refs_9_), channel_id=1, source_target_pairs={{0,4},{1,5},{2,6},{3,7},{4,0},{5,1},{6,2},{7,3},{8,12},{9,13},{10,... | collective-permute-start | bytes 786440 | tf_op jit(solution)/shard_map/ppermute | solution.py:264
  252.0 13.3 %all-to-all-start.4 = ((bf16[16,64,256]{2,1,0:T(8,128)(2,1)}), bf16[16,64,256]{2,1,0:T(8,128)(2,1)S(1)}, u32[]{:S(2)}, u32[]{:S(2)}) async-start(bf16[16,64,256]{2,1,0:T(8,128)(2,1)} %fan.3), calls=%async_computation.4 | async-start | bytes 1048576 | tf_op jit(solution)/shard_map/all_to_all | solution.py:397
  266.5 8.9 %collective-permute-start.18 = (f32[64,256]{1,0:T(8,128)S(1)}, f32[64,256]{1,0:T(8,128)S(1)}, u32[]{:S(2)}, u32[]{:S(2)}) collective-permute-start(f32[64,256]{1,0:T(8,128)S(1)} %get-tuple-element.40), channel_id=1, source_target_pairs={{0,0},{1,1},{2,8},{3,9},{4,4},{5,5},{6,12},{7,13},{8,2},{9,3},{10,... | collective-permute-start | bytes 196616 | tf_op jit(solution)/shard_map/ppermute | solution.py:264
  267.1 8.2 %collective-permute-start.21 = (f32[64,256]{1,0:T(8,128)S(1)}, f32[64,256]{1,0:T(8,128)S(1)}, u32[]{:S(2)}, u32[]{:S(2)}) collective-permute-start(f32[64,256]{1,0:T(8,128)S(1)} %get-tuple-element.41), channel_id=1, source_target_pairs={{0,3},{1,2},{2,11},{3,10},{4,7},{5,6},{6,15},{7,14},{8,1},{9,0},{1... | collective-permute-start | bytes 196616 | tf_op jit(solution)/shard_map/ppermute | solution.py:264
  270.1 5.3 %collective-permute-start.20 = (f32[64,256]{1,0:T(8,128)S(1)}, f32[64,256]{1,0:T(8,128)S(1)}, u32[]{:S(2)}, u32[]{:S(2)}) collective-permute-start(f32[64,256]{1,0:T(8,128)S(1)} %get-tuple-element.42), channel_id=1, source_target_pairs={{0,2},{1,3},{2,10},{3,11},{4,6},{5,7},{6,14},{7,15},{8,0},{9,1},{1... | collective-permute-start | bytes 196616 | tf_op jit(solution)/shard_map/ppermute | solution.py:264
  270.1 5.3 %collective-permute-start.19 = (f32[64,256]{1,0:T(8,128)S(1)}, f32[64,256]{1,0:T(8,128)S(1)}, u32[]{:S(2)}, u32[]{:S(2)}) collective-permute-start(f32[64,256]{1,0:T(8,128)S(1)} %get-tuple-element.43), channel_id=1, source_target_pairs={{0,1},{1,0},{2,9},{3,8},{4,5},{5,4},{6,13},{7,12},{8,3},{9,2},{10,... | collective-permute-start | bytes 196616 | tf_op jit(solution)/shard_map/ppermute | solution.py:264
  273.4 6.8 %collective-permute-start.17 = (f32[128,128]{1,0:T(8,128)}, f32[128,128]{1,0:T(8,128)S(1)}, u32[]{:S(2)}, u32[]{:S(2)}) collective-permute-start(f32[128,128]{1,0:T(8,128)} %gram.5.part_ref), channel_id=1, source_target_pairs={{0,4},{1,5},{2,6},{3,7},{4,0},{5,1},{6,2},{7,3},{8,12},{9,13},{10,... | collective-permute-start | bytes 196616 | tf_op jit(solution)/shard_map/ppermute | solution.py:264
  (13 other events, 153.4 us)

commit v3 on v2

--- a/solution.py
+++ b/solution.py
@@ -14,6 +14,9 @@
 step_size = 0.5
 AXES = ("view", "samp")
 GROUP = 4
+
+SMALL = pltpu.CompilerParams(vmem_limit_bytes=4 << 20)
+LARGE = pltpu.CompilerParams(vmem_limit_bytes=16 << 20)
 
 
 def split(value):
@@ -76,17 +79,17 @@
         mixing_ref[...] = newton(total, part_ref[...] + other_ref[...])
 
     return pl.pallas_call(
-        kernel, out_shape=jax.ShapeDtypeStruct(pair[0].shape, jnp.float32), name="newton"
+        kernel, out_shape=jax.ShapeDtypeStruct(pair[0].shape, jnp.float32), name="newton", compiler_params=SMALL
     )(*pair)
 
 
-def newton_scores(total, pair, gathered, first_block, n_blocks):
+def newton_scores(total, pair, gathered, where, n_blocks):
     comps, sub = pair[0].shape[0], gathered.shape[2]
 
-    def kernel(first_ref, part_ref, other_ref, gathered_ref, out_ref):
+    def kernel(where_ref, part_ref, other_ref, gathered_ref, out_ref):
         mixing = newton(total, part_ref[...] + other_ref[...])
         for n in range(n_blocks):
-            sums = gathered_block(gathered_ref, first_ref[0] + n)
+            sums = gathered_block(gathered_ref, where_ref[2] + n)
             out_ref[pl.ds(n * sub, sub), :] = mixed_dot(mixing, sums).T
 
     vmem = pl.BlockSpec(memory_space=pltpu.VMEM)
@@ -96,7 +99,8 @@
         out_specs=vmem,
         out_shape=jax.ShapeDtypeStruct((n_blocks * sub, comps), jnp.float32),
         name="newton_scores",
-    )(first_block, *pair, gathered)
+        compiler_params=SMALL,
+    )(where, *pair, gathered)
 
 
 def gram_part(gathered):
@@ -112,7 +116,7 @@
         out_ref[...] = acc
 
     return pl.pallas_call(
-        kernel, out_shape=jax.ShapeDtypeStruct((2 * half_k, 2 * half_k), jnp.float32), name="gram"
+        kernel, out_shape=jax.ShapeDtypeStruct((2 * half_k, 2 * half_k), jnp.float32), name="gram", compiler_params=SMALL
     )(gathered)
 
 
@@ -128,7 +132,7 @@
             out_ref[i] = acc
 
     return pl.pallas_call(
-        kernel, out_shape=jax.ShapeDtypeStruct((2 * n, half_k, sub), jnp.bfloat16), name="fan"
+        kernel, out_shape=jax.ShapeDtypeStruct((2 * n, half_k, sub), jnp.bfloat16), name="fan", compiler_params=SMALL
     )(parts)
 
 
@@ -141,7 +145,7 @@
     half_k = (coeffs if coeffs is not None else values).shape[0]
     low = jnp.bfloat16
     vmem, smem = pl.BlockSpec(memory_space=pltpu.VMEM), pl.BlockSpec(memory_space=pltpu.SMEM)
-    args, specs, shapes = [where, *data], [smem] + [pl.BlockSpec(memory_space=pl.ANY)] * n_pieces, []
+    args, specs, shapes = [where, *data], [smem] + [vmem] * n_pieces, []
     names = []
 
     def give(name, *arrays):
@@ -172,16 +176,8 @@
         ins = dict(zip(names, refs[at : at + len(names)], strict=True))
         at += len(names)
         outs = dict(zip([name for name, _ in shapes], refs[at : at + len(shapes)], strict=True))
-        held, resid, sems = refs[at + len(shapes) :]
+        (resid,) = refs[at + len(shapes) :]
         base, core = where_ref[0], where_ref[1]
-
-        def copy(i):
-            return pltpu.make_async_copy(
-                pieces[i], held.at[pl.ds(i * piece_rows, piece_rows), :], sems.at[i]
-            )
-
-        for i in range(n_pieces):
-            copy(i).start()
 
         def block_at(i):
             own = core if i % 2 == 0 else 1 - core
@@ -209,8 +205,7 @@
                 outs["new_coeffs"][...] = weights
             weights = weights.astype(low)
             for i in range(n_pieces):
-                copy(i).wait()
-                value = tall_dot(weights, held[pl.ds(i * piece_rows, piece_rows), :])
+                value = tall_dot(weights, pieces[i][...])
                 if n_sub is not None:
                     outs["out_values"][:, pl.ds(i * piece_rows, piece_rows)] = value
                     ratio_out = piece_rows // sub
@@ -223,12 +218,18 @@
         else:
             for i in range(n_pieces):
                 set_resid(i, ins["values0"][:, pl.ds(i * piece_rows, piece_rows)])
-            for i in range(n_pieces):
-                copy(i).wait()
         if mixing is not None:
-            outs["term"][...] = jnp.dot(
-                resid[...], held[...], preferred_element_type=jnp.float32
-            ).astype(low)
+            wide = feats // 4
+            for n in range(4):
+                acc = None
+                for i in range(n_pieces):
+                    add = jnp.dot(
+                        resid[:, pl.ds(i * piece_rows, piece_rows)],
+                        pieces[i][:, pl.ds(n * wide, wide)],
+                        preferred_element_type=jnp.float32,
+                    )
+                    acc = add if acc is None else acc + add
+                outs["term"][:, pl.ds(n * wide, wide)] = acc.astype(low)
 
     return pl.pallas_call(
         kernel,
@@ -236,11 +237,10 @@
         out_specs=[vmem] * len(shapes),
         out_shape=[shape for _, shape in shapes],
         scratch_shapes=[
-            pltpu.VMEM((pooled, feats), low),
             pltpu.VMEM((half_k, pooled), low),
-            pltpu.SemaphoreType.DMA((n_pieces,)),
         ],
         name="step",
+        compiler_params=LARGE,
     )(*args)
 
 
@@ -284,12 +284,20 @@
         return value
 
 
-def pick(parts, index, axis=0):
-    return lax.dynamic_index_in_dim(parts, index, axis, keepdims=False)
-
-
-def pick(parts, index, axis=0):
-    return lax.dynamic_index_in_dim(parts, index, axis, keepdims=False)
+def pick(parts, index):
+    return lax.dynamic_index_in_dim(parts, index, 0, keepdims=False, allow_negative_indices=False)
+
+
+def cut(value, start, size, axis):
+    return lax.dynamic_slice_in_dim(value, start, size, axis, allow_negative_indices=False)
+
+
+def pick(parts, index):
+    return lax.dynamic_index_in_dim(parts, index, 0, keepdims=False, allow_negative_indices=False)
+
+
+def cut(value, start, size, axis):
+    return lax.dynamic_slice_in_dim(value, start, size, axis, allow_negative_indices=False)
 
 
 def body(view_data, init_coeffs):
@@ -299,20 +307,32 @@
     comps = init_coeffs.shape[2]
     half_k, half_rows = comps // 2, rows // 2
     total = rows * lax.axis_size("samp")
-    view_at, samp_at = lax.axis_index("view"), lax.axis_index("samp")
-    core = view_at % 2
-    square, corner = samp_at // GROUP, samp_at % GROUP
-    base = 2 * core + corner % 2
-    where = jnp.stack([base, core]).astype(jnp.int32)
     n_sub = GROUP * grid.planes
     sub = rows // grid.planes
+    out_rows = feats // lax.axis_size("samp")
+    view_at = lax.axis_index("view").astype(jnp.uint32)
+    samp_at = lax.axis_index("samp").astype(jnp.uint32)
+    core, other_core = view_at & 1, 1 - (view_at & 1)
+    corner = samp_at & (GROUP - 1)
+    base = 2 * core + (corner & 1)
+    own_view = corner & 1
+    holder = core == (corner >> 1)
+    where = jnp.stack([base, core, corner * grid.planes]).astype(jnp.int32)
+    pool_at = [((corner ^ k) & 1, ((corner ^ k) >> 1) * half_rows) for k in range(GROUP)]
+    own_at, their_at = core * half_rows, other_core * half_rows
+    out_at = [((samp_at & ~jnp.uint32(GROUP - 1)) + (base ^ k)) * out_rows for k in range(GROUP)]
+    order_at = [corner ^ r for r in range(GROUP)]
+    zero = jnp.uint32(0)
+    held = (core, other_core, own_view, holder, where, pool_at, own_at, their_at, out_at, order_at)
+    view_data, init_coeffs, held = lax.optimization_barrier((view_data, init_coeffs, held))
+    core, other_core, own_view, holder, where, pool_at, own_at, their_at, out_at, order_at = held
 
     slots = [None] * GROUP
 
     def pool(k):
-        m = corner ^ k
+        at = (*pool_at[k], zero)
         piece = lax.dynamic_slice(
-            view_data, (m % 2, (m // 2) * half_rows, 0), (1, half_rows, feats)
+            view_data, at, (1, half_rows, feats), allow_negative_indices=False
         )[0]
         slots[k] = grid.permute(
             piece, lambda a, c, q, p, k=k: (a, (p ^ k) // 2, q, 2 * c + (p ^ k) % 2)
@@ -332,8 +352,8 @@
         )
     pool(3)
     pool(2)
-    mine = lax.dynamic_slice_in_dim(part, core * half_rows, half_rows, 1)
-    theirs = lax.dynamic_slice_in_dim(part, (1 - core) * half_rows, half_rows, 1)
+    mine = cut(part, own_at, half_rows, 1)
+    theirs = cut(part, their_at, half_rows, 1)
     mine = mine + grid.swap_core(theirs)
     mine, init_later = lax.optimization_barrier((mine, init_coeffs))
     mine = grid.sum_planes(mine)
@@ -346,9 +366,9 @@
         jnp.broadcast_to(mine.astype(low), (2 * GROUP, comps, half_rows)),
         AXES, 0, 0, axis_index_groups=square_groups,
     )
-    local = jnp.transpose(pick(init_later, corner % 2)).reshape(2, half_k, feats)
-    from_core = grid.swap_core(pick(local, 1 - core))
-    coeffs = jnp.where(core == corner // 2, pick(local, core), from_core)
+    local = jnp.transpose(pick(init_later, own_view)).reshape(2, half_k, feats)
+    from_core = grid.swap_core(pick(local, other_core))
+    coeffs = jnp.where(holder, pick(local, core), from_core)
     gathered, coeffs = lax.optimization_barrier((gathered, coeffs))
     gathered = jnp.transpose(
         gathered.reshape(2 * GROUP, 2, half_k, half_rows // sub, sub), (1, 0, 3, 2, 4)
@@ -400,14 +420,11 @@
         if outer_step < OUTER - 1:
             mixing = newton_mixing(total, gram_pair(gathered))
     gathered, coeffs = lax.optimization_barrier((gathered, coeffs))
-    first_block = (corner * grid.planes).astype(jnp.int32).reshape(1)
-    shared = newton_scores(total, gram_pair(gathered), gathered, first_block, grid.planes)
-
-    out_rows = feats // lax.axis_size("samp")
+    shared = newton_scores(total, gram_pair(gathered), gathered, where, grid.planes)
+
     pieces = []
     for k in range(GROUP):
-        start = (square * GROUP + (base ^ k)) * out_rows
-        piece = lax.dynamic_slice_in_dim(coeffs, start, out_rows, 1)
+        piece = cut(coeffs, out_at[k], out_rows, 1)
         pieces.append(
             grid.permute(
                 piece,
@@ -415,7 +432,7 @@
             )
         )
     pieces = jnp.stack(pieces)
-    ordered = [pick(pieces, corner ^ r) for r in range(GROUP)]
+    ordered = [pick(pieces, order_at[r]) for r in range(GROUP)]
     final = jnp.stack(
         [jnp.concatenate([ordered[member], ordered[2 + member]], axis=0).T for member in range(2)]
     )

time: 290 us -> 247 us (0.85)
  Pallas kernels: 82.5 us -> 51 us
  waiting for transfers between devices: 101 us -> 92.5 us
  blocking collectives: 37.2 us -> 44.6 us
  local copies, waits for them, and re-layouts: 20.8 us -> 14.8 us
    pallas_call x6, Pallas kernels: 54.3 us -> 34.9 us  [step_call(): pl.pallas_call(kernel, in_specs=specs, out_specs=[vmem] * len(shapes), ou...]
    all_to_all x1 -> x2, blocking collectives: 14 us -> 24.8 us  [body(): lax.all_to_all(sum_and_fan(parts), AXES, 0, 0, axis_index_groups=gather_g...]
    all_to_all x1 -> x0, waiting for transfers between devices: 9.72 us -> none  [body(): lax.all_to_all(sum_and_fan(parts), AXES, 0, 0, axis_index_groups=gather_g...]
    pallas_call x3, Pallas kernels: 5.9 us -> 0.87 us  [gram_part(): pl.pallas_call(kernel, out_shape=jax.ShapeDtypeStruct((2 * half_k, 2 * ha...]
    unnamed x27 -> x7, local copies, waits for them, and re-layouts: 5.56 us -> 1.88 us
    all_to_all x1 -> x0, starting transfers between devices: 3.57 us -> none  [body(): lax.all_to_all(sum_and_fan(parts), AXES, 0, 0, axis_index_groups=gather_g...]
    pallas_call x2, Pallas kernels: 3.62 us -> 0.11 us  [sum_and_fan(): pl.pallas_call(kernel, out_shape=jax.ShapeDtypeStruct((2 * n, half_k, sub...]
    all_to_all x2, blocking collectives: 23.2 us -> 19.8 us  [body(): parts = lax.all_to_all(parts, AXES, 0, 0, axis_index_groups=reduce_groups)]
  transfers between devices with their start and end apart: 24 -> 23, of which waited for: 12 -> 12; matrix products, arithmetic and copies ran while one was open for 5% -> 5% of each run, Pallas kernels for 3% -> 2%
where the time goes in v3:
time: 247 us; the launch traced here: 246 us
  waiting for transfers between devices  92.5 us (37%)
  Pallas kernels  51 us (21%)
  blocking collectives  44.6 us (18%)
  starting transfers between devices  38.3 us (16%)
  local copies, waits for them, and re-layouts  14.8 us (6%)
    ppermute x22, waiting for transfers between devices, permute(): return lax.ppermute(value, AXES, pairs)  85.7 us
    pallas_call x6, Pallas kernels, step_call(): pl.pallas_call(kernel, in_specs=specs, out_specs=[vmem] * len(shapes), ou...  34.9 us
    ppermute x22, starting transfers between devices, permute(): return lax.ppermute(value, AXES, pairs)  34 us
    all_to_all x2, blocking collectives, body(): lax.all_to_all(sum_and_fan(parts), AXES, 0, 0, axis_index_groups=gather_g...  24.8 us
    all_to_all x2, blocking collectives, body(): parts = lax.all_to_all(parts, AXES, 0, 0, axis_index_groups=reduce_groups)  19.8 us
    pallas_call x2, Pallas kernels, newton_mixing(): pl.pallas_call(kernel, out_shape=jax.ShapeDtypeStruct(pair[0].shape, jnp....  9.04 us
    all_to_all x1, waiting for transfers between devices, body(): lax.all_to_all(jnp.broadcast_to(mine.astype(low), (2 * GROUP, comps, half...  6.77 us
    pallas_call x1, Pallas kernels, newton_scores(): pl.pallas_call(kernel, in_specs=[pl.BlockSpec(memory_space=pltpu.SMEM), v...  6.06 us
  transfers between devices with their start and end apart: 23, of which 12 were waited for; matrix products, arithmetic and copies ran while one was open for 5% of the time, Pallas kernels for 2%

profile of v3, /device:TPU:0, one launch (start us, length us, event | category | flops | bytes accessed | tf_op | source)
XLA Modules:
  0.0 246.1 jit_solution(16670925428687079332)
XLA Ops:
  0.7 5.2 %dynamic-slice_bitcast_fusion.1 = (bf16[256,2048]{1,0:T(8,128)(2,1)}, bf16[256,2048]{1,0:T(8,128)(2,1)}, bf16[256,2048]{1,0:T(8,128)(2,1)}, bf16[256,2048]{1,0:T(8,128)(2,1)}) fusion(bf16[2,512,2048]{2,1,0:T(8,128)(2,1)} %param.2, u32[]{:T(128)S(6)} %and.34, u32[]{:T(128)S(6)} %mul.41, u32[]{:T(128)S(6)} %and.32, u32[]{:T(128)S(6)} %mul.39, u32[]{:T(128)S(6)} %and.33, ...), kind=kLoop, calls=%fused_computation.8 | loop fusion | bytes 8388640 | tf_op jit(solution)/shard_map/squeeze | solution.py:334
  10.1 9.5 %collective-permute-start = (bf16[256,2048]{1,0:T(8,128)(2,1)}, bf16[256,2048]{1,0:T(8,128)(2,1)}, u32[]{:S(2)}, u32[]{:S(2)}) collective-permute-start(bf16[256,2048]{1,0:T(8,128)(2,1)} %get-tuple-element.89), channel_id=1, source_target_pairs={{0,0},{1,1},{2,8},{3,9},{4,4},{5,5},{6,12},{7,13},{8,2},{9,3},{10,... | collective-permute-start | bytes 3145736 | tf_op jit(solution)/shard_map/ppermute | solution.py:264
  30.4 13.0 %collective-permute-done.4.refs_6_ = bf16[256,2048]{1,0:T(8,128)(2,1)S(1)} collective-permute-done((bf16[256,2048]{1,0:T(8,128)(2,1)}, bf16[256,2048]{1,0:T(8,128)(2,1)S(1)}, u32[]{:S(2)}, u32[]{:S(2)}) %collective-permute-start.4) | collective-permute-done | bytes 1048608 | tf_op jit(solution)/shard_map/ppermute | solution.py:264
  44.5 11.1 %collective-permute-done.3.refs_2_ = bf16[256,2048]{1,0:T(8,128)(2,1)S(1)} collective-permute-done((bf16[256,2048]{1,0:T(8,128)(2,1)}, bf16[256,2048]{1,0:T(8,128)(2,1)S(1)}, u32[]{:S(2)}, u32[]{:S(2)}) %collective-permute-start.3) | collective-permute-done | bytes 1048608 | tf_op jit(solution)/shard_map/ppermute | solution.py:264
  57.9 4.3 %all-to-all-start = ((bf16[8,128,256]{2,1,0:T(8,128)(2,1)}), bf16[8,128,256]{2,1,0:T(8,128)(2,1)}, u32[]{:S(2)}, u32[]{:S(2)}) async-start(bf16[8,128,256]{2,1,0:T(8,128)(2,1)} %broadcast_in_dim.3), calls=%async_computation | async-start | bytes 1048576 | tf_op jit(solution)/shard_map/all_to_all | solution.py:365
  64.2 6.8 %all-to-all-done = bf16[8,128,256]{2,1,0:T(8,128)(2,1)} async-done(((bf16[8,128,256]{2,1,0:T(8,128)(2,1)}), bf16[8,128,256]{2,1,0:T(8,128)(2,1)}, u32[]{:S(2)}, u32[]{:S(2)}) %all-to-all-start) | async-done | bytes 524320 | tf_op jit(solution)/shard_map/all_to_all | solution.py:365
  77.6 4.5 %newton.2.refs_9_.refs_11_ = f32[128,128]{1,0:T(8,128)S(1)} custom-call(f32[128,128]{1,0:T(8,128)S(1)} %gram.3.part_ref, f32[128,128]{1,0:T(8,128)S(1)} %collective-permute-done.11.other_ref), custom_call_target="tpu_custom_call" | custom-call | tf_op jit(solution)/shard_map/newton/pallas_call | solution.py:81
  83.2 6.5 %step.6.refs_9_ = bf16[64,2048]{1,0:T(8,128)(2,1)S(1)} custom-call(s32[3]{0:T(128)S(1)} %add_convert_fusion.1.where_ref, bf16[256,2048]{1,0:T(8,128)(2,1)} %collective-permute-done.refs_0_, bf16[256,2048]{1,0:T(8,128)(2,1)} %collective-permute-done.2.refs_1_, bf16[256,2048]{1,0:T(8,128)(2,1)S(1)} %collective-permute-done.3.refs_2_, ...), custom_call_target="tpu_custom_call" | custom-call | tf_op jit(solution)/shard_map/step/pallas_call | solution.py:234
  92.4 11.1 %collective-permute-done.12.refs_10_ = bf16[64,2048]{1,0:T(8,128)(2,1)S(1)} collective-permute-done((bf16[64,2048]{1,0:T(8,128)(2,1)S(1)}, bf16[64,2048]{1,0:T(8,128)(2,1)S(1)}, u32[]{:S(2)}, u32[]{:S(2)}) %collective-permute-start.12) | collective-permute-done | bytes 262176 | tf_op jit(solution)/shard_map/ppermute | solution.py:264
  103.6 6.5 %step.7 = (f32[64,2048]{1,0:T(8,128)S(1)}, bf16[64,2048]{1,0:T(8,128)(2,1)S(1)}) custom-call(s32[3]{0:T(128)S(1)} %add_convert_fusion.1.where_ref, bf16[256,2048]{1,0:T(8,128)(2,1)} %collective-permute-done.refs_0_, bf16[256,2048]{1,0:T(8,128)(2,1)} %collective-permute-done.2.refs_1_, bf16[256,2048]{1,0:T(8,128)(2,1)S(1)} %collective-permute-done.3.refs_2_, ...), custom_call_target="tpu_custom_call" | custom-call | tf_op jit(solution)/shard_map/step/pallas_call | solution.py:234
  110.1 14.2 %collective-permute-done.13.refs_10_ = bf16[64,2048]{1,0:T(8,128)(2,1)S(1)} collective-permute-done((bf16[64,2048]{1,0:T(8,128)(2,1)S(1)}, bf16[64,2048]{1,0:T(8,128)(2,1)S(1)}, u32[]{:S(2)}, u32[]{:S(2)}) %collective-permute-start.13) | collective-permute-done | bytes 262176 | tf_op jit(solution)/shard_map/ppermute | solution.py:264
  124.3 5.2 %step.8 = (f32[64,2048]{1,0:T(8,128)S(1)}, f32[64,2048]{1,0:T(8,128)S(1)}, bf16[8,64,256]{2,1,0:T(8,128)(2,1)S(1)}) custom-call(s32[3]{0:T(128)S(1)} %add_convert_fusion.1.where_ref, bf16[256,2048]{1,0:T(8,128)(2,1)} %collective-permute-done.refs_0_, bf16[256,2048]{1,0:T(8,128)(2,1)} %collective-permute-done.2.refs_1_, ...), custom_call_target="tpu_custom_call" | custom-call | tf_op jit(solution)/shard_map/step/pallas_call | solution.py:234
  129.5 9.2 %all_to_all.25.parts_ref = bf16[8,64,256]{2,1,0:T(8,128)(2,1)S(1)} all-to-all(bf16[8,64,256]{2,1,0:T(8,128)(2,1)S(1)} %get-tuple-element.67), channel_id=1, replica_groups={{0,16,1,17,2,18,3,19},{4,20,5,21,6,22,7,23},{8,24,9,25,10,26,11,27},{12..., dimensions={0} | all-to-all | bytes 524288 | tf_op jit(solution)/shard_map/all_to_all | solution.py:416
  138.8 12.4 %all_to_all.26.gathered_ref.refs_10_.refs_12_ = bf16[16,64,256]{2,1,0:T(8,128)(2,1)S(1)} all-to-all(bf16[16,64,256]{2,1,0:T(8,128)(2,1)S(1)} %fan.2), channel_id=1, replica_groups={{0,16,1,17,2,18,3,19,8,24,9,25,10,26,11,27},{4,20,5,21,6,22,7,23,12,28,..., dimensions={0} | all-to-all | bytes 1048576 | tf_op jit(solution)/shard_map/all_to_all | solution.py:417
  153.7 4.1 %collective-permute-done.14.other_ref = f32[128,128]{1,0:T(8,128)S(1)} collective-permute-done((f32[128,128]{1,0:T(8,128)S(1)}, f32[128,128]{1,0:T(8,128)S(1)}, u32[]{:S(2)}, u32[]{:S(2)}) %collective-permute-start.14) | collective-permute-done | bytes 65568 | tf_op jit(solution)/shard_map/ppermute | solution.py:264
  157.8 4.5 %newton.3.refs_9_.refs_11_ = f32[128,128]{1,0:T(8,128)S(1)} custom-call(f32[128,128]{1,0:T(8,128)S(1)} %gram.4.part_ref, f32[128,128]{1,0:T(8,128)S(1)} %collective-permute-done.14.other_ref), custom_call_target="tpu_custom_call" | custom-call | tf_op jit(solution)/shard_map/newton/pallas_call | solution.py:81
  162.3 4.3 %step.9.refs_9_ = bf16[64,2048]{1,0:T(8,128)(2,1)S(1)} custom-call(s32[3]{0:T(128)S(1)} %add_convert_fusion.1.where_ref, bf16[256,2048]{1,0:T(8,128)(2,1)} %collective-permute-done.refs_0_, bf16[256,2048]{1,0:T(8,128)(2,1)} %collective-permute-done.2.refs_1_, bf16[256,2048]{1,0:T(8,128)(2,1)S(1)} %collective-permute-done.3.refs_2_, ...), custom_call_target="tpu_custom_call" | custom-call | tf_op jit(solution)/shard_map/step/pallas_call | solution.py:234
  167.7 11.4 %collective-permute-done.15.refs_10_ = bf16[64,2048]{1,0:T(8,128)(2,1)S(1)} collective-permute-done((bf16[64,2048]{1,0:T(8,128)(2,1)S(1)}, bf16[64,2048]{1,0:T(8,128)(2,1)S(1)}, u32[]{:S(2)}, u32[]{:S(2)}) %collective-permute-start.15) | collective-permute-done | bytes 262176 | tf_op jit(solution)/shard_map/ppermute | solution.py:264
  179.2 6.5 %step.10 = (f32[64,2048]{1,0:T(8,128)S(1)}, bf16[64,2048]{1,0:T(8,128)(2,1)S(1)}) custom-call(s32[3]{0:T(128)S(1)} %add_convert_fusion.1.where_ref, bf16[256,2048]{1,0:T(8,128)(2,1)} %collective-permute-done.refs_0_, bf16[256,2048]{1,0:T(8,128)(2,1)} %collective-permute-done.2.refs_1_, bf16[256,2048]{1,0:T(8,128)(2,1)S(1)} %collective-permute-done.3.refs_2_, ...), custom_call_target="tpu_custom_call" | custom-call | tf_op jit(solution)/shard_map/step/pallas_call | solution.py:234
  185.7 13.1 %collective-permute-done.16.refs_10_ = bf16[64,2048]{1,0:T(8,128)(2,1)S(1)} collective-permute-done((bf16[64,2048]{1,0:T(8,128)(2,1)S(1)}, bf16[64,2048]{1,0:T(8,128)(2,1)S(1)}, u32[]{:S(2)}, u32[]{:S(2)}) %collective-permute-start.16) | collective-permute-done | bytes 262176 | tf_op jit(solution)/shard_map/ppermute | solution.py:264
  198.8 6.0 %step.11 = (f32[64,2048]{1,0:T(8,128)S(1)}, f32[64,2048]{1,0:T(8,128)}, bf16[8,64,256]{2,1,0:T(8,128)(2,1)S(1)}) custom-call(s32[3]{0:T(128)S(1)} %add_convert_fusion.1.where_ref, bf16[256,2048]{1,0:T(8,128)(2,1)} %collective-permute-done.refs_0_, bf16[256,2048]{1,0:T(8,128)(2,1)} %collective-permute-done.2.refs_1_, ...), custom_call_target="tpu_custom_call" | custom-call | tf_op jit(solution)/shard_map/step/pallas_call | solution.py:234
  204.8 10.6 %all_to_all.27.parts_ref = bf16[8,64,256]{2,1,0:T(8,128)(2,1)S(1)} all-to-all(bf16[8,64,256]{2,1,0:T(8,128)(2,1)S(1)} %get-tuple-element.70), channel_id=1, replica_groups={{0,16,1,17,2,18,3,19},{4,20,5,21,6,22,7,23},{8,24,9,25,10,26,11,27},{12..., dimensions={0} | all-to-all | bytes 524288 | tf_op jit(solution)/shard_map/all_to_all | solution.py:416
  215.4 12.4 %all_to_all.28.gathered_ref = bf16[16,64,256]{2,1,0:T(8,128)(2,1)S(1)} all-to-all(bf16[16,64,256]{2,1,0:T(8,128)(2,1)S(1)} %fan.3), channel_id=1, replica_groups={{0,16,1,17,2,18,3,19,8,24,9,25,10,26,11,27},{4,20,5,21,6,22,7,23,12,28,..., dimensions={0} | all-to-all | bytes 1048576 | tf_op jit(solution)/shard_map/all_to_all | solution.py:417
  240.0 6.1 %newton_scores.1 = f32[512,128]{1,0:T(8,128)} custom-call(s32[3]{0:T(128)S(1)} %add_convert_fusion.1.where_ref, f32[128,128]{1,0:T(8,128)S(1)} %gram.5.part_ref, f32[128,128]{1,0:T(8,128)S(1)} %collective-permute-done.17.other_ref, bf16[16,64,256]{2,1,0:T(8,128)(2,1)S(1)} %all_to_all.28.gathered_ref), custom_call_target="tpu_custom_call" | custom-call | tf_op jit(solution)/shard_map/newton_scores/pallas_call | solution.py:96
  (66 shorter events, 46.7 us)
Async XLA Ops:
  0.7 18.9 %copy-start.2 = (bf16[2,512,2048]{2,1,0:T(8,128)(2,1)S(1)}, bf16[2,512,2048]{2,1,0:T(8,128)(2,1)}, u32[]{:S(2)}) copy-start(bf16[2,512,2048]{2,1,0:T(8,128)(2,1)} %param.2) | copy-start | bytes 12582916
  5.9 37.5 %collective-permute-start.4 = (bf16[256,2048]{1,0:T(8,128)(2,1)}, bf16[256,2048]{1,0:T(8,128)(2,1)S(1)}, u32[]{:S(2)}, u32[]{:S(2)}) collective-permute-start(bf16[256,2048]{1,0:T(8,128)(2,1)} %get-tuple-element.86), channel_id=1, source_target_pairs={{0,9},{1,8},{2,1},{3,0},{4,13},{5,12},{6,5},{7,4},{8,11},{9,10},{1... | collective-permute-start | bytes 3145736 | tf_op jit(solution)/shard_map/ppermute | solution.py:264
  8.4 47.3 %collective-permute-start.3 = (bf16[256,2048]{1,0:T(8,128)(2,1)}, bf16[256,2048]{1,0:T(8,128)(2,1)S(1)}, u32[]{:S(2)}, u32[]{:S(2)}) collective-permute-start(bf16[256,2048]{1,0:T(8,128)(2,1)} %get-tuple-element.87), channel_id=1, source_target_pairs={{0,1},{1,0},{2,9},{3,8},{4,5},{5,4},{6,13},{7,12},{8,3},{9,2},{10,... | collective-permute-start | bytes 3145736 | tf_op jit(solution)/shard_map/ppermute | solution.py:264
  8.9 46.7 %collective-permute-start.1 = (bf16[256,2048]{1,0:T(8,128)(2,1)}, bf16[256,2048]{1,0:T(8,128)(2,1)S(1)}, u32[]{:S(2)}, u32[]{:S(2)}) collective-permute-start(bf16[256,2048]{1,0:T(8,128)(2,1)} %get-tuple-element.88), channel_id=1, source_target_pairs={{0,8},{1,9},{2,0},{3,1},{4,12},{5,13},{6,4},{7,5},{8,10},{9,11},{1... | collective-permute-start | bytes 3145736 | tf_op jit(solution)/shard_map/ppermute | solution.py:264
  10.1 46.1 %collective-permute-start = (bf16[256,2048]{1,0:T(8,128)(2,1)}, bf16[256,2048]{1,0:T(8,128)(2,1)}, u32[]{:S(2)}, u32[]{:S(2)}) collective-permute-start(bf16[256,2048]{1,0:T(8,128)(2,1)} %get-tuple-element.89), channel_id=1, source_target_pairs={{0,0},{1,1},{2,8},{3,9},{4,4},{5,5},{6,12},{7,13},{8,2},{9,3},{10,... | collective-permute-start | bytes 3145736 | tf_op jit(solution)/shard_map/ppermute | solution.py:264
  21.5 1.4 collective-permute-start.8
  23.0 7.4 %collective-permute-start.9 = (f32[128,256]{1,0:T(8,128)S(1)}, f32[128,256]{1,0:T(8,128)S(1)}, u32[]{:S(2)}, u32[]{:S(2)}) collective-permute-start(f32[128,256]{1,0:T(8,128)S(1)} %dynamic-slice_add_fusion), channel_id=1, source_target_pairs={{0,16},{1,17},{2,18},{3,19},{4,20},{5,21},{6,22},{7,23},{8,24},{9,... | collective-permute-start | bytes 393224 | tf_op jit(solution)/shard_map/ppermute | solution.py:264
  30.4 31.9 %collective-permute-start.10 = (f32[64,2048]{1,0:T(8,128)}, f32[64,2048]{1,0:T(8,128)}, u32[]{:S(2)}, u32[]{:S(2)}) collective-permute-start(f32[64,2048]{1,0:T(8,128)} %dynamic-slice_bitcast_fusion.5), channel_id=1, source_target_pairs={{0,8},{1,9},{2,10},{3,11},{4,12},{5,13},{6,14},{7,15},{8,0},{9,1},... | collective-permute-start | bytes 1572872 | tf_op jit(solution)/shard_map/ppermute | solution.py:264
  43.5 38.6 %collective-permute-start.5 = (bf16[256,2048]{1,0:T(8,128)(2,1)S(1)}, bf16[256,2048]{1,0:T(8,128)(2,1)}, u32[]{:S(2)}, u32[]{:S(2)}) collective-permute-start(bf16[256,2048]{1,0:T(8,128)(2,1)S(1)} %collective-permute-done.4.refs_6_), channel_id=1, source_target_pairs={{0,8},{1,9},{2,10},{3,11},{4,12},{5,13},{6,14},{7,15},{8,0},{9,1},... | collective-permute-start | bytes 3145736 | tf_op jit(solution)/shard_map/ppermute | solution.py:264
  55.6 26.5 %collective-permute-start.7 = (bf16[256,2048]{1,0:T(8,128)(2,1)S(1)}, bf16[256,2048]{1,0:T(8,128)(2,1)}, u32[]{:S(2)}, u32[]{:S(2)}) collective-permute-start(bf16[256,2048]{1,0:T(8,128)(2,1)S(1)} %collective-permute-done.3.refs_2_), channel_id=1, source_target_pairs={{0,8},{1,9},{2,10},{3,11},{4,12},{5,13},{6,14},{7,15},{8,0},{9,1},... | collective-permute-start | bytes 3145736 | tf_op jit(solution)/shard_map/ppermute | solution.py:264
  55.6 26.5 %collective-permute-start.2 = (bf16[256,2048]{1,0:T(8,128)(2,1)S(1)}, bf16[256,2048]{1,0:T(8,128)(2,1)}, u32[]{:S(2)}, u32[]{:S(2)}) collective-permute-start(bf16[256,2048]{1,0:T(8,128)(2,1)S(1)} %collective-permute-done.1.refs_4_), channel_id=1, source_target_pairs={{0,8},{1,9},{2,10},{3,11},{4,12},{5,13},{6,14},{7,15},{8,0},{9,1},... | collective-permute-start | bytes 3145736 | tf_op jit(solution)/shard_map/ppermute | solution.py:264
  56.1 26.0 %collective-permute-start.6 = (bf16[256,2048]{1,0:T(8,128)(2,1)}, bf16[256,2048]{1,0:T(8,128)(2,1)}, u32[]{:S(2)}, u32[]{:S(2)}) collective-permute-start(bf16[256,2048]{1,0:T(8,128)(2,1)} %collective-permute-done.refs_0_), channel_id=1, source_target_pairs={{0,8},{1,9},{2,10},{3,11},{4,12},{5,13},{6,14},{7,15},{8,0},{9,1},... | collective-permute-start | bytes 3145736 | tf_op jit(solution)/shard_map/ppermute | solution.py:264
  57.9 13.0 %all-to-all-start = ((bf16[8,128,256]{2,1,0:T(8,128)(2,1)}), bf16[8,128,256]{2,1,0:T(8,128)(2,1)}, u32[]{:S(2)}, u32[]{:S(2)}) async-start(bf16[8,128,256]{2,1,0:T(8,128)(2,1)} %broadcast_in_dim.3), calls=%async_computation | async-start | bytes 1048576 | tf_op jit(solution)/shard_map/all_to_all | solution.py:365
  72.4 5.2 %collective-permute-start.11 = (f32[128,128]{1,0:T(8,128)S(1)}, f32[128,128]{1,0:T(8,128)S(1)}, u32[]{:S(2)}, u32[]{:S(2)}) collective-permute-start(f32[128,128]{1,0:T(8,128)S(1)} %gram.3.part_ref), channel_id=1, source_target_pairs={{0,4},{1,5},{2,6},{3,7},{4,0},{5,1},{6,2},{7,3},{8,12},{9,13},{10,... | collective-permute-start | bytes 196616 | tf_op jit(solution)/shard_map/ppermute | solution.py:264
  89.7 13.9 %collective-permute-start.12 = (bf16[64,2048]{1,0:T(8,128)(2,1)S(1)}, bf16[64,2048]{1,0:T(8,128)(2,1)S(1)}, u32[]{:S(2)}, u32[]{:S(2)}) collective-permute-start(bf16[64,2048]{1,0:T(8,128)(2,1)S(1)} %step.6.refs_9_), channel_id=1, source_target_pairs={{0,4},{1,5},{2,6},{3,7},{4,0},{5,1},{6,2},{7,3},{8,12},{9,13},{10,... | collective-permute-start | bytes 786440 | tf_op jit(solution)/shard_map/ppermute | solution.py:264
  110.1 14.3 %collective-permute-start.13 = (bf16[64,2048]{1,0:T(8,128)(2,1)S(1)}, bf16[64,2048]{1,0:T(8,128)(2,1)S(1)}, u32[]{:S(2)}, u32[]{:S(2)}) collective-permute-start(bf16[64,2048]{1,0:T(8,128)(2,1)S(1)} %get-tuple-element.64.refs_9_), channel_id=1, source_target_pairs={{0,4},{1,5},{2,6},{3,7},{4,0},{5,1},{6,2},{7,3},{8,12},{9,13},{10,... | collective-permute-start | bytes 786440 | tf_op jit(solution)/shard_map/ppermute | solution.py:264
  151.5 6.3 %collective-permute-start.14 = (f32[128,128]{1,0:T(8,128)S(1)}, f32[128,128]{1,0:T(8,128)S(1)}, u32[]{:S(2)}, u32[]{:S(2)}) collective-permute-start(f32[128,128]{1,0:T(8,128)S(1)} %gram.4.part_ref), channel_id=1, source_target_pairs={{0,4},{1,5},{2,6},{3,7},{4,0},{5,1},{6,2},{7,3},{8,12},{9,13},{10,... | collective-permute-start | bytes 196616 | tf_op jit(solution)/shard_map/ppermute | solution.py:264
  166.6 12.6 %collective-permute-start.15 = (bf16[64,2048]{1,0:T(8,128)(2,1)S(1)}, bf16[64,2048]{1,0:T(8,128)(2,1)S(1)}, u32[]{:S(2)}, u32[]{:S(2)}) collective-permute-start(bf16[64,2048]{1,0:T(8,128)(2,1)S(1)} %step.9.refs_9_), channel_id=1, source_target_pairs={{0,4},{1,5},{2,6},{3,7},{4,0},{5,1},{6,2},{7,3},{8,12},{9,13},{10,... | collective-permute-start | bytes 786440 | tf_op jit(solution)/shard_map/ppermute | solution.py:264
  185.7 13.2 %collective-permute-start.16 = (bf16[64,2048]{1,0:T(8,128)(2,1)S(1)}, bf16[64,2048]{1,0:T(8,128)(2,1)S(1)}, u32[]{:S(2)}, u32[]{:S(2)}) collective-permute-start(bf16[64,2048]{1,0:T(8,128)(2,1)S(1)} %get-tuple-element.69.refs_9_), channel_id=1, source_target_pairs={{0,4},{1,5},{2,6},{3,7},{4,0},{5,1},{6,2},{7,3},{8,12},{9,13},{10,... | collective-permute-start | bytes 786440 | tf_op jit(solution)/shard_map/ppermute | solution.py:264
  228.0 7.3 %collective-permute-start.18 = (f32[64,256]{1,0:T(8,128)S(1)}, f32[64,256]{1,0:T(8,128)S(1)}, u32[]{:S(2)}, u32[]{:S(2)}) collective-permute-start(f32[64,256]{1,0:T(8,128)S(1)} %get-tuple-element.90), channel_id=1, source_target_pairs={{0,0},{1,1},{2,8},{3,9},{4,4},{5,5},{6,12},{7,13},{8,2},{9,3},{10,... | collective-permute-start | bytes 196616 | tf_op jit(solution)/shard_map/ppermute | solution.py:264
  228.7 6.6 %collective-permute-start.21 = (f32[64,256]{1,0:T(8,128)S(1)}, f32[64,256]{1,0:T(8,128)S(1)}, u32[]{:S(2)}, u32[]{:S(2)}) collective-permute-start(f32[64,256]{1,0:T(8,128)S(1)} %get-tuple-element.91), channel_id=1, source_target_pairs={{0,3},{1,2},{2,11},{3,10},{4,7},{5,6},{6,15},{7,14},{8,1},{9,0},{1... | collective-permute-start | bytes 196616 | tf_op jit(solution)/shard_map/ppermute | solution.py:264
  231.6 3.7 %collective-permute-start.20 = (f32[64,256]{1,0:T(8,128)S(1)}, f32[64,256]{1,0:T(8,128)S(1)}, u32[]{:S(2)}, u32[]{:S(2)}) collective-permute-start(f32[64,256]{1,0:T(8,128)S(1)} %get-tuple-element.92), channel_id=1, source_target_pairs={{0,2},{1,3},{2,10},{3,11},{4,6},{5,7},{6,14},{7,15},{8,0},{9,1},{1... | collective-permute-start | bytes 196616 | tf_op jit(solution)/shard_map/ppermute | solution.py:264
  231.6 4.3 %collective-permute-start.19 = (f32[64,256]{1,0:T(8,128)S(1)}, f32[64,256]{1,0:T(8,128)S(1)}, u32[]{:S(2)}, u32[]{:S(2)}) collective-permute-start(f32[64,256]{1,0:T(8,128)S(1)} %get-tuple-element.93), channel_id=1, source_target_pairs={{0,1},{1,0},{2,9},{3,8},{4,5},{5,4},{6,13},{7,12},{8,3},{9,2},{10,... | collective-permute-start | bytes 196616 | tf_op jit(solution)/shard_map/ppermute | solution.py:264
  233.3 6.7 %collective-permute-start.17 = (f32[128,128]{1,0:T(8,128)S(1)}, f32[128,128]{1,0:T(8,128)S(1)}, u32[]{:S(2)}, u32[]{:S(2)}) collective-permute-start(f32[128,128]{1,0:T(8,128)S(1)} %gram.5.part_ref), channel_id=1, source_target_pairs={{0,4},{1,5},{2,6},{3,7},{4,0},{5,1},{6,2},{7,3},{8,12},{9,13},{10,... | collective-permute-start | bytes 196616 | tf_op jit(solution)/shard_map/ppermute | solution.py:264
  (2 other events, 19.8 us)

commit v4 on v3

--- a/solution.py
+++ b/solution.py
@@ -69,7 +69,9 @@
     return inverse * jnp.sqrt(total / scale)
 
 
-def gathered_block(gathered_ref, index):
+def gathered_block(gathered_ref, index, comps):
+    if gathered_ref.shape[1] == comps:
+        return gathered_ref[index]
     half = gathered_ref.shape[0] // 2
     return jnp.concatenate([gathered_ref[index], gathered_ref[half + index]], axis=0)
 
@@ -89,7 +91,7 @@
     def kernel(where_ref, part_ref, other_ref, gathered_ref, out_ref):
         mixing = newton(total, part_ref[...] + other_ref[...])
         for n in range(n_blocks):
-            sums = gathered_block(gathered_ref, where_ref[2] + n)
+            sums = gathered_block(gathered_ref, where_ref[2] + n, comps)
             out_ref[pl.ds(n * sub, sub), :] = mixed_dot(mixing, sums).T
 
     vmem = pl.BlockSpec(memory_space=pltpu.VMEM)
@@ -103,21 +105,46 @@
     )(where, *pair, gathered)
 
 
-def gram_part(gathered):
-    half, half_k, _ = gathered.shape
-    half = half // 2
+def gram_part(gathered, comps):
+    count = gathered.shape[0] * gathered.shape[1] // comps
 
     def kernel(gathered_ref, out_ref):
         acc = None
-        for n in range(half):
-            sums = gathered_block(gathered_ref, n)
+        for n in range(count):
+            sums = gathered_block(gathered_ref, n, comps)
             add = tall_dot(sums, sums)
             acc = add if acc is None else acc + add
         out_ref[...] = acc
 
     return pl.pallas_call(
-        kernel, out_shape=jax.ShapeDtypeStruct((2 * half_k, 2 * half_k), jnp.float32), name="gram", compiler_params=SMALL
+        kernel,
+        out_shape=jax.ShapeDtypeStruct((comps, comps), jnp.float32),
+        name="gram",
+        compiler_params=SMALL,
     )(gathered)
+
+
+def first_coeffs(init_coeffs, where):
+    _, feats, comps = init_coeffs.shape
+    half_k = comps // 2
+
+    def kernel(where_ref, init_ref, own_ref, other_ref):
+        turned = init_ref[where_ref[3]].T
+        first, second = turned[:half_k], turned[half_k:]
+        swap = where_ref[1] == 1
+        own_ref[...] = jnp.where(swap, second, first)
+        other_ref[...] = jnp.where(swap, first, second)
+
+    vmem = pl.BlockSpec(memory_space=pltpu.VMEM)
+    half = jax.ShapeDtypeStruct((half_k, feats), jnp.float32)
+    return pl.pallas_call(
+        kernel,
+        in_specs=[pl.BlockSpec(memory_space=pltpu.SMEM), vmem],
+        out_specs=[vmem, vmem],
+        out_shape=[half, half],
+        name="first_coeffs",
+        compiler_params=LARGE,
+    )(where, init_coeffs)
 
 
 def sum_and_fan(parts):
@@ -137,7 +164,15 @@
 
 
 def step_call(
-    total, where, data, coeffs=None, grads=None, values=None, mixing=None, gathered=None, n_sub=None
+    total,
+    where,
+    data,
+    coeffs=None,
+    grads=None,
+    values=None,
+    mixing=None,
+    gathered=None,
+    n_sub=None,
 ):
     piece_rows, feats = data[0].shape
     n_pieces = len(data)
@@ -190,7 +225,8 @@
 
             def set_resid(i, value):
                 sums = [
-                    gathered_block(ins["gathered0"], block_at(i) * ratio + r) for r in range(ratio)
+                    gathered_block(ins["gathered0"], block_at(i) * ratio + r, 2 * half_k)
+                    for r in range(ratio)
                 ]
                 sums = sums[0] if ratio == 1 else jnp.concatenate(sums, axis=1)
                 resid[:, pl.ds(i * piece_rows, piece_rows)] = (
@@ -305,35 +341,39 @@
     grid = Grid(lax.axis_size("view"), lax.axis_size("samp"))
     rows, feats = view_data.shape[1:]
     comps = init_coeffs.shape[2]
-    half_k, half_rows = comps // 2, rows // 2
+    half_rows = rows // 2
     total = rows * lax.axis_size("samp")
     n_sub = GROUP * grid.planes
-    sub = rows // grid.planes
     out_rows = feats // lax.axis_size("samp")
     view_at = lax.axis_index("view").astype(jnp.uint32)
     samp_at = lax.axis_index("samp").astype(jnp.uint32)
     core, other_core = view_at & 1, 1 - (view_at & 1)
     corner = samp_at & (GROUP - 1)
     base = 2 * core + (corner & 1)
-    own_view = corner & 1
-    holder = core == (corner >> 1)
-    where = jnp.stack([base, core, corner * grid.planes]).astype(jnp.int32)
+    holder = (core == (corner >> 1)).astype(jnp.uint32)
+    where = jnp.stack([base, core, corner * grid.planes, corner & 1]).astype(jnp.int32)
     pool_at = [((corner ^ k) & 1, ((corner ^ k) >> 1) * half_rows) for k in range(GROUP)]
     own_at, their_at = core * half_rows, other_core * half_rows
     out_at = [((samp_at & ~jnp.uint32(GROUP - 1)) + (base ^ k)) * out_rows for k in range(GROUP)]
     order_at = [corner ^ r for r in range(GROUP)]
     zero = jnp.uint32(0)
-    held = (core, other_core, own_view, holder, where, pool_at, own_at, their_at, out_at, order_at)
+    held = (where, holder, pool_at, own_at, their_at, out_at, order_at)
     view_data, init_coeffs, held = lax.optimization_barrier((view_data, init_coeffs, held))
-    core, other_core, own_view, holder, where, pool_at, own_at, their_at, out_at, order_at = held
+    where, holder, pool_at, own_at, their_at, out_at, order_at = held
 
     slots = [None] * GROUP
 
+    def slice_piece(source, k):
+        at = (*pool_at[k], zero)
+        return lax.dynamic_slice(source, at, (1, half_rows, feats), allow_negative_indices=False)[0]
+
+    early = [slice_piece(view_data, 1), slice_piece(view_data, 0)]
+    view_later, *early = lax.optimization_barrier((view_data, *early))
+    late = [slice_piece(view_later, 3), slice_piece(view_later, 2)]
+    cut_pieces = {1: early[0], 0: early[1], 3: late[0], 2: late[1]}
+
     def pool(k):
-        at = (*pool_at[k], zero)
-        piece = lax.dynamic_slice(
-            view_data, at, (1, half_rows, feats), allow_negative_indices=False
-        )[0]
+        piece = cut_pieces[k]
         slots[k] = grid.permute(
             piece, lambda a, c, q, p, k=k: (a, (p ^ k) // 2, q, 2 * c + (p ^ k) % 2)
         )
@@ -355,7 +395,6 @@
     mine = cut(part, own_at, half_rows, 1)
     theirs = cut(part, their_at, half_rows, 1)
     mine = mine + grid.swap_core(theirs)
-    mine, init_later = lax.optimization_barrier((mine, init_coeffs))
     mine = grid.sum_planes(mine)
     square_groups = [
         [grid.encode(a, c, q, p) for p in range(GROUP) for c in range(2)]
@@ -366,20 +405,20 @@
         jnp.broadcast_to(mine.astype(low), (2 * GROUP, comps, half_rows)),
         AXES, 0, 0, axis_index_groups=square_groups,
     )
-    local = jnp.transpose(pick(init_later, own_view)).reshape(2, half_k, feats)
-    from_core = grid.swap_core(pick(local, other_core))
-    coeffs = jnp.where(holder, pick(local, core), from_core)
+    coeffs, for_core = first_coeffs(init_coeffs, where)
+    from_core = grid.swap_core(for_core)
+    coeffs = jnp.where(holder == 1, coeffs, from_core)
     gathered, coeffs = lax.optimization_barrier((gathered, coeffs))
-    gathered = jnp.transpose(
-        gathered.reshape(2 * GROUP, 2, half_k, half_rows // sub, sub), (1, 0, 3, 2, 4)
-    ).reshape(2 * n_sub, half_k, sub)
-
+
+    shared_slots = {}
+    for k in range(GROUP):
+        shared_slots[k ^ 2] = grid.swap_core(slots[k])
     data = []
     for k in range(GROUP):
-        data += [slots[k], grid.swap_core(slots[k ^ 2])]
+        data += [slots[k], shared_slots[k]]
 
     def gram_pair(gathered):
-        return grid.sum_squares(gram_part(gathered), jnp.float32)
+        return grid.sum_squares(gram_part(gathered, comps), jnp.float32)
 
     pair = gram_pair(gathered)
     mixing = newton_mixing(total, pair)
@@ -414,13 +453,11 @@
         )
         grads = None
         parts = lax.all_to_all(parts, AXES, 0, 0, axis_index_groups=reduce_groups)
-        gathered = lax.all_to_all(
-            sum_and_fan(parts), AXES, 0, 0, axis_index_groups=gather_groups
-        )
+        gathered = lax.all_to_all(sum_and_fan(parts), AXES, 0, 0, axis_index_groups=gather_groups)
         if outer_step < OUTER - 1:
             mixing = newton_mixing(total, gram_pair(gathered))
-    gathered, coeffs = lax.optimization_barrier((gathered, coeffs))
-    shared = newton_scores(total, gram_pair(gathered), gathered, where, grid.planes)
+    pair = gram_pair(gathered)
+    shared = newton_scores(total, pair, gathered, where, grid.planes)
 
     pieces = []
     for k in range(GROUP):

time: 247 us -> 243 us (0.984)
  blocking collectives: 44.6 us -> 32.4 us
  starting transfers between devices: 38.3 us -> 47.1 us
  local copies, waits for them, and re-layouts: 14.8 us -> 7.68 us
  Pallas kernels: 51 us -> 54.7 us
  waiting for transfers between devices: 92.5 us -> 96 us
    all_to_all x2 -> x1, blocking collectives: 24.8 us -> 12.4 us  [body(): lax.all_to_all(sum_and_fan(parts), AXES, 0, 0, axis_index_groups=gather_g...]
    ppermute x22, starting transfers between devices: 34 us -> 39.2 us  [permute(): return lax.ppermute(value, AXES, pairs)]
    transpose x3 -> x0, local copies, waits for them, and re-layouts: 4.7 us -> none  [the longest x2 3.62 us: body(): local = jnp.transpose(pick(init_later, own_view)).reshape(2, half_k, feats)]
    all_to_all x0 -> x1, starting transfers between devices: none -> 3.57 us  [body(): lax.all_to_all(sum_and_fan(parts), AXES, 0, 0, axis_index_groups=gather_g...]
    ppermute x22, waiting for transfers between devices: 85.7 us -> 89.2 us  [permute(): return lax.ppermute(value, AXES, pairs)]
    pallas_call x3 -> x4, Pallas kernels: 0.87 us -> 3.6 us  [the longest x3 1.92 us: gram_part(): pl.pallas_call(kernel, out_shape=jax.ShapeDtypeStruct((comps, comps), jnp...]
    squeeze x1 -> x2, local copies, waits for them, and re-layouts: 5.19 us -> 2.82 us  [slice_piece(): lax.dynamic_slice(source, at, (1, half_rows, feats), allow_negative_indic...]
  transfers between devices with their start and end apart: 23 -> 24, of which waited for: 12 -> 14; matrix products, arithmetic and copies ran while one was open for 5% -> 3% of each run, Pallas kernels for 2% -> 3%
where the time goes in v4:
time: 243 us
  waiting for transfers between devices  96 us (40%)
  Pallas kernels  54.7 us (23%)
  starting transfers between devices  47.1 us (19%)
  blocking collectives  32.4 us (13%)
  local copies, waits for them, and re-layouts  7.68 us (3%)
    ppermute x22, waiting for transfers between devices, permute(): return lax.ppermute(value, AXES, pairs)  89.2 us
    ppermute x22, starting transfers between devices, permute(): return lax.ppermute(value, AXES, pairs)  39.2 us
    pallas_call x6, Pallas kernels, step_call(): pl.pallas_call(kernel, in_specs=specs, out_specs=[vmem] * len(shapes), ou...  35.1 us
    all_to_all x2, blocking collectives, body(): parts = lax.all_to_all(parts, AXES, 0, 0, axis_index_groups=reduce_groups)  20 us
    all_to_all x1, blocking collectives, body(): lax.all_to_all(sum_and_fan(parts), AXES, 0, 0, axis_index_groups=gather_g...  12.4 us
    pallas_call x2, Pallas kernels, newton_mixing(): pl.pallas_call(kernel, out_shape=jax.ShapeDtypeStruct(pair[0].shape, jnp....  9.04 us
    all_to_all x1, waiting for transfers between devices, body(): lax.all_to_all(jnp.broadcast_to(mine.astype(low), (2 * GROUP, comps, half...  6.78 us
    pallas_call x1, Pallas kernels, newton_scores(): pl.pallas_call(kernel, in_specs=[pl.BlockSpec(memory_space=pltpu.SMEM), v...  6.06 us
  transfers between devices with their start and end apart: 24, of which 14 were waited for; matrix products, arithmetic and copies ran while one was open for 3% of the time, Pallas kernels for 3%

profile of v4, /device:TPU:0, one launch (start us, length us, event | category | flops | bytes accessed | tf_op | source)
XLA Modules:
  0.0 242.8 jit_solution(6241685262279856675)
XLA Ops:
  21.3 11.7 %collective-permute-start.7 = (bf16[256,2048]{1,0:T(8,128)(2,1)S(1)}, bf16[256,2048]{1,0:T(8,128)(2,1)}, u32[]{:S(2)}, u32[]{:S(2)}) collective-permute-start(bf16[256,2048]{1,0:T(8,128)(2,1)S(1)} %collective-permute-done.3.refs_2_), channel_id=1, source_target_pairs={{0,8},{1,9},{2,10},{3,11},{4,12},{5,13},{6,14},{7,15},{8,0},{9,1},... | collective-permute-start | bytes 3145736 | tf_op jit(solution)/shard_map/ppermute | solution.py:300
  32.9 20.0 %collective-permute-done.4.refs_6_ = bf16[256,2048]{1,0:T(8,128)(2,1)S(1)} collective-permute-done((bf16[256,2048]{1,0:T(8,128)(2,1)S(1)}, bf16[256,2048]{1,0:T(8,128)(2,1)S(1)}, u32[]{:S(2)}, u32[]{:S(2)}) %collective-permute-start.4) | collective-permute-done | bytes 1048608 | tf_op jit(solution)/shard_map/ppermute | solution.py:300
  55.6 4.3 %all-to-all-start = ((bf16[8,128,256]{2,1,0:T(8,128)(2,1)}), bf16[8,128,256]{2,1,0:T(8,128)(2,1)}, u32[]{:S(2)}, u32[]{:S(2)}) async-start(bf16[8,128,256]{2,1,0:T(8,128)(2,1)} %broadcast_in_dim.3), calls=%async_computation | async-start | bytes 1048576 | tf_op jit(solution)/shard_map/all_to_all | solution.py:404
  61.9 6.8 %all-to-all-done.gathered_ref.refs_10_.refs_12_ = bf16[8,128,256]{2,1,0:T(8,128)(2,1)} async-done(((bf16[8,128,256]{2,1,0:T(8,128)(2,1)}), bf16[8,128,256]{2,1,0:T(8,128)(2,1)}, u32[]{:S(2)}, u32[]{:S(2)}) %all-to-all-start) | async-done | bytes 524320 | tf_op jit(solution)/shard_map/all_to_all | solution.py:404
  75.2 4.5 %newton.2.refs_9_.refs_11_ = f32[128,128]{1,0:T(8,128)S(1)} custom-call(f32[128,128]{1,0:T(8,128)S(1)} %gram.3.part_ref, f32[128,128]{1,0:T(8,128)S(1)} %collective-permute-done.11.other_ref), custom_call_target="tpu_custom_call" | custom-call | tf_op jit(solution)/shard_map/newton/pallas_call | solution.py:83
  80.8 6.6 %step.6.refs_9_ = bf16[64,2048]{1,0:T(8,128)(2,1)S(1)} custom-call(s32[4]{0:T(128)S(1)} %add_convert_fusion.1.where_ref, bf16[256,2048]{1,0:T(8,128)(2,1)S(1)} %collective-permute-done.refs_0_, bf16[256,2048]{1,0:T(8,128)(2,1)} %collective-permute-done.2.refs_1_, bf16[256,2048]{1,0:T(8,128)(2,1)S(1)} %collective-permute-done.3.refs_2_, ...), custom_call_target="tpu_custom_call" | custom-call | tf_op jit(solution)/shard_map/step/pallas_call | solution.py:270
  90.2 11.1 %collective-permute-done.12.refs_10_ = bf16[64,2048]{1,0:T(8,128)(2,1)S(1)} collective-permute-done((bf16[64,2048]{1,0:T(8,128)(2,1)S(1)}, bf16[64,2048]{1,0:T(8,128)(2,1)S(1)}, u32[]{:S(2)}, u32[]{:S(2)}) %collective-permute-start.12) | collective-permute-done | bytes 262176 | tf_op jit(solution)/shard_map/ppermute | solution.py:300
  101.3 6.6 %step.7 = (f32[64,2048]{1,0:T(8,128)S(1)}, bf16[64,2048]{1,0:T(8,128)(2,1)S(1)}) custom-call(s32[4]{0:T(128)S(1)} %add_convert_fusion.1.where_ref, bf16[256,2048]{1,0:T(8,128)(2,1)S(1)} %collective-permute-done.refs_0_, bf16[256,2048]{1,0:T(8,128)(2,1)} %collective-permute-done.2.refs_1_, bf16[256,2048]{1,0:T(8,128)(2,1)S(1)} %collective-permute-done.3.refs_2_, ...), custom_call_target="tpu_custom_call" | custom-call | tf_op jit(solution)/shard_map/step/pallas_call | solution.py:270
  108.0 14.2 %collective-permute-done.13.refs_10_ = bf16[64,2048]{1,0:T(8,128)(2,1)S(1)} collective-permute-done((bf16[64,2048]{1,0:T(8,128)(2,1)S(1)}, bf16[64,2048]{1,0:T(8,128)(2,1)S(1)}, u32[]{:S(2)}, u32[]{:S(2)}) %collective-permute-start.13) | collective-permute-done | bytes 262176 | tf_op jit(solution)/shard_map/ppermute | solution.py:300
  122.1 5.2 %step.8 = (f32[64,2048]{1,0:T(8,128)S(1)}, f32[64,2048]{1,0:T(8,128)S(1)}, bf16[8,64,256]{2,1,0:T(8,128)(2,1)S(1)}) custom-call(s32[4]{0:T(128)S(1)} %add_convert_fusion.1.where_ref, bf16[256,2048]{1,0:T(8,128)(2,1)S(1)} %collective-permute-done.refs_0_, bf16[256,2048]{1,0:T(8,128)(2,1)} %collective-permute-done.2.refs_1_, ...), custom_call_target="tpu_custom_call" | custom-call | tf_op jit(solution)/shard_map/step/pallas_call | solution.py:270
  127.3 9.4 %all_to_all.25.parts_ref = bf16[8,64,256]{2,1,0:T(8,128)(2,1)S(1)} all-to-all(bf16[8,64,256]{2,1,0:T(8,128)(2,1)S(1)} %get-tuple-element.65), channel_id=1, replica_groups={{0,16,1,17,2,18,3,19},{4,20,5,21,6,22,7,23},{8,24,9,25,10,26,11,27},{12..., dimensions={0} | all-to-all | bytes 524288 | tf_op jit(solution)/shard_map/all_to_all | solution.py:455
  136.8 12.4 %all_to_all.26.gathered_ref.refs_10_.refs_12_ = bf16[16,64,256]{2,1,0:T(8,128)(2,1)S(1)} all-to-all(bf16[16,64,256]{2,1,0:T(8,128)(2,1)S(1)} %fan.2), channel_id=1, replica_groups={{0,16,1,17,2,18,3,19,8,24,9,25,10,26,11,27},{4,20,5,21,6,22,7,23,12,28,..., dimensions={0} | all-to-all | bytes 1048576 | tf_op jit(solution)/shard_map/all_to_all | solution.py:456
  151.7 4.1 %collective-permute-done.14.other_ref = f32[128,128]{1,0:T(8,128)S(1)} collective-permute-done((f32[128,128]{1,0:T(8,128)S(1)}, f32[128,128]{1,0:T(8,128)S(1)}, u32[]{:S(2)}, u32[]{:S(2)}) %collective-permute-start.14) | collective-permute-done | bytes 65568 | tf_op jit(solution)/shard_map/ppermute | solution.py:300
  155.8 4.5 %newton.3.refs_9_.refs_11_ = f32[128,128]{1,0:T(8,128)S(1)} custom-call(f32[128,128]{1,0:T(8,128)S(1)} %gram.4.part_ref, f32[128,128]{1,0:T(8,128)S(1)} %collective-permute-done.14.other_ref), custom_call_target="tpu_custom_call" | custom-call | tf_op jit(solution)/shard_map/newton/pallas_call | solution.py:83
  160.3 4.3 %step.9.refs_9_ = bf16[64,2048]{1,0:T(8,128)(2,1)S(1)} custom-call(s32[4]{0:T(128)S(1)} %add_convert_fusion.1.where_ref, bf16[256,2048]{1,0:T(8,128)(2,1)S(1)} %collective-permute-done.refs_0_, bf16[256,2048]{1,0:T(8,128)(2,1)} %collective-permute-done.2.refs_1_, bf16[256,2048]{1,0:T(8,128)(2,1)S(1)} %collective-permute-done.3.refs_2_, ...), custom_call_target="tpu_custom_call" | custom-call | tf_op jit(solution)/shard_map/step/pallas_call | solution.py:270
  165.7 11.4 %collective-permute-done.15.refs_10_ = bf16[64,2048]{1,0:T(8,128)(2,1)S(1)} collective-permute-done((bf16[64,2048]{1,0:T(8,128)(2,1)S(1)}, bf16[64,2048]{1,0:T(8,128)(2,1)S(1)}, u32[]{:S(2)}, u32[]{:S(2)}) %collective-permute-start.15) | collective-permute-done | bytes 262176 | tf_op jit(solution)/shard_map/ppermute | solution.py:300
  177.2 6.5 %step.10 = (f32[64,2048]{1,0:T(8,128)S(1)}, bf16[64,2048]{1,0:T(8,128)(2,1)S(1)}) custom-call(s32[4]{0:T(128)S(1)} %add_convert_fusion.1.where_ref, bf16[256,2048]{1,0:T(8,128)(2,1)S(1)} %collective-permute-done.refs_0_, bf16[256,2048]{1,0:T(8,128)(2,1)} %collective-permute-done.2.refs_1_, bf16[256,2048]{1,0:T(8,128)(2,1)S(1)} %collective-permute-done.3.refs_2_, ...), custom_call_target="tpu_custom_call" | custom-call | tf_op jit(solution)/shard_map/step/pallas_call | solution.py:270
  183.7 13.0 %collective-permute-done.16.refs_10_ = bf16[64,2048]{1,0:T(8,128)(2,1)S(1)} collective-permute-done((bf16[64,2048]{1,0:T(8,128)(2,1)S(1)}, bf16[64,2048]{1,0:T(8,128)(2,1)S(1)}, u32[]{:S(2)}, u32[]{:S(2)}) %collective-permute-start.16) | collective-permute-done | bytes 262176 | tf_op jit(solution)/shard_map/ppermute | solution.py:300
  196.7 6.0 %step.11 = (f32[64,2048]{1,0:T(8,128)S(1)}, f32[64,2048]{1,0:T(8,128)}, bf16[8,64,256]{2,1,0:T(8,128)(2,1)S(1)}) custom-call(s32[4]{0:T(128)S(1)} %add_convert_fusion.1.where_ref, bf16[256,2048]{1,0:T(8,128)(2,1)S(1)} %collective-permute-done.refs_0_, bf16[256,2048]{1,0:T(8,128)(2,1)} %collective-permute-done.2.refs_1_, ...), custom_call_target="tpu_custom_call" | custom-call | tf_op jit(solution)/shard_map/step/pallas_call | solution.py:270
  202.7 10.6 %all_to_all.27.parts_ref = bf16[8,64,256]{2,1,0:T(8,128)(2,1)S(1)} all-to-all(bf16[8,64,256]{2,1,0:T(8,128)(2,1)S(1)} %get-tuple-element.68), channel_id=1, replica_groups={{0,16,1,17,2,18,3,19},{4,20,5,21,6,22,7,23},{8,24,9,25,10,26,11,27},{12..., dimensions={0} | all-to-all | bytes 524288 | tf_op jit(solution)/shard_map/all_to_all | solution.py:455
  219.6 4.3 %collective-permute-start.21 = (f32[64,256]{1,0:T(8,128)S(1)}, f32[64,256]{1,0:T(8,128)S(1)}, u32[]{:S(2)}, u32[]{:S(2)}) collective-permute-start(f32[64,256]{1,0:T(8,128)S(1)} %get-tuple-element.85), channel_id=1, source_target_pairs={{0,3},{1,2},{2,11},{3,10},{4,7},{5,6},{6,15},{7,14},{8,1},{9,0},{1... | collective-permute-start | bytes 196616 | tf_op jit(solution)/shard_map/ppermute | solution.py:300
  224.6 3.9 %collective-permute-done.21 = f32[64,256]{1,0:T(8,128)S(1)} collective-permute-done((f32[64,256]{1,0:T(8,128)S(1)}, f32[64,256]{1,0:T(8,128)S(1)}, u32[]{:S(2)}, u32[]{:S(2)}) %collective-permute-start.21) | collective-permute-done | bytes 65568 | tf_op jit(solution)/shard_map/ppermute | solution.py:300
  232.3 4.4 %collective-permute-done.17.other_ref = f32[128,128]{1,0:T(8,128)S(1)} collective-permute-done((f32[128,128]{1,0:T(8,128)S(1)}, f32[128,128]{1,0:T(8,128)S(1)}, u32[]{:S(2)}, u32[]{:S(2)}) %collective-permute-start.17) | collective-permute-done | bytes 65568 | tf_op jit(solution)/shard_map/ppermute | solution.py:300
  236.7 6.1 %newton_scores.1 = f32[512,128]{1,0:T(8,128)} custom-call(s32[4]{0:T(128)S(1)} %add_convert_fusion.1.where_ref, f32[128,128]{1,0:T(8,128)S(1)} %gram.5.part_ref, f32[128,128]{1,0:T(8,128)S(1)} %collective-permute-done.17.other_ref, bf16[16,64,256]{2,1,0:T(8,128)(2,1)S(1)} %all-to-all-done.4.gathered_ref), custom_call_target="tpu_custom_call" | custom-call | tf_op jit(solution)/shard_map/newton_scores/pallas_call | solution.py:98
  (69 shorter events, 49.9 us)
Async XLA Ops:
  3.0 17.8 %collective-permute-start = (bf16[256,2048]{1,0:T(8,128)(2,1)S(1)}, bf16[256,2048]{1,0:T(8,128)(2,1)S(1)}, u32[]{:S(2)}, u32[]{:S(2)}) collective-permute-start(bf16[256,2048]{1,0:T(8,128)(2,1)S(1)} %get-tuple-element.46), channel_id=1, source_target_pairs={{0,0},{1,1},{2,8},{3,9},{4,4},{5,5},{6,12},{7,13},{8,2},{9,3},{10,... | collective-permute-start | bytes 3145736 | tf_op jit(solution)/shard_map/ppermute | solution.py:300
  3.9 17.4 %collective-permute-start.3 = (bf16[256,2048]{1,0:T(8,128)(2,1)S(1)}, bf16[256,2048]{1,0:T(8,128)(2,1)S(1)}, u32[]{:S(2)}, u32[]{:S(2)}) collective-permute-start(bf16[256,2048]{1,0:T(8,128)(2,1)S(1)} %get-tuple-element.50), channel_id=1, source_target_pairs={{0,1},{1,0},{2,9},{3,8},{4,5},{5,4},{6,13},{7,12},{8,3},{9,2},{10,... | collective-permute-start | bytes 3145736 | tf_op jit(solution)/shard_map/ppermute | solution.py:300
  7.5 45.4 %collective-permute-start.4 = (bf16[256,2048]{1,0:T(8,128)(2,1)S(1)}, bf16[256,2048]{1,0:T(8,128)(2,1)S(1)}, u32[]{:S(2)}, u32[]{:S(2)}) collective-permute-start(bf16[256,2048]{1,0:T(8,128)(2,1)S(1)} %get-tuple-element.80), channel_id=1, source_target_pairs={{0,9},{1,8},{2,1},{3,0},{4,13},{5,12},{6,5},{7,4},{8,11},{9,10},{1... | collective-permute-start | bytes 3145736 | tf_op jit(solution)/shard_map/ppermute | solution.py:300
  10.1 44.6 %collective-permute-start.1 = (bf16[256,2048]{1,0:T(8,128)(2,1)S(1)}, bf16[256,2048]{1,0:T(8,128)(2,1)}, u32[]{:S(2)}, u32[]{:S(2)}) collective-permute-start(bf16[256,2048]{1,0:T(8,128)(2,1)S(1)} %get-tuple-element.81), channel_id=1, source_target_pairs={{0,8},{1,9},{2,0},{3,1},{4,12},{5,13},{6,4},{7,5},{8,10},{9,11},{1... | collective-permute-start | bytes 3145736 | tf_op jit(solution)/shard_map/ppermute | solution.py:300
  12.0 2.8 %collective-permute-start.8 = (f32[128,256]{1,0:T(8,128)S(1)}, f32[128,256]{1,0:T(8,128)S(1)}, u32[]{:S(2)}, u32[]{:S(2)}) collective-permute-start(f32[128,256]{1,0:T(8,128)S(1)} %constant_dynamic-slice_fusion.4), channel_id=1, source_target_pairs={{0,8},{1,9},{2,10},{3,11},{4,12},{5,13},{6,14},{7,15},{8,0},{9,1},... | collective-permute-start | bytes 393224 | tf_op jit(solution)/shard_map/ppermute | solution.py:300
  14.9 5.8 %collective-permute-start.9 = (f32[128,256]{1,0:T(8,128)S(1)}, f32[128,256]{1,0:T(8,128)S(1)}, u32[]{:S(2)}, u32[]{:S(2)}) collective-permute-start(f32[128,256]{1,0:T(8,128)S(1)} %dynamic-slice_add_fusion), channel_id=1, source_target_pairs={{0,16},{1,17},{2,18},{3,19},{4,20},{5,21},{6,22},{7,23},{8,24},{9,... | collective-permute-start | bytes 393224 | tf_op jit(solution)/shard_map/ppermute | solution.py:300
  20.8 39.2 %collective-permute-start.10 = (f32[64,2048]{1,0:T(8,128)}, f32[64,2048]{1,0:T(8,128)}, u32[]{:S(2)}, u32[]{:S(2)}) collective-permute-start(f32[64,2048]{1,0:T(8,128)} %get-tuple-element.58), channel_id=1, source_target_pairs={{0,8},{1,9},{2,10},{3,11},{4,12},{5,13},{6,14},{7,15},{8,0},{9,1},... | collective-permute-start | bytes 1572872 | tf_op jit(solution)/shard_map/ppermute | solution.py:300
  20.8 59.0 %collective-permute-start.6 = (bf16[256,2048]{1,0:T(8,128)(2,1)S(1)}, bf16[256,2048]{1,0:T(8,128)(2,1)}, u32[]{:S(2)}, u32[]{:S(2)}) collective-permute-start(bf16[256,2048]{1,0:T(8,128)(2,1)S(1)} %collective-permute-done.refs_0_), channel_id=1, source_target_pairs={{0,8},{1,9},{2,10},{3,11},{4,12},{5,13},{6,14},{7,15},{8,0},{9,1},... | collective-permute-start | bytes 3145736 | tf_op jit(solution)/shard_map/ppermute | solution.py:300
  21.3 58.5 %collective-permute-start.7 = (bf16[256,2048]{1,0:T(8,128)(2,1)S(1)}, bf16[256,2048]{1,0:T(8,128)(2,1)}, u32[]{:S(2)}, u32[]{:S(2)}) collective-permute-start(bf16[256,2048]{1,0:T(8,128)(2,1)S(1)} %collective-permute-done.3.refs_2_), channel_id=1, source_target_pairs={{0,8},{1,9},{2,10},{3,11},{4,12},{5,13},{6,14},{7,15},{8,0},{9,1},... | collective-permute-start | bytes 3145736 | tf_op jit(solution)/shard_map/ppermute | solution.py:300
  52.9 26.8 %collective-permute-start.5 = (bf16[256,2048]{1,0:T(8,128)(2,1)S(1)}, bf16[256,2048]{1,0:T(8,128)(2,1)}, u32[]{:S(2)}, u32[]{:S(2)}) collective-permute-start(bf16[256,2048]{1,0:T(8,128)(2,1)S(1)} %collective-permute-done.4.refs_6_), channel_id=1, source_target_pairs={{0,8},{1,9},{2,10},{3,11},{4,12},{5,13},{6,14},{7,15},{8,0},{9,1},... | collective-permute-start | bytes 3145736 | tf_op jit(solution)/shard_map/ppermute | solution.py:300
  54.7 25.1 %collective-permute-start.2 = (bf16[256,2048]{1,0:T(8,128)(2,1)}, bf16[256,2048]{1,0:T(8,128)(2,1)}, u32[]{:S(2)}, u32[]{:S(2)}) collective-permute-start(bf16[256,2048]{1,0:T(8,128)(2,1)} %collective-permute-done.1.refs_4_), channel_id=1, source_target_pairs={{0,8},{1,9},{2,10},{3,11},{4,12},{5,13},{6,14},{7,15},{8,0},{9,1},... | collective-permute-start | bytes 3145736 | tf_op jit(solution)/shard_map/ppermute | solution.py:300
  55.6 13.0 %all-to-all-start = ((bf16[8,128,256]{2,1,0:T(8,128)(2,1)}), bf16[8,128,256]{2,1,0:T(8,128)(2,1)}, u32[]{:S(2)}, u32[]{:S(2)}) async-start(bf16[8,128,256]{2,1,0:T(8,128)(2,1)} %broadcast_in_dim.3), calls=%async_computation | async-start | bytes 1048576 | tf_op jit(solution)/shard_map/all_to_all | solution.py:404
  70.0 5.2 %collective-permute-start.11 = (f32[128,128]{1,0:T(8,128)S(1)}, f32[128,128]{1,0:T(8,128)S(1)}, u32[]{:S(2)}, u32[]{:S(2)}) collective-permute-start(f32[128,128]{1,0:T(8,128)S(1)} %gram.3.part_ref), channel_id=1, source_target_pairs={{0,4},{1,5},{2,6},{3,7},{4,0},{5,1},{6,2},{7,3},{8,12},{9,13},{10,... | collective-permute-start | bytes 196616 | tf_op jit(solution)/shard_map/ppermute | solution.py:300
  87.4 13.9 %collective-permute-start.12 = (bf16[64,2048]{1,0:T(8,128)(2,1)S(1)}, bf16[64,2048]{1,0:T(8,128)(2,1)S(1)}, u32[]{:S(2)}, u32[]{:S(2)}) collective-permute-start(bf16[64,2048]{1,0:T(8,128)(2,1)S(1)} %step.6.refs_9_), channel_id=1, source_target_pairs={{0,4},{1,5},{2,6},{3,7},{4,0},{5,1},{6,2},{7,3},{8,12},{9,13},{10,... | collective-permute-start | bytes 786440 | tf_op jit(solution)/shard_map/ppermute | solution.py:300
  107.9 14.3 %collective-permute-start.13 = (bf16[64,2048]{1,0:T(8,128)(2,1)S(1)}, bf16[64,2048]{1,0:T(8,128)(2,1)S(1)}, u32[]{:S(2)}, u32[]{:S(2)}) collective-permute-start(bf16[64,2048]{1,0:T(8,128)(2,1)S(1)} %get-tuple-element.62.refs_9_), channel_id=1, source_target_pairs={{0,4},{1,5},{2,6},{3,7},{4,0},{5,1},{6,2},{7,3},{8,12},{9,13},{10,... | collective-permute-start | bytes 786440 | tf_op jit(solution)/shard_map/ppermute | solution.py:300
  149.5 6.3 %collective-permute-start.14 = (f32[128,128]{1,0:T(8,128)S(1)}, f32[128,128]{1,0:T(8,128)S(1)}, u32[]{:S(2)}, u32[]{:S(2)}) collective-permute-start(f32[128,128]{1,0:T(8,128)S(1)} %gram.4.part_ref), channel_id=1, source_target_pairs={{0,4},{1,5},{2,6},{3,7},{4,0},{5,1},{6,2},{7,3},{8,12},{9,13},{10,... | collective-permute-start | bytes 196616 | tf_op jit(solution)/shard_map/ppermute | solution.py:300
  164.6 12.6 %collective-permute-start.15 = (bf16[64,2048]{1,0:T(8,128)(2,1)S(1)}, bf16[64,2048]{1,0:T(8,128)(2,1)S(1)}, u32[]{:S(2)}, u32[]{:S(2)}) collective-permute-start(bf16[64,2048]{1,0:T(8,128)(2,1)S(1)} %step.9.refs_9_), channel_id=1, source_target_pairs={{0,4},{1,5},{2,6},{3,7},{4,0},{5,1},{6,2},{7,3},{8,12},{9,13},{10,... | collective-permute-start | bytes 786440 | tf_op jit(solution)/shard_map/ppermute | solution.py:300
  183.6 13.1 %collective-permute-start.16 = (bf16[64,2048]{1,0:T(8,128)(2,1)S(1)}, bf16[64,2048]{1,0:T(8,128)(2,1)S(1)}, u32[]{:S(2)}, u32[]{:S(2)}) collective-permute-start(bf16[64,2048]{1,0:T(8,128)(2,1)S(1)} %get-tuple-element.67.refs_9_), channel_id=1, source_target_pairs={{0,4},{1,5},{2,6},{3,7},{4,0},{5,1},{6,2},{7,3},{8,12},{9,13},{10,... | collective-permute-start | bytes 786440 | tf_op jit(solution)/shard_map/ppermute | solution.py:300
  214.2 15.0 %all-to-all-start.4 = ((bf16[16,64,256]{2,1,0:T(8,128)(2,1)}), bf16[16,64,256]{2,1,0:T(8,128)(2,1)S(1)}, u32[]{:S(2)}, u32[]{:S(2)}) async-start(bf16[16,64,256]{2,1,0:T(8,128)(2,1)} %fan.3), calls=%async_computation.4 | async-start | bytes 1048576 | tf_op jit(solution)/shard_map/all_to_all | solution.py:456
  219.0 5.7 %collective-permute-start.18 = (f32[64,256]{1,0:T(8,128)S(1)}, f32[64,256]{1,0:T(8,128)S(1)}, u32[]{:S(2)}, u32[]{:S(2)}) collective-permute-start(f32[64,256]{1,0:T(8,128)S(1)} %get-tuple-element.84), channel_id=1, source_target_pairs={{0,0},{1,1},{2,8},{3,9},{4,4},{5,5},{6,12},{7,13},{8,2},{9,3},{10,... | collective-permute-start | bytes 196616 | tf_op jit(solution)/shard_map/ppermute | solution.py:300
  219.6 8.9 %collective-permute-start.21 = (f32[64,256]{1,0:T(8,128)S(1)}, f32[64,256]{1,0:T(8,128)S(1)}, u32[]{:S(2)}, u32[]{:S(2)}) collective-permute-start(f32[64,256]{1,0:T(8,128)S(1)} %get-tuple-element.85), channel_id=1, source_target_pairs={{0,3},{1,2},{2,11},{3,10},{4,7},{5,6},{6,15},{7,14},{8,1},{9,0},{1... | collective-permute-start | bytes 196616 | tf_op jit(solution)/shard_map/ppermute | solution.py:300
  224.0 4.6 %collective-permute-start.20 = (f32[64,256]{1,0:T(8,128)S(1)}, f32[64,256]{1,0:T(8,128)S(1)}, u32[]{:S(2)}, u32[]{:S(2)}) collective-permute-start(f32[64,256]{1,0:T(8,128)S(1)} %get-tuple-element.86), channel_id=1, source_target_pairs={{0,2},{1,3},{2,10},{3,11},{4,6},{5,7},{6,14},{7,15},{8,0},{9,1},{1... | collective-permute-start | bytes 196616 | tf_op jit(solution)/shard_map/ppermute | solution.py:300
  224.0 5.1 %collective-permute-start.19 = (f32[64,256]{1,0:T(8,128)S(1)}, f32[64,256]{1,0:T(8,128)S(1)}, u32[]{:S(2)}, u32[]{:S(2)}) collective-permute-start(f32[64,256]{1,0:T(8,128)S(1)} %get-tuple-element.87), channel_id=1, source_target_pairs={{0,1},{1,0},{2,9},{3,8},{4,5},{5,4},{6,13},{7,12},{8,3},{9,2},{10,... | collective-permute-start | bytes 196616 | tf_op jit(solution)/shard_map/ppermute | solution.py:300
  229.5 7.3 %collective-permute-start.17 = (f32[128,128]{1,0:T(8,128)S(1)}, f32[128,128]{1,0:T(8,128)S(1)}, u32[]{:S(2)}, u32[]{:S(2)}) collective-permute-start(f32[128,128]{1,0:T(8,128)S(1)} %gram.5.part_ref), channel_id=1, source_target_pairs={{0,4},{1,5},{2,6},{3,7},{4,0},{5,1},{6,2},{7,3},{8,12},{9,13},{10,... | collective-permute-start | bytes 196616 | tf_op jit(solution)/shard_map/ppermute | solution.py:300
  (5 other events, 28.0 us)

commit v5 on v4

--- a/solution.py
+++ b/solution.py
@@ -13,6 +13,7 @@
 ridge_weight = 0.1
 step_size = 0.5
 AXES = ("view", "samp")
+SETS = 2
 GROUP = 4
 
 SMALL = pltpu.CompilerParams(vmem_limit_bytes=4 << 20)
@@ -55,17 +56,18 @@
     shrunk = gram + whole_sum(gram * eye_mat) / size_k * eye_mat
     scale = jnp.sqrt(whole_sum(shrunk * shrunk))
     approx = shrunk / scale
-    inverse = eye_mat
-    for turn in range(NS_ITERS):
-        both = approx if turn == 0 else fine_dot(inverse, approx)
-        factor = 0.5 * (3.0 * eye_mat - both)
-        if turn == 0:
-            approx, inverse = fine_dot(approx, factor), factor
-        elif turn < NS_ITERS - 1:
-            stacked = fine_dot(jnp.concatenate([approx, inverse], axis=0), factor)
-            approx, inverse = stacked[:size_k], stacked[size_k:]
-        else:
-            inverse = fine_dot(inverse, factor)
+    inverse = 0.5 * (3.0 * eye_mat - approx)
+    approx = fine_dot(approx, inverse)
+
+    def turn(_, state):
+        approx, inverse = state
+        factor = 0.5 * (3.0 * eye_mat - fine_dot(inverse, approx))
+        stacked = fine_dot(jnp.concatenate([approx, inverse], axis=0), factor)
+        return stacked[:size_k], stacked[size_k:]
+
+    approx, inverse = lax.fori_loop(1, NS_ITERS - 1, turn, (approx, inverse))
+    factor = 0.5 * (3.0 * eye_mat - fine_dot(inverse, approx))
+    inverse = fine_dot(inverse, factor)
     return inverse * jnp.sqrt(total / scale)
 
 
@@ -173,11 +175,14 @@
     mixing=None,
     gathered=None,
     n_sub=None,
+    rows=None,
+    half_k=None,
 ):
     piece_rows, feats = data[0].shape
     n_pieces = len(data)
     pooled = n_pieces * piece_rows
-    half_k = (coeffs if coeffs is not None else values).shape[0]
+    row_at, n_rows = rows
+    comps = 2 * half_k
     low = jnp.bfloat16
     vmem, smem = pl.BlockSpec(memory_space=pltpu.VMEM), pl.BlockSpec(memory_space=pltpu.SMEM)
     args, specs, shapes = [where, *data], [smem] + [vmem] * n_pieces, []
@@ -190,20 +195,21 @@
             specs.append(vmem)
 
     if values is None:
-        give("coeffs", coeffs)
+        give("coeffs", *coeffs)
         if grads is not None:
-            give("grads", *grads)
-            shapes.append(("new_coeffs", jax.ShapeDtypeStruct((half_k, feats), jnp.float32)))
+            give("grads", *[term for pair in grads for term in pair])
+            for i, one in enumerate(coeffs):
+                shapes.append((f"new_coeffs{i}", jax.ShapeDtypeStruct(one.shape, jnp.float32)))
     else:
         give("values", values)
     if n_sub is not None:
         sub = pooled // n_sub
-        shapes.append(("out_values", jax.ShapeDtypeStruct((half_k, pooled), jnp.float32)))
-        shapes.append(("parts", jax.ShapeDtypeStruct((n_sub, half_k, sub), low)))
+        shapes.append(("out_values", jax.ShapeDtypeStruct((n_rows, pooled), jnp.float32)))
+        shapes.append(("parts", jax.ShapeDtypeStruct((n_sub, n_rows, sub), low)))
     if mixing is not None:
         give("mixing", mixing)
         give("gathered", gathered)
-        shapes.append(("term", jax.ShapeDtypeStruct((half_k, feats), low)))
+        shapes.append(("term", jax.ShapeDtypeStruct((n_rows, feats), low)))
 
     def kernel(where_ref, *refs):
         pieces = refs[:n_pieces]
@@ -219,13 +225,15 @@
             return 2 * lax.bitwise_xor(base, i // 2) + own
 
         if mixing is not None:
-            mixing_rows = ins["mixing0"][pl.ds(pl.multiple_of(core * half_k, half_k), half_k), :]
+            mixing_rows = ins["mixing0"][
+                pl.ds(pl.multiple_of(core * half_k + row_at, n_rows), n_rows), :
+            ]
             sub_in = gathered.shape[2]
             ratio = piece_rows // sub_in
 
             def set_resid(i, value):
                 sums = [
-                    gathered_block(ins["gathered0"], block_at(i) * ratio + r, 2 * half_k)
+                    gathered_block(ins["gathered0"], block_at(i) * ratio + r, comps)
                     for r in range(ratio)
                 ]
                 sums = sums[0] if ratio == 1 else jnp.concatenate(sums, axis=1)
@@ -234,12 +242,16 @@
                 ).astype(low)
 
         if values is None:
-            weights = ins["coeffs0"][...]
-            if grads is not None:
-                grad = ins["grads0"][...].astype(jnp.float32) + ins["grads1"][...].astype(jnp.float32)
-                weights = weights - step_size * (grad / total + ridge_weight * weights)
-                outs["new_coeffs"][...] = weights
-            weights = weights.astype(low)
+            lows = []
+            for i in range(len(coeffs)):
+                weights = ins[f"coeffs{i}"][...]
+                if grads is not None:
+                    grad = ins[f"grads{2 * i}"][...].astype(jnp.float32)
+                    grad = grad + ins[f"grads{2 * i + 1}"][...].astype(jnp.float32)
+                    weights = weights - step_size * (grad / total + ridge_weight * weights)
+                    outs[f"new_coeffs{i}"][...] = weights
+                lows.append(weights.astype(low))
+            weights = lows[0] if len(lows) == 1 else jnp.concatenate(lows, axis=0)
             for i in range(n_pieces):
                 value = tall_dot(weights, pieces[i][...])
                 if n_sub is not None:
@@ -253,7 +265,12 @@
                     set_resid(i, value)
         else:
             for i in range(n_pieces):
-                set_resid(i, ins["values0"][:, pl.ds(i * piece_rows, piece_rows)])
+                set_resid(
+                    i,
+                    ins["values0"][
+                        row_at : row_at + n_rows, pl.ds(i * piece_rows, piece_rows)
+                    ],
+                )
         if mixing is not None:
             wide = feats // 4
             for n in range(4):
@@ -273,7 +290,7 @@
         out_specs=[vmem] * len(shapes),
         out_shape=[shape for _, shape in shapes],
         scratch_shapes=[
-            pltpu.VMEM((half_k, pooled), low),
+            pltpu.VMEM((n_rows, pooled), low),
         ],
         name="step",
         compiler_params=LARGE,
@@ -341,7 +358,7 @@
     grid = Grid(lax.axis_size("view"), lax.axis_size("samp"))
     rows, feats = view_data.shape[1:]
     comps = init_coeffs.shape[2]
-    half_rows = rows // 2
+    half_k, half_rows = comps // 2, rows // 2
     total = rows * lax.axis_size("samp")
     n_sub = GROUP * grid.planes
     out_rows = feats // lax.axis_size("samp")
@@ -437,21 +454,43 @@
         ]
         for q in range(grid.squares)
     ]
-    values = grads = None
+    n_rows = half_k // SETS
+    values = None
+    coeffs = [coeffs[n * n_rows : (n + 1) * n_rows] for n in range(SETS)]
+    grads = [None] * SETS
     for outer_step in range(OUTER):
+        given = {"mixing": mixing, "gathered": gathered, "half_k": half_k}
         for inner_step in range(INNER):
-            given = {"mixing": mixing, "gathered": gathered}
-            if inner_step == 0 and outer_step > 0:
-                (term,) = step_call(total, where, data, values=values, **given)
-            elif grads is None:
-                (term,) = step_call(total, where, data, coeffs=coeffs, **given)
-            else:
-                coeffs, term = step_call(total, where, data, coeffs=coeffs, grads=grads, **given)
-            grads = grid.sum_squares(term, low)
-        coeffs, values, parts = step_call(
-            total, where, data, coeffs=coeffs, grads=grads, n_sub=n_sub
+            for n in range(SETS):
+                rows_of = (n * n_rows, n_rows)
+                if inner_step == 0 and outer_step > 0:
+                    (term,) = step_call(total, where, data, values=values, rows=rows_of, **given)
+                elif grads[n] is None:
+                    (term,) = step_call(
+                        total, where, data, coeffs=[coeffs[n]], rows=rows_of, **given
+                    )
+                else:
+                    coeffs[n], term = step_call(
+                        total,
+                        where,
+                        data,
+                        coeffs=[coeffs[n]],
+                        grads=[grads[n]],
+                        rows=rows_of,
+                        **given,
+                    )
+                grads[n] = grid.sum_squares(term, low)
+        *coeffs, values, parts = step_call(
+            total,
+            where,
+            data,
+            coeffs=coeffs,
+            grads=grads,
+            n_sub=n_sub,
+            rows=(0, half_k),
+            half_k=half_k,
         )
-        grads = None
+        grads = [None] * SETS
         parts = lax.all_to_all(parts, AXES, 0, 0, axis_index_groups=reduce_groups)
         gathered = lax.all_to_all(sum_and_fan(parts), AXES, 0, 0, axis_index_groups=gather_groups)
         if outer_step < OUTER - 1:
@@ -461,7 +500,7 @@
 
     pieces = []
     for k in range(GROUP):
-        piece = cut(coeffs, out_at[k], out_rows, 1)
+        piece = jnp.concatenate([cut(one, out_at[k], out_rows, 1) for one in coeffs], axis=0)
         pieces.append(
             grid.permute(
                 piece,

time: 243 us -> 234 us (0.963)
  waiting for transfers between devices: 96 us -> 61.7 us
  Pallas kernels: 54.7 us -> 77.8 us
  blocking collectives: 32.4 us -> 22.7 us
  starting transfers between devices: 47.1 us -> 52.7 us
    ppermute x22 -> x26, waiting for transfers between devices: 89.2 us -> 56.2 us  [permute(): return lax.ppermute(value, AXES, pairs)]
    pallas_call x6 -> x10, Pallas kernels: 35.1 us -> 57.5 us  [step_call(): pl.pallas_call(kernel, in_specs=specs, out_specs=[vmem] * len(shapes), ou...]
    all_to_all x2 -> x1, blocking collectives: 20 us -> 10.3 us  [body(): parts = lax.all_to_all(parts, AXES, 0, 0, axis_index_groups=reduce_groups)]
    all_to_all x1, waiting for transfers between devices: 6.78 us -> 0.01 us  [body(): lax.all_to_all(jnp.broadcast_to(mine.astype(low), (2 * GROUP, comps, half...]
    all_to_all x0 -> x1, waiting for transfers between devices: none -> 5.51 us  [body(): parts = lax.all_to_all(parts, AXES, 0, 0, axis_index_groups=reduce_groups)]
    all_to_all x0 -> x1, starting transfers between devices: none -> 3.41 us  [body(): parts = lax.all_to_all(parts, AXES, 0, 0, axis_index_groups=reduce_groups)]
    ppermute x22 -> x26, starting transfers between devices: 39.2 us -> 41.5 us  [permute(): return lax.ppermute(value, AXES, pairs)]
  transfers between devices with their start and end apart: 24 -> 29, of which waited for: 14 -> 11; matrix products, arithmetic and copies ran while one was open for 3% -> 4% of each run, Pallas kernels for 3% -> 19%
where the time goes in v5:
time: 234 us; the launch traced here: 232 us
  Pallas kernels  77.8 us (33%)
  waiting for transfers between devices  61.7 us (26%)
  starting transfers between devices  52.7 us (23%)
  blocking collectives  22.7 us (10%)
  local copies, waits for them, and re-layouts  9.15 us (4%)
  other arithmetic  4.1 us (2%)
  matrix products  3.26 us (1%)
    pallas_call x10, Pallas kernels, step_call(): pl.pallas_call(kernel, in_specs=specs, out_specs=[vmem] * len(shapes), ou...  57.5 us
    ppermute x26, waiting for transfers between devices, permute(): return lax.ppermute(value, AXES, pairs)  56.2 us
    ppermute x26, starting transfers between devices, permute(): return lax.ppermute(value, AXES, pairs)  41.5 us
    all_to_all x1, blocking collectives, body(): lax.all_to_all(sum_and_fan(parts), AXES, 0, 0, axis_index_groups=gather_g...  12.4 us
    all_to_all x1, blocking collectives, body(): parts = lax.all_to_all(parts, AXES, 0, 0, axis_index_groups=reduce_groups)  10.3 us
    pallas_call x2, Pallas kernels, newton_mixing(): pl.pallas_call(kernel, out_shape=jax.ShapeDtypeStruct(pair[0].shape, jnp....  9.54 us
    pallas_call x1, Pallas kernels, newton_scores(): pl.pallas_call(kernel, in_specs=[pl.BlockSpec(memory_space=pltpu.SMEM), v...  6.22 us
    all_to_all x1, waiting for transfers between devices, body(): parts = lax.all_to_all(parts, AXES, 0, 0, axis_index_groups=reduce_groups)  5.51 us
  transfers between devices with their start and end apart: 29, of which 11 were waited for; matrix products, arithmetic and copies ran while one was open for 4% of the time, Pallas kernels for 19%

profile of v5, /device:TPU:0, one launch (start us, length us, event | category | flops | bytes accessed | tf_op | source)
XLA Modules:
  0.0 232.4 jit_solution(11772734477865900169)
XLA Ops:
  24.0 4.1 %all-to-all-start = ((bf16[8,128,256]{2,1,0:T(8,128)(2,1)}), bf16[8,128,256]{2,1,0:T(8,128)(2,1)}, u32[]{:S(2)}, u32[]{:S(2)}) async-start(bf16[8,128,256]{2,1,0:T(8,128)(2,1)} %broadcast_in_dim.3), calls=%async_computation | async-start | bytes 1048576 | tf_op jit(solution)/shard_map/all_to_all | solution.py:421
  31.5 9.8 %collective-permute-start.7 = (bf16[256,2048]{1,0:T(8,128)(2,1)S(1)}, bf16[256,2048]{1,0:T(8,128)(2,1)}, u32[]{:S(2)}, u32[]{:S(2)}) collective-permute-start(bf16[256,2048]{1,0:T(8,128)(2,1)S(1)} %collective-permute-done.3.refs_2_), channel_id=1, source_target_pairs={{0,8},{1,9},{2,10},{3,11},{4,12},{5,13},{6,14},{7,15},{8,0},{9,1},... | collective-permute-start | bytes 3145736 | tf_op jit(solution)/shard_map/ppermute | solution.py:317
  41.3 22.1 %collective-permute-done.4.refs_6_ = bf16[256,2048]{1,0:T(8,128)(2,1)S(1)} collective-permute-done((bf16[256,2048]{1,0:T(8,128)(2,1)}, bf16[256,2048]{1,0:T(8,128)(2,1)S(1)}, u32[]{:S(2)}, u32[]{:S(2)}) %collective-permute-start.4) | collective-permute-done | bytes 1048608 | tf_op jit(solution)/shard_map/ppermute | solution.py:317
  73.6 4.9 %newton.2.refs_9_.refs_11_ = f32[128,128]{1,0:T(8,128)S(1)} custom-call(f32[128,128]{1,0:T(8,128)S(1)} %gram.3.part_ref, f32[128,128]{1,0:T(8,128)S(1)} %collective-permute-done.11.other_ref), custom_call_target="tpu_custom_call" | custom-call | tf_op jit(solution)/shard_map/newton/pallas_call | solution.py:85
  78.5 6.3 %step.10.refs_9_ = bf16[32,2048]{1,0:T(8,128)(2,1)S(1)} custom-call(s32[4]{0:T(128)S(1)} %add_convert_fusion.1.where_ref, bf16[256,2048]{1,0:T(8,128)(2,1)S(1)} %collective-permute-done.refs_0_, bf16[256,2048]{1,0:T(8,128)(2,1)} %collective-permute-done.2.refs_1_, bf16[256,2048]{1,0:T(8,128)(2,1)S(1)} %collective-permute-done.3.refs_2_, ...), custom_call_target="tpu_custom_call" | custom-call | tf_op jit(solution)/shard_map/step/pallas_call | solution.py:287
  86.5 6.3 %step.12.refs_9_ = bf16[32,2048]{1,0:T(8,128)(2,1)S(1)} custom-call(s32[4]{0:T(128)S(1)} %add_convert_fusion.1.where_ref, bf16[256,2048]{1,0:T(8,128)(2,1)S(1)} %collective-permute-done.refs_0_, bf16[256,2048]{1,0:T(8,128)(2,1)} %collective-permute-done.2.refs_1_, bf16[256,2048]{1,0:T(8,128)(2,1)S(1)} %collective-permute-done.3.refs_2_, ...), custom_call_target="tpu_custom_call" | custom-call | tf_op jit(solution)/shard_map/step/pallas_call | solution.py:287
  94.2 6.3 %step.11 = (f32[32,2048]{1,0:T(8,128)S(1)}, bf16[32,2048]{1,0:T(8,128)(2,1)S(1)}) custom-call(s32[4]{0:T(128)S(1)} %add_convert_fusion.1.where_ref, bf16[256,2048]{1,0:T(8,128)(2,1)S(1)} %collective-permute-done.refs_0_, bf16[256,2048]{1,0:T(8,128)(2,1)} %collective-permute-done.2.refs_1_, bf16[256,2048]{1,0:T(8,128)(2,1)S(1)} %collective-permute-done.3.refs_2_, ...), custom_call_target="tpu_custom_call" | custom-call | tf_op jit(solution)/shard_map/step/pallas_call | solution.py:287
  102.2 6.3 %step.13 = (f32[32,2048]{1,0:T(8,128)S(1)}, bf16[32,2048]{1,0:T(8,128)(2,1)S(1)}) custom-call(s32[4]{0:T(128)S(1)} %add_convert_fusion.1.where_ref, bf16[256,2048]{1,0:T(8,128)(2,1)S(1)} %collective-permute-done.refs_0_, bf16[256,2048]{1,0:T(8,128)(2,1)} %collective-permute-done.2.refs_1_, bf16[256,2048]{1,0:T(8,128)(2,1)S(1)} %collective-permute-done.3.refs_2_, ...), custom_call_target="tpu_custom_call" | custom-call | tf_op jit(solution)/shard_map/step/pallas_call | solution.py:287
  109.9 6.8 %collective-permute-done.15.refs_13_ = bf16[32,2048]{1,0:T(8,128)(2,1)S(1)} collective-permute-done((bf16[32,2048]{1,0:T(8,128)(2,1)S(1)}, bf16[32,2048]{1,0:T(8,128)(2,1)S(1)}, u32[]{:S(2)}, u32[]{:S(2)}) %collective-permute-start.15) | collective-permute-done | bytes 131104 | tf_op jit(solution)/shard_map/ppermute | solution.py:317
  116.7 5.4 %step.14 = (f32[32,2048]{1,0:T(8,128)S(1)}, f32[32,2048]{1,0:T(8,128)S(1)}, f32[64,2048]{1,0:T(8,128)S(1)}, bf16[8,64,256]{2,1,0:T(8,128)(2,1)S(1)}) custom-call(s32[4]{0:T(128)S(1)} %add_convert_fusion.1.where_ref, bf16[256,2048]{1,0:T(8,128)(2,1)S(1)} %collective-permute-done.refs_0_, bf16[256,2048]{1,0:T(8,128)(2,1)} %collective-permute-done.2.refs_1_, ...), custom_call_target="tpu_custom_call" | custom-call | tf_op jit(solution)/shard_map/step/pallas_call | solution.py:287
  122.1 10.3 %all_to_all.25.parts_ref = bf16[8,64,256]{2,1,0:T(8,128)(2,1)S(1)} all-to-all(bf16[8,64,256]{2,1,0:T(8,128)(2,1)S(1)} %get-tuple-element.73), channel_id=1, replica_groups={{0,16,1,17,2,18,3,19},{4,20,5,21,6,22,7,23},{8,24,9,25,10,26,11,27},{12..., dimensions={0} | all-to-all | bytes 524288 | tf_op jit(solution)/shard_map/all_to_all | solution.py:494
  132.4 12.4 %all_to_all.26.gathered_ref.refs_10_.refs_12_ = bf16[16,64,256]{2,1,0:T(8,128)(2,1)S(1)} all-to-all(bf16[16,64,256]{2,1,0:T(8,128)(2,1)S(1)} %fan.2), channel_id=1, replica_groups={{0,16,1,17,2,18,3,19,8,24,9,25,10,26,11,27},{4,20,5,21,6,22,7,23,12,28,..., dimensions={0} | all-to-all | bytes 1048576 | tf_op jit(solution)/shard_map/all_to_all | solution.py:495
  146.0 5.4 %collective-permute-done.16.other_ref = f32[128,128]{1,0:T(8,128)S(1)} collective-permute-done((f32[128,128]{1,0:T(8,128)S(1)}, f32[128,128]{1,0:T(8,128)S(1)}, u32[]{:S(2)}, u32[]{:S(2)}) %collective-permute-start.16) | collective-permute-done | bytes 65568 | tf_op jit(solution)/shard_map/ppermute | solution.py:317
  151.4 4.7 %newton.3.refs_9_.refs_11_ = f32[128,128]{1,0:T(8,128)S(1)} custom-call(f32[128,128]{1,0:T(8,128)S(1)} %gram.4.part_ref, f32[128,128]{1,0:T(8,128)S(1)} %collective-permute-done.16.other_ref), custom_call_target="tpu_custom_call" | custom-call | tf_op jit(solution)/shard_map/newton/pallas_call | solution.py:85
  156.1 4.2 %step.15.refs_9_ = bf16[32,2048]{1,0:T(8,128)(2,1)S(1)} custom-call(s32[4]{0:T(128)S(1)} %add_convert_fusion.1.where_ref, bf16[256,2048]{1,0:T(8,128)(2,1)S(1)} %collective-permute-done.refs_0_, bf16[256,2048]{1,0:T(8,128)(2,1)} %collective-permute-done.2.refs_1_, bf16[256,2048]{1,0:T(8,128)(2,1)S(1)} %collective-permute-done.3.refs_2_, ...), custom_call_target="tpu_custom_call" | custom-call | tf_op jit(solution)/shard_map/step/pallas_call | solution.py:287
  160.4 4.2 %step.17.refs_9_ = bf16[32,2048]{1,0:T(8,128)(2,1)S(1)} custom-call(s32[4]{0:T(128)S(1)} %add_convert_fusion.1.where_ref, bf16[256,2048]{1,0:T(8,128)(2,1)S(1)} %collective-permute-done.refs_0_, bf16[256,2048]{1,0:T(8,128)(2,1)} %collective-permute-done.2.refs_1_, bf16[256,2048]{1,0:T(8,128)(2,1)S(1)} %collective-permute-done.3.refs_2_, ...), custom_call_target="tpu_custom_call" | custom-call | tf_op jit(solution)/shard_map/step/pallas_call | solution.py:287
  169.9 6.2 %step.16 = (f32[32,2048]{1,0:T(8,128)S(1)}, bf16[32,2048]{1,0:T(8,128)(2,1)S(1)}) custom-call(s32[4]{0:T(128)S(1)} %add_convert_fusion.1.where_ref, bf16[256,2048]{1,0:T(8,128)(2,1)S(1)} %collective-permute-done.refs_0_, bf16[256,2048]{1,0:T(8,128)(2,1)} %collective-permute-done.2.refs_1_, bf16[256,2048]{1,0:T(8,128)(2,1)S(1)} %collective-permute-done.3.refs_2_, ...), custom_call_target="tpu_custom_call" | custom-call | tf_op jit(solution)/shard_map/step/pallas_call | solution.py:287
  176.2 6.2 %step.18 = (f32[32,2048]{1,0:T(8,128)S(1)}, bf16[32,2048]{1,0:T(8,128)(2,1)S(1)}) custom-call(s32[4]{0:T(128)S(1)} %add_convert_fusion.1.where_ref, bf16[256,2048]{1,0:T(8,128)(2,1)S(1)} %collective-permute-done.refs_0_, bf16[256,2048]{1,0:T(8,128)(2,1)} %collective-permute-done.2.refs_1_, bf16[256,2048]{1,0:T(8,128)(2,1)S(1)} %collective-permute-done.3.refs_2_, ...), custom_call_target="tpu_custom_call" | custom-call | tf_op jit(solution)/shard_map/step/pallas_call | solution.py:287
  185.4 4.0 %collective-permute-done.20.refs_13_ = bf16[32,2048]{1,0:T(8,128)(2,1)S(1)} collective-permute-done((bf16[32,2048]{1,0:T(8,128)(2,1)S(1)}, bf16[32,2048]{1,0:T(8,128)(2,1)S(1)}, u32[]{:S(2)}, u32[]{:S(2)}) %collective-permute-start.20) | collective-permute-done | bytes 131104 | tf_op jit(solution)/shard_map/ppermute | solution.py:317
  189.3 6.1 %step.19 = (f32[32,2048]{1,0:T(8,128)S(1)}, f32[32,2048]{1,0:T(8,128)S(1)}, f32[64,2048]{1,0:T(8,128)}, bf16[8,64,256]{2,1,0:T(8,128)(2,1)}) custom-call(s32[4]{0:T(128)S(1)} %add_convert_fusion.1.where_ref, bf16[256,2048]{1,0:T(8,128)(2,1)S(1)} %collective-permute-done.refs_0_, bf16[256,2048]{1,0:T(8,128)(2,1)} %collective-permute-done.2.refs_1_, ...), custom_call_target="tpu_custom_call" | custom-call | tf_op jit(solution)/shard_map/step/pallas_call | solution.py:287
  200.6 5.5 %all-to-all-done.3.parts_ref = bf16[8,64,256]{2,1,0:T(8,128)(2,1)S(1)} async-done(((bf16[8,64,256]{2,1,0:T(8,128)(2,1)}), bf16[8,64,256]{2,1,0:T(8,128)(2,1)S(1)}, u32[]{:S(2)}, u32[]{:S(2)}) %all-to-all-start.3) | async-done | bytes 262176 | tf_op jit(solution)/shard_map/all_to_all | solution.py:494
  206.9 3.6 %all-to-all-start.4 = ((bf16[16,64,256]{2,1,0:T(8,128)(2,1)}), bf16[16,64,256]{2,1,0:T(8,128)(2,1)S(1)}, u32[]{:S(2)}, u32[]{:S(2)}) async-start(bf16[16,64,256]{2,1,0:T(8,128)(2,1)} %fan.3), calls=%async_computation.4 | async-start | bytes 1048576 | tf_op jit(solution)/shard_map/all_to_all | solution.py:495
  214.4 6.1 %collective-permute-done.23 = f32[64,256]{1,0:T(8,128)S(1)} collective-permute-done((f32[64,256]{1,0:T(8,128)S(1)}, f32[64,256]{1,0:T(8,128)S(1)}, u32[]{:S(2)}, u32[]{:S(2)}) %collective-permute-start.23) | collective-permute-done | bytes 65568 | tf_op jit(solution)/shard_map/ppermute | solution.py:317
  226.2 6.2 %newton_scores.1 = f32[512,128]{1,0:T(8,128)} custom-call(s32[4]{0:T(128)S(1)} %add_convert_fusion.1.where_ref, f32[128,128]{1,0:T(8,128)S(1)} %gram.5.part_ref, f32[128,128]{1,0:T(8,128)S(1)} %collective-permute-done.21.other_ref, bf16[16,64,256]{2,1,0:T(8,128)(2,1)S(1)} %all-to-all-done.4.gathered_ref), custom_call_target="tpu_custom_call" | custom-call | tf_op jit(solution)/shard_map/newton_scores/pallas_call | solution.py:100
  (86 shorter events, 68.0 us)
Async XLA Ops:
  6.0 10.5 %collective-permute-start.8 = (f32[128,256]{1,0:T(8,128)S(1)}, f32[128,256]{1,0:T(8,128)S(1)}, u32[]{:S(2)}, u32[]{:S(2)}) collective-permute-start(f32[128,256]{1,0:T(8,128)S(1)} %constant_dynamic-slice_fusion.8), channel_id=1, source_target_pairs={{0,8},{1,9},{2,10},{3,11},{4,12},{5,13},{6,14},{7,15},{8,0},{9,1},... | collective-permute-start | bytes 393224 | tf_op jit(solution)/shard_map/ppermute | solution.py:317
  8.5 19.7 %collective-permute-start = (bf16[256,2048]{1,0:T(8,128)(2,1)}, bf16[256,2048]{1,0:T(8,128)(2,1)S(1)}, u32[]{:S(2)}, u32[]{:S(2)}) collective-permute-start(bf16[256,2048]{1,0:T(8,128)(2,1)} %get-tuple-element.52), channel_id=1, source_target_pairs={{0,0},{1,1},{2,8},{3,9},{4,4},{5,5},{6,12},{7,13},{8,2},{9,3},{10,... | collective-permute-start | bytes 3145736 | tf_op jit(solution)/shard_map/ppermute | solution.py:317
  10.3 21.2 %collective-permute-start.3 = (bf16[256,2048]{1,0:T(8,128)(2,1)}, bf16[256,2048]{1,0:T(8,128)(2,1)S(1)}, u32[]{:S(2)}, u32[]{:S(2)}) collective-permute-start(bf16[256,2048]{1,0:T(8,128)(2,1)} %get-tuple-element.56), channel_id=1, source_target_pairs={{0,1},{1,0},{2,9},{3,8},{4,5},{5,4},{6,13},{7,12},{8,3},{9,2},{10,... | collective-permute-start | bytes 3145736 | tf_op jit(solution)/shard_map/ppermute | solution.py:317
  14.7 48.7 %collective-permute-start.4 = (bf16[256,2048]{1,0:T(8,128)(2,1)}, bf16[256,2048]{1,0:T(8,128)(2,1)S(1)}, u32[]{:S(2)}, u32[]{:S(2)}) collective-permute-start(bf16[256,2048]{1,0:T(8,128)(2,1)} %get-tuple-element.92), channel_id=1, source_target_pairs={{0,9},{1,8},{2,1},{3,0},{4,13},{5,12},{6,5},{7,4},{8,11},{9,10},{1... | collective-permute-start | bytes 3145736 | tf_op jit(solution)/shard_map/ppermute | solution.py:317
  16.2 47.3 %collective-permute-start.1 = (bf16[256,2048]{1,0:T(8,128)(2,1)}, bf16[256,2048]{1,0:T(8,128)(2,1)}, u32[]{:S(2)}, u32[]{:S(2)}) collective-permute-start(bf16[256,2048]{1,0:T(8,128)(2,1)} %get-tuple-element.93), channel_id=1, source_target_pairs={{0,8},{1,9},{2,0},{3,1},{4,12},{5,13},{6,4},{7,5},{8,10},{9,11},{1... | collective-permute-start | bytes 3145736 | tf_op jit(solution)/shard_map/ppermute | solution.py:317
  22.6 41.4 %collective-permute-start.10 = (f32[64,2048]{1,0:T(8,128)}, f32[64,2048]{1,0:T(8,128)}, u32[]{:S(2)}, u32[]{:S(2)}) collective-permute-start(f32[64,2048]{1,0:T(8,128)} %get-tuple-element.64), channel_id=1, source_target_pairs={{0,8},{1,9},{2,10},{3,11},{4,12},{5,13},{6,14},{7,15},{8,0},{9,1},... | collective-permute-start | bytes 1572872 | tf_op jit(solution)/shard_map/ppermute | solution.py:317
  24.0 41.9 %all-to-all-start = ((bf16[8,128,256]{2,1,0:T(8,128)(2,1)}), bf16[8,128,256]{2,1,0:T(8,128)(2,1)}, u32[]{:S(2)}, u32[]{:S(2)}) async-start(bf16[8,128,256]{2,1,0:T(8,128)(2,1)} %broadcast_in_dim.3), calls=%async_computation | async-start | bytes 1048576 | tf_op jit(solution)/shard_map/all_to_all | solution.py:421
  28.2 50.3 %collective-permute-start.6 = (bf16[256,2048]{1,0:T(8,128)(2,1)S(1)}, bf16[256,2048]{1,0:T(8,128)(2,1)}, u32[]{:S(2)}, u32[]{:S(2)}) collective-permute-start(bf16[256,2048]{1,0:T(8,128)(2,1)S(1)} %collective-permute-done.refs_0_), channel_id=1, source_target_pairs={{0,8},{1,9},{2,10},{3,11},{4,12},{5,13},{6,14},{7,15},{8,0},{9,1},... | collective-permute-start | bytes 3145736 | tf_op jit(solution)/shard_map/ppermute | solution.py:317
  31.5 47.0 %collective-permute-start.7 = (bf16[256,2048]{1,0:T(8,128)(2,1)S(1)}, bf16[256,2048]{1,0:T(8,128)(2,1)}, u32[]{:S(2)}, u32[]{:S(2)}) collective-permute-start(bf16[256,2048]{1,0:T(8,128)(2,1)S(1)} %collective-permute-done.3.refs_2_), channel_id=1, source_target_pairs={{0,8},{1,9},{2,10},{3,11},{4,12},{5,13},{6,14},{7,15},{8,0},{9,1},... | collective-permute-start | bytes 3145736 | tf_op jit(solution)/shard_map/ppermute | solution.py:317
  63.4 15.1 %collective-permute-start.5 = (bf16[256,2048]{1,0:T(8,128)(2,1)S(1)}, bf16[256,2048]{1,0:T(8,128)(2,1)}, u32[]{:S(2)}, u32[]{:S(2)}) collective-permute-start(bf16[256,2048]{1,0:T(8,128)(2,1)S(1)} %collective-permute-done.4.refs_6_), channel_id=1, source_target_pairs={{0,8},{1,9},{2,10},{3,11},{4,12},{5,13},{6,14},{7,15},{8,0},{9,1},... | collective-permute-start | bytes 3145736 | tf_op jit(solution)/shard_map/ppermute | solution.py:317
  63.4 15.1 %collective-permute-start.2 = (bf16[256,2048]{1,0:T(8,128)(2,1)}, bf16[256,2048]{1,0:T(8,128)(2,1)}, u32[]{:S(2)}, u32[]{:S(2)}) collective-permute-start(bf16[256,2048]{1,0:T(8,128)(2,1)} %collective-permute-done.1.refs_4_), channel_id=1, source_target_pairs={{0,8},{1,9},{2,10},{3,11},{4,12},{5,13},{6,14},{7,15},{8,0},{9,1},... | collective-permute-start | bytes 3145736 | tf_op jit(solution)/shard_map/ppermute | solution.py:317
  84.8 9.4 %collective-permute-start.12 = (bf16[32,2048]{1,0:T(8,128)(2,1)S(1)}, bf16[32,2048]{1,0:T(8,128)(2,1)S(1)}, u32[]{:S(2)}, u32[]{:S(2)}) collective-permute-start(bf16[32,2048]{1,0:T(8,128)(2,1)S(1)} %step.10.refs_9_), channel_id=1, source_target_pairs={{0,4},{1,5},{2,6},{3,7},{4,0},{5,1},{6,2},{7,3},{8,12},{9,13},{10,... | collective-permute-start | bytes 393224 | tf_op jit(solution)/shard_map/ppermute | solution.py:317
  92.8 9.4 %collective-permute-start.13 = (bf16[32,2048]{1,0:T(8,128)(2,1)S(1)}, bf16[32,2048]{1,0:T(8,128)(2,1)S(1)}, u32[]{:S(2)}, u32[]{:S(2)}) collective-permute-start(bf16[32,2048]{1,0:T(8,128)(2,1)S(1)} %step.12.refs_9_), channel_id=1, source_target_pairs={{0,4},{1,5},{2,6},{3,7},{4,0},{5,1},{6,2},{7,3},{8,12},{9,13},{10,... | collective-permute-start | bytes 393224 | tf_op jit(solution)/shard_map/ppermute | solution.py:317
  100.5 9.4 %collective-permute-start.14 = (bf16[32,2048]{1,0:T(8,128)(2,1)S(1)}, bf16[32,2048]{1,0:T(8,128)(2,1)S(1)}, u32[]{:S(2)}, u32[]{:S(2)}) collective-permute-start(bf16[32,2048]{1,0:T(8,128)(2,1)S(1)} %get-tuple-element.69.refs_10_), channel_id=1, source_target_pairs={{0,4},{1,5},{2,6},{3,7},{4,0},{5,1},{6,2},{7,3},{8,12},{9,13},{10,... | collective-permute-start | bytes 393224 | tf_op jit(solution)/shard_map/ppermute | solution.py:317
  108.5 8.2 %collective-permute-start.15 = (bf16[32,2048]{1,0:T(8,128)(2,1)S(1)}, bf16[32,2048]{1,0:T(8,128)(2,1)S(1)}, u32[]{:S(2)}, u32[]{:S(2)}) collective-permute-start(bf16[32,2048]{1,0:T(8,128)(2,1)S(1)} %get-tuple-element.70.refs_12_), channel_id=1, source_target_pairs={{0,4},{1,5},{2,6},{3,7},{4,0},{5,1},{6,2},{7,3},{8,12},{9,13},{10,... | collective-permute-start | bytes 393224 | tf_op jit(solution)/shard_map/ppermute | solution.py:317
  160.4 9.6 %collective-permute-start.17 = (bf16[32,2048]{1,0:T(8,128)(2,1)S(1)}, bf16[32,2048]{1,0:T(8,128)(2,1)S(1)}, u32[]{:S(2)}, u32[]{:S(2)}) collective-permute-start(bf16[32,2048]{1,0:T(8,128)(2,1)S(1)} %step.15.refs_9_), channel_id=1, source_target_pairs={{0,4},{1,5},{2,6},{3,7},{4,0},{5,1},{6,2},{7,3},{8,12},{9,13},{10,... | collective-permute-start | bytes 393224 | tf_op jit(solution)/shard_map/ppermute | solution.py:317
  164.7 11.5 %collective-permute-start.18 = (bf16[32,2048]{1,0:T(8,128)(2,1)S(1)}, bf16[32,2048]{1,0:T(8,128)(2,1)S(1)}, u32[]{:S(2)}, u32[]{:S(2)}) collective-permute-start(bf16[32,2048]{1,0:T(8,128)(2,1)S(1)} %step.17.refs_9_), channel_id=1, source_target_pairs={{0,4},{1,5},{2,6},{3,7},{4,0},{5,1},{6,2},{7,3},{8,12},{9,13},{10,... | collective-permute-start | bytes 393224 | tf_op jit(solution)/shard_map/ppermute | solution.py:317
  176.1 9.2 %collective-permute-start.19 = (bf16[32,2048]{1,0:T(8,128)(2,1)S(1)}, bf16[32,2048]{1,0:T(8,128)(2,1)S(1)}, u32[]{:S(2)}, u32[]{:S(2)}) collective-permute-start(bf16[32,2048]{1,0:T(8,128)(2,1)S(1)} %get-tuple-element.77.refs_10_), channel_id=1, source_target_pairs={{0,4},{1,5},{2,6},{3,7},{4,0},{5,1},{6,2},{7,3},{8,12},{9,13},{10,... | collective-permute-start | bytes 393224 | tf_op jit(solution)/shard_map/ppermute | solution.py:317
  182.4 6.9 %collective-permute-start.20 = (bf16[32,2048]{1,0:T(8,128)(2,1)S(1)}, bf16[32,2048]{1,0:T(8,128)(2,1)S(1)}, u32[]{:S(2)}, u32[]{:S(2)}) collective-permute-start(bf16[32,2048]{1,0:T(8,128)(2,1)S(1)} %get-tuple-element.78.refs_12_), channel_id=1, source_target_pairs={{0,4},{1,5},{2,6},{3,7},{4,0},{5,1},{6,2},{7,3},{8,12},{9,13},{10,... | collective-permute-start | bytes 393224 | tf_op jit(solution)/shard_map/ppermute | solution.py:317
  196.1 10.0 %all-to-all-start.3 = ((bf16[8,64,256]{2,1,0:T(8,128)(2,1)}), bf16[8,64,256]{2,1,0:T(8,128)(2,1)S(1)}, u32[]{:S(2)}, u32[]{:S(2)}) async-start(bf16[8,64,256]{2,1,0:T(8,128)(2,1)} %get-tuple-element.79), calls=%async_computation.3 | async-start | bytes 524288 | tf_op jit(solution)/shard_map/all_to_all | solution.py:494
  206.9 13.7 %all-to-all-start.4 = ((bf16[16,64,256]{2,1,0:T(8,128)(2,1)}), bf16[16,64,256]{2,1,0:T(8,128)(2,1)S(1)}, u32[]{:S(2)}, u32[]{:S(2)}) async-start(bf16[16,64,256]{2,1,0:T(8,128)(2,1)} %fan.3), calls=%async_computation.4 | async-start | bytes 1048576 | tf_op jit(solution)/shard_map/all_to_all | solution.py:495
  210.5 10.0 %collective-permute-start.23 = (f32[64,256]{1,0:T(8,128)S(1)}, f32[64,256]{1,0:T(8,128)S(1)}, u32[]{:S(2)}, u32[]{:S(2)}) collective-permute-start(f32[64,256]{1,0:T(8,128)S(1)} %pad_maximum_fusion.3), channel_id=1, source_target_pairs={{0,1},{1,0},{2,9},{3,8},{4,5},{5,4},{6,13},{7,12},{8,3},{9,2},{10,... | collective-permute-start | bytes 196616 | tf_op jit(solution)/shard_map/ppermute | solution.py:317
  212.4 8.1 %collective-permute-start.24 = (f32[64,256]{1,0:T(8,128)S(1)}, f32[64,256]{1,0:T(8,128)S(1)}, u32[]{:S(2)}, u32[]{:S(2)}) collective-permute-start(f32[64,256]{1,0:T(8,128)S(1)} %pad_maximum_fusion.4), channel_id=1, source_target_pairs={{0,2},{1,3},{2,10},{3,11},{4,6},{5,7},{6,14},{7,15},{8,0},{9,1},{1... | collective-permute-start | bytes 196616 | tf_op jit(solution)/shard_map/ppermute | solution.py:317
  213.7 6.9 %collective-permute-start.25 = (f32[64,256]{1,0:T(8,128)S(1)}, f32[64,256]{1,0:T(8,128)S(1)}, u32[]{:S(2)}, u32[]{:S(2)}) collective-permute-start(f32[64,256]{1,0:T(8,128)S(1)} %pad_maximum_fusion.5), channel_id=1, source_target_pairs={{0,3},{1,2},{2,11},{3,10},{4,7},{5,6},{6,15},{7,14},{8,1},{9,0},{1... | collective-permute-start | bytes 196616 | tf_op jit(solution)/shard_map/ppermute | solution.py:317
  (9 other events, 48.8 us)

commit v6 on v5

--- a/solution.py
+++ b/solution.py
@@ -65,7 +65,7 @@
         stacked = fine_dot(jnp.concatenate([approx, inverse], axis=0), factor)
         return stacked[:size_k], stacked[size_k:]
 
-    approx, inverse = lax.fori_loop(1, NS_ITERS - 1, turn, (approx, inverse))
+    approx, inverse = lax.fori_loop(1, NS_ITERS - 1, turn, (approx, inverse), unroll=5)
     factor = 0.5 * (3.0 * eye_mat - fine_dot(inverse, approx))
     inverse = fine_dot(inverse, factor)
     return inverse * jnp.sqrt(total / scale)
@@ -384,8 +384,10 @@
         at = (*pool_at[k], zero)
         return lax.dynamic_slice(source, at, (1, half_rows, feats), allow_negative_indices=False)[0]
 
-    early = [slice_piece(view_data, 1), slice_piece(view_data, 0)]
-    view_later, *early = lax.optimization_barrier((view_data, *early))
+    early = [slice_piece(view_data, 1)]
+    view_later, early[0] = lax.optimization_barrier((view_data, early[0]))
+    early.append(slice_piece(view_later, 0))
+    view_later, early[1] = lax.optimization_barrier((view_later, early[1]))
     late = [slice_piece(view_later, 3), slice_piece(view_later, 2)]
     cut_pieces = {1: early[0], 0: early[1], 3: late[0], 2: late[1]}
 
@@ -425,7 +427,9 @@
     coeffs, for_core = first_coeffs(init_coeffs, where)
     from_core = grid.swap_core(for_core)
     coeffs = jnp.where(holder == 1, coeffs, from_core)
-    gathered, coeffs = lax.optimization_barrier((gathered, coeffs))
+    n_rows = half_k // SETS
+    coeffs = [coeffs[n * n_rows : (n + 1) * n_rows] for n in range(SETS)]
+    gathered, *coeffs = lax.optimization_barrier((gathered, *coeffs))
 
     shared_slots = {}
     for k in range(GROUP):
@@ -454,9 +458,7 @@
         ]
         for q in range(grid.squares)
     ]
-    n_rows = half_k // SETS
     values = None
-    coeffs = [coeffs[n * n_rows : (n + 1) * n_rows] for n in range(SETS)]
     grads = [None] * SETS
     for outer_step in range(OUTER):
         given = {"mixing": mixing, "gathered": gathered, "half_k": half_k}

time: 234 us -> 239 us (1.021)
  waiting for transfers between devices: 61.7 us -> 75.4 us
  starting transfers between devices: 52.7 us -> 44.1 us
  local copies, waits for them, and re-layouts: 9.15 us -> 13 us
  other arithmetic: 4.1 us -> 1.53 us
    ppermute x26, starting transfers between devices: 41.5 us -> 32.9 us  [permute(): return lax.ppermute(value, AXES, pairs)]
    all_to_all x1, waiting for transfers between devices: 0.01 us -> 6.99 us  [body(): lax.all_to_all(jnp.broadcast_to(mine.astype(low), (2 * GROUP, comps, half...]
    ppermute x26, waiting for transfers between devices: 56.2 us -> 62.9 us  [permute(): return lax.ppermute(value, AXES, pairs)]
    squeeze x2 -> x3, local copies, waits for them, and re-layouts: 3.74 us -> 6.97 us  [slice_piece(): lax.dynamic_slice(source, at, (1, half_rows, feats), allow_negative_indic...]
  transfers between devices with their start and end apart: 29 -> 29, of which waited for: 11 -> 13; matrix products, arithmetic and copies ran while one was open for 4% -> 4% of each run, Pallas kernels for 19% -> 18%
where the time goes in v6:
time: 239 us; the launch traced here: 238 us
  Pallas kernels  77.2 us (32%)
  waiting for transfers between devices  75.4 us (32%)
  starting transfers between devices  44.1 us (18%)
  blocking collectives  23.8 us (10%)
  local copies, waits for them, and re-layouts  13 us (5%)
    ppermute x26, waiting for transfers between devices, permute(): return lax.ppermute(value, AXES, pairs)  62.9 us
    pallas_call x10, Pallas kernels, step_call(): pl.pallas_call(kernel, in_specs=specs, out_specs=[vmem] * len(shapes), ou...  57.3 us
    ppermute x26, starting transfers between devices, permute(): return lax.ppermute(value, AXES, pairs)  32.9 us
    all_to_all x1, blocking collectives, body(): lax.all_to_all(sum_and_fan(parts), AXES, 0, 0, axis_index_groups=gather_g...  12.4 us
    all_to_all x1, blocking collectives, body(): parts = lax.all_to_all(parts, AXES, 0, 0, axis_index_groups=reduce_groups)  11.4 us
    pallas_call x2, Pallas kernels, newton_mixing(): pl.pallas_call(kernel, out_shape=jax.ShapeDtypeStruct(pair[0].shape, jnp....  9.29 us
    all_to_all x1, waiting for transfers between devices, body(): lax.all_to_all(jnp.broadcast_to(mine.astype(low), (2 * GROUP, comps, half...  6.99 us
    squeeze x3, local copies, waits for them, and re-layouts, slice_piece(): lax.dynamic_slice(source, at, (1, half_rows, feats), allow_negative_indic...  6.97 us
  transfers between devices with their start and end apart: 29, of which 13 were waited for; matrix products, arithmetic and copies ran while one was open for 4% of the time, Pallas kernels for 18%

profile of v6, /device:TPU:0, one launch (start us, length us, event | category | flops | bytes accessed | tf_op | source)
XLA Modules:
  0.0 237.7 jit_solution(15930435603304140633)
XLA Ops:
  25.2 20.6 %collective-permute-done.3.refs_2_ = bf16[256,2048]{1,0:T(8,128)(2,1)S(1)} collective-permute-done((bf16[256,2048]{1,0:T(8,128)(2,1)}, bf16[256,2048]{1,0:T(8,128)(2,1)S(1)}, u32[]{:S(2)}, u32[]{:S(2)}) %collective-permute-start.3) | collective-permute-done | bytes 1048608 | tf_op jit(solution)/shard_map/ppermute | solution.py:317
  45.9 11.2 %collective-permute-done.4.refs_6_ = bf16[256,2048]{1,0:T(8,128)(2,1)S(1)} collective-permute-done((bf16[256,2048]{1,0:T(8,128)(2,1)}, bf16[256,2048]{1,0:T(8,128)(2,1)S(1)}, u32[]{:S(2)}, u32[]{:S(2)}) %collective-permute-start.4) | collective-permute-done | bytes 1048608 | tf_op jit(solution)/shard_map/ppermute | solution.py:317
  58.5 4.1 %all-to-all-start = ((bf16[8,128,256]{2,1,0:T(8,128)(2,1)}), bf16[8,128,256]{2,1,0:T(8,128)(2,1)}, u32[]{:S(2)}, u32[]{:S(2)}) async-start(bf16[8,128,256]{2,1,0:T(8,128)(2,1)} %broadcast_in_dim.3), calls=%async_computation | async-start | bytes 1048576 | tf_op jit(solution)/shard_map/all_to_all | solution.py:423
  64.5 7.0 %all-to-all-done.gathered_ref.refs_10_.refs_12_ = bf16[8,128,256]{2,1,0:T(8,128)(2,1)} async-done(((bf16[8,128,256]{2,1,0:T(8,128)(2,1)}), bf16[8,128,256]{2,1,0:T(8,128)(2,1)}, u32[]{:S(2)}, u32[]{:S(2)}) %all-to-all-start) | async-done | bytes 524320 | tf_op jit(solution)/shard_map/all_to_all | solution.py:423
  78.1 4.7 %newton.2.refs_9_.refs_11_ = f32[128,128]{1,0:T(8,128)S(1)} custom-call(f32[128,128]{1,0:T(8,128)S(1)} %gram.3.part_ref, f32[128,128]{1,0:T(8,128)S(1)} %collective-permute-done.11.other_ref), custom_call_target="tpu_custom_call" | custom-call | tf_op jit(solution)/shard_map/newton/pallas_call | solution.py:85
  83.9 6.3 %step.10.refs_9_ = bf16[32,2048]{1,0:T(8,128)(2,1)S(1)} custom-call(s32[4]{0:T(128)S(1)} %add_convert_fusion.1.where_ref, bf16[256,2048]{1,0:T(8,128)(2,1)S(1)} %collective-permute-done.refs_0_, bf16[256,2048]{1,0:T(8,128)(2,1)} %collective-permute-done.2.refs_1_, bf16[256,2048]{1,0:T(8,128)(2,1)S(1)} %collective-permute-done.3.refs_2_, ...), custom_call_target="tpu_custom_call" | custom-call | tf_op jit(solution)/shard_map/step/pallas_call | solution.py:287
  93.0 6.3 %step.12.refs_9_ = bf16[32,2048]{1,0:T(8,128)(2,1)S(1)} custom-call(s32[4]{0:T(128)S(1)} %add_convert_fusion.1.where_ref, bf16[256,2048]{1,0:T(8,128)(2,1)S(1)} %collective-permute-done.refs_0_, bf16[256,2048]{1,0:T(8,128)(2,1)} %collective-permute-done.2.refs_1_, bf16[256,2048]{1,0:T(8,128)(2,1)S(1)} %collective-permute-done.3.refs_2_, ...), custom_call_target="tpu_custom_call" | custom-call | tf_op jit(solution)/shard_map/step/pallas_call | solution.py:287
  99.5 6.3 %step.11 = (f32[32,2048]{1,0:T(8,128)S(1)}, bf16[32,2048]{1,0:T(8,128)(2,1)S(1)}) custom-call(s32[4]{0:T(128)S(1)} %add_convert_fusion.1.where_ref, bf16[256,2048]{1,0:T(8,128)(2,1)S(1)} %collective-permute-done.refs_0_, bf16[256,2048]{1,0:T(8,128)(2,1)} %collective-permute-done.2.refs_1_, bf16[256,2048]{1,0:T(8,128)(2,1)S(1)} %collective-permute-done.3.refs_2_, ...), custom_call_target="tpu_custom_call" | custom-call | tf_op jit(solution)/shard_map/step/pallas_call | solution.py:287
  108.7 6.3 %step.13 = (f32[32,2048]{1,0:T(8,128)S(1)}, bf16[32,2048]{1,0:T(8,128)(2,1)S(1)}) custom-call(s32[4]{0:T(128)S(1)} %add_convert_fusion.1.where_ref, bf16[256,2048]{1,0:T(8,128)(2,1)S(1)} %collective-permute-done.refs_0_, bf16[256,2048]{1,0:T(8,128)(2,1)} %collective-permute-done.2.refs_1_, bf16[256,2048]{1,0:T(8,128)(2,1)S(1)} %collective-permute-done.3.refs_2_, ...), custom_call_target="tpu_custom_call" | custom-call | tf_op jit(solution)/shard_map/step/pallas_call | solution.py:287
  115.2 5.7 %collective-permute-done.15.refs_13_ = bf16[32,2048]{1,0:T(8,128)(2,1)S(1)} collective-permute-done((bf16[32,2048]{1,0:T(8,128)(2,1)S(1)}, bf16[32,2048]{1,0:T(8,128)(2,1)S(1)}, u32[]{:S(2)}, u32[]{:S(2)}) %collective-permute-start.15) | collective-permute-done | bytes 131104 | tf_op jit(solution)/shard_map/ppermute | solution.py:317
  120.9 5.2 %step.14 = (f32[32,2048]{1,0:T(8,128)S(1)}, f32[32,2048]{1,0:T(8,128)S(1)}, f32[64,2048]{1,0:T(8,128)S(1)}, bf16[8,64,256]{2,1,0:T(8,128)(2,1)S(1)}) custom-call(s32[4]{0:T(128)S(1)} %add_convert_fusion.1.where_ref, bf16[256,2048]{1,0:T(8,128)(2,1)S(1)} %collective-permute-done.refs_0_, bf16[256,2048]{1,0:T(8,128)(2,1)} %collective-permute-done.2.refs_1_, ...), custom_call_target="tpu_custom_call" | custom-call | tf_op jit(solution)/shard_map/step/pallas_call | solution.py:287
  126.1 11.4 %all_to_all.25.parts_ref = bf16[8,64,256]{2,1,0:T(8,128)(2,1)S(1)} all-to-all(bf16[8,64,256]{2,1,0:T(8,128)(2,1)S(1)} %get-tuple-element.77), channel_id=1, replica_groups={{0,16,1,17,2,18,3,19},{4,20,5,21,6,22,7,23},{8,24,9,25,10,26,11,27},{12..., dimensions={0} | all-to-all | bytes 524288 | tf_op jit(solution)/shard_map/all_to_all | solution.py:496
  137.6 12.4 %all_to_all.26.gathered_ref.refs_10_.refs_12_ = bf16[16,64,256]{2,1,0:T(8,128)(2,1)S(1)} all-to-all(bf16[16,64,256]{2,1,0:T(8,128)(2,1)S(1)} %fan.2), channel_id=1, replica_groups={{0,16,1,17,2,18,3,19,8,24,9,25,10,26,11,27},{4,20,5,21,6,22,7,23,12,28,..., dimensions={0} | all-to-all | bytes 1048576 | tf_op jit(solution)/shard_map/all_to_all | solution.py:497
  150.7 5.9 %collective-permute-done.16.other_ref = f32[128,128]{1,0:T(8,128)S(1)} collective-permute-done((f32[128,128]{1,0:T(8,128)S(1)}, f32[128,128]{1,0:T(8,128)S(1)}, u32[]{:S(2)}, u32[]{:S(2)}) %collective-permute-start.16) | collective-permute-done | bytes 65568 | tf_op jit(solution)/shard_map/ppermute | solution.py:317
  156.6 4.6 %newton.3.refs_9_.refs_11_ = f32[128,128]{1,0:T(8,128)S(1)} custom-call(f32[128,128]{1,0:T(8,128)S(1)} %gram.4.part_ref, f32[128,128]{1,0:T(8,128)S(1)} %collective-permute-done.16.other_ref), custom_call_target="tpu_custom_call" | custom-call | tf_op jit(solution)/shard_map/newton/pallas_call | solution.py:85
  161.2 4.2 %step.15.refs_9_ = bf16[32,2048]{1,0:T(8,128)(2,1)S(1)} custom-call(s32[4]{0:T(128)S(1)} %add_convert_fusion.1.where_ref, bf16[256,2048]{1,0:T(8,128)(2,1)S(1)} %collective-permute-done.refs_0_, bf16[256,2048]{1,0:T(8,128)(2,1)} %collective-permute-done.2.refs_1_, bf16[256,2048]{1,0:T(8,128)(2,1)S(1)} %collective-permute-done.3.refs_2_, ...), custom_call_target="tpu_custom_call" | custom-call | tf_op jit(solution)/shard_map/step/pallas_call | solution.py:287
  165.5 4.2 %step.17.refs_9_ = bf16[32,2048]{1,0:T(8,128)(2,1)S(1)} custom-call(s32[4]{0:T(128)S(1)} %add_convert_fusion.1.where_ref, bf16[256,2048]{1,0:T(8,128)(2,1)S(1)} %collective-permute-done.refs_0_, bf16[256,2048]{1,0:T(8,128)(2,1)} %collective-permute-done.2.refs_1_, bf16[256,2048]{1,0:T(8,128)(2,1)S(1)} %collective-permute-done.3.refs_2_, ...), custom_call_target="tpu_custom_call" | custom-call | tf_op jit(solution)/shard_map/step/pallas_call | solution.py:287
  172.7 3.7 %collective-permute-done.17.refs_10_ = bf16[32,2048]{1,0:T(8,128)(2,1)S(1)} collective-permute-done((bf16[32,2048]{1,0:T(8,128)(2,1)S(1)}, bf16[32,2048]{1,0:T(8,128)(2,1)S(1)}, u32[]{:S(2)}, u32[]{:S(2)}) %collective-permute-start.17) | collective-permute-done | bytes 131104 | tf_op jit(solution)/shard_map/ppermute | solution.py:317
  176.4 6.2 %step.16 = (f32[32,2048]{1,0:T(8,128)S(1)}, bf16[32,2048]{1,0:T(8,128)(2,1)S(1)}) custom-call(s32[4]{0:T(128)S(1)} %add_convert_fusion.1.where_ref, bf16[256,2048]{1,0:T(8,128)(2,1)S(1)} %collective-permute-done.refs_0_, bf16[256,2048]{1,0:T(8,128)(2,1)} %collective-permute-done.2.refs_1_, bf16[256,2048]{1,0:T(8,128)(2,1)S(1)} %collective-permute-done.3.refs_2_, ...), custom_call_target="tpu_custom_call" | custom-call | tf_op jit(solution)/shard_map/step/pallas_call | solution.py:287
  182.6 6.2 %step.18 = (f32[32,2048]{1,0:T(8,128)S(1)}, bf16[32,2048]{1,0:T(8,128)(2,1)S(1)}) custom-call(s32[4]{0:T(128)S(1)} %add_convert_fusion.1.where_ref, bf16[256,2048]{1,0:T(8,128)(2,1)S(1)} %collective-permute-done.refs_0_, bf16[256,2048]{1,0:T(8,128)(2,1)} %collective-permute-done.2.refs_1_, bf16[256,2048]{1,0:T(8,128)(2,1)S(1)} %collective-permute-done.3.refs_2_, ...), custom_call_target="tpu_custom_call" | custom-call | tf_op jit(solution)/shard_map/step/pallas_call | solution.py:287
  194.8 6.1 %step.19 = (f32[32,2048]{1,0:T(8,128)S(1)}, f32[32,2048]{1,0:T(8,128)S(1)}, f32[64,2048]{1,0:T(8,128)}, bf16[8,64,256]{2,1,0:T(8,128)(2,1)}) custom-call(s32[4]{0:T(128)S(1)} %add_convert_fusion.1.where_ref, bf16[256,2048]{1,0:T(8,128)(2,1)S(1)} %collective-permute-done.refs_0_, bf16[256,2048]{1,0:T(8,128)(2,1)} %collective-permute-done.2.refs_1_, ...), custom_call_target="tpu_custom_call" | custom-call | tf_op jit(solution)/shard_map/step/pallas_call | solution.py:287
  206.0 5.5 %all-to-all-done.3.parts_ref = bf16[8,64,256]{2,1,0:T(8,128)(2,1)S(1)} async-done(((bf16[8,64,256]{2,1,0:T(8,128)(2,1)}), bf16[8,64,256]{2,1,0:T(8,128)(2,1)S(1)}, u32[]{:S(2)}, u32[]{:S(2)}) %all-to-all-start.3) | async-done | bytes 262176 | tf_op jit(solution)/shard_map/all_to_all | solution.py:496
  219.9 6.1 %collective-permute-done.23 = f32[64,256]{1,0:T(8,128)S(1)} collective-permute-done((f32[64,256]{1,0:T(8,128)S(1)}, f32[64,256]{1,0:T(8,128)S(1)}, u32[]{:S(2)}, u32[]{:S(2)}) %collective-permute-start.23) | collective-permute-done | bytes 65568 | tf_op jit(solution)/shard_map/ppermute | solution.py:317
  231.6 6.1 %newton_scores.1 = f32[512,128]{1,0:T(8,128)} custom-call(s32[4]{0:T(128)S(1)} %add_convert_fusion.1.where_ref, f32[128,128]{1,0:T(8,128)S(1)} %gram.5.part_ref, f32[128,128]{1,0:T(8,128)S(1)} %collective-permute-done.21.other_ref, bf16[16,64,256]{2,1,0:T(8,128)(2,1)S(1)} %all-to-all-done.4.gathered_ref), custom_call_target="tpu_custom_call" | custom-call | tf_op jit(solution)/shard_map/newton_scores/pallas_call | solution.py:100
  (89 shorter events, 70.4 us)
Async XLA Ops:
  5.8 18.9 %collective-permute-start = (bf16[256,2048]{1,0:T(8,128)(2,1)}, bf16[256,2048]{1,0:T(8,128)(2,1)S(1)}, u32[]{:S(2)}, u32[]{:S(2)}) collective-permute-start(bf16[256,2048]{1,0:T(8,128)(2,1)} %dynamic-slice_bitcast_fusion.2), channel_id=1, source_target_pairs={{0,0},{1,1},{2,8},{3,9},{4,4},{5,5},{6,12},{7,13},{8,2},{9,3},{10,... | collective-permute-start | bytes 3145736 | tf_op jit(solution)/shard_map/ppermute | solution.py:317
  7.7 38.1 %collective-permute-start.3 = (bf16[256,2048]{1,0:T(8,128)(2,1)}, bf16[256,2048]{1,0:T(8,128)(2,1)S(1)}, u32[]{:S(2)}, u32[]{:S(2)}) collective-permute-start(bf16[256,2048]{1,0:T(8,128)(2,1)} %dynamic-slice_bitcast_fusion.3), channel_id=1, source_target_pairs={{0,1},{1,0},{2,9},{3,8},{4,5},{5,4},{6,13},{7,12},{8,3},{9,2},{10,... | collective-permute-start | bytes 3145736 | tf_op jit(solution)/shard_map/ppermute | solution.py:317
  12.6 44.5 %collective-permute-start.4 = (bf16[256,2048]{1,0:T(8,128)(2,1)}, bf16[256,2048]{1,0:T(8,128)(2,1)S(1)}, u32[]{:S(2)}, u32[]{:S(2)}) collective-permute-start(bf16[256,2048]{1,0:T(8,128)(2,1)} %get-tuple-element.96), channel_id=1, source_target_pairs={{0,9},{1,8},{2,1},{3,0},{4,13},{5,12},{6,5},{7,4},{8,11},{9,10},{1... | collective-permute-start | bytes 3145736 | tf_op jit(solution)/shard_map/ppermute | solution.py:317
  14.0 43.6 %collective-permute-start.1 = (bf16[256,2048]{1,0:T(8,128)(2,1)}, bf16[256,2048]{1,0:T(8,128)(2,1)}, u32[]{:S(2)}, u32[]{:S(2)}) collective-permute-start(bf16[256,2048]{1,0:T(8,128)(2,1)} %get-tuple-element.97), channel_id=1, source_target_pairs={{0,8},{1,9},{2,0},{3,1},{4,12},{5,13},{6,4},{7,5},{8,10},{9,11},{1... | collective-permute-start | bytes 3145736 | tf_op jit(solution)/shard_map/ppermute | solution.py:317
  24.7 38.0 %collective-permute-start.10 = (f32[64,2048]{1,0:T(8,128)}, f32[64,2048]{1,0:T(8,128)}, u32[]{:S(2)}, u32[]{:S(2)}) collective-permute-start(f32[64,2048]{1,0:T(8,128)} %get-tuple-element.67), channel_id=1, source_target_pairs={{0,8},{1,9},{2,10},{3,11},{4,12},{5,13},{6,14},{7,15},{8,0},{9,1},... | collective-permute-start | bytes 1572872 | tf_op jit(solution)/shard_map/ppermute | solution.py:317
  24.7 58.2 %collective-permute-start.6 = (bf16[256,2048]{1,0:T(8,128)(2,1)S(1)}, bf16[256,2048]{1,0:T(8,128)(2,1)}, u32[]{:S(2)}, u32[]{:S(2)}) collective-permute-start(bf16[256,2048]{1,0:T(8,128)(2,1)S(1)} %collective-permute-done.refs_0_), channel_id=1, source_target_pairs={{0,8},{1,9},{2,10},{3,11},{4,12},{5,13},{6,14},{7,15},{8,0},{9,1},... | collective-permute-start | bytes 3145736 | tf_op jit(solution)/shard_map/ppermute | solution.py:317
  45.8 37.0 %collective-permute-start.7 = (bf16[256,2048]{1,0:T(8,128)(2,1)S(1)}, bf16[256,2048]{1,0:T(8,128)(2,1)}, u32[]{:S(2)}, u32[]{:S(2)}) collective-permute-start(bf16[256,2048]{1,0:T(8,128)(2,1)S(1)} %collective-permute-done.3.refs_2_), channel_id=1, source_target_pairs={{0,8},{1,9},{2,10},{3,11},{4,12},{5,13},{6,14},{7,15},{8,0},{9,1},... | collective-permute-start | bytes 3145736 | tf_op jit(solution)/shard_map/ppermute | solution.py:317
  57.0 25.8 %collective-permute-start.5 = (bf16[256,2048]{1,0:T(8,128)(2,1)S(1)}, bf16[256,2048]{1,0:T(8,128)(2,1)}, u32[]{:S(2)}, u32[]{:S(2)}) collective-permute-start(bf16[256,2048]{1,0:T(8,128)(2,1)S(1)} %collective-permute-done.4.refs_6_), channel_id=1, source_target_pairs={{0,8},{1,9},{2,10},{3,11},{4,12},{5,13},{6,14},{7,15},{8,0},{9,1},... | collective-permute-start | bytes 3145736 | tf_op jit(solution)/shard_map/ppermute | solution.py:317
  57.6 25.3 %collective-permute-start.2 = (bf16[256,2048]{1,0:T(8,128)(2,1)}, bf16[256,2048]{1,0:T(8,128)(2,1)}, u32[]{:S(2)}, u32[]{:S(2)}) collective-permute-start(bf16[256,2048]{1,0:T(8,128)(2,1)} %collective-permute-done.1.refs_4_), channel_id=1, source_target_pairs={{0,8},{1,9},{2,10},{3,11},{4,12},{5,13},{6,14},{7,15},{8,0},{9,1},... | collective-permute-start | bytes 3145736 | tf_op jit(solution)/shard_map/ppermute | solution.py:317
  58.5 13.0 %all-to-all-start = ((bf16[8,128,256]{2,1,0:T(8,128)(2,1)}), bf16[8,128,256]{2,1,0:T(8,128)(2,1)}, u32[]{:S(2)}, u32[]{:S(2)}) async-start(bf16[8,128,256]{2,1,0:T(8,128)(2,1)} %broadcast_in_dim.3), calls=%async_computation | async-start | bytes 1048576 | tf_op jit(solution)/shard_map/all_to_all | solution.py:423
  90.2 9.4 %collective-permute-start.12 = (bf16[32,2048]{1,0:T(8,128)(2,1)S(1)}, bf16[32,2048]{1,0:T(8,128)(2,1)S(1)}, u32[]{:S(2)}, u32[]{:S(2)}) collective-permute-start(bf16[32,2048]{1,0:T(8,128)(2,1)S(1)} %step.10.refs_9_), channel_id=1, source_target_pairs={{0,4},{1,5},{2,6},{3,7},{4,0},{5,1},{6,2},{7,3},{8,12},{9,13},{10,... | collective-permute-start | bytes 393224 | tf_op jit(solution)/shard_map/ppermute | solution.py:317
  99.3 9.4 %collective-permute-start.13 = (bf16[32,2048]{1,0:T(8,128)(2,1)S(1)}, bf16[32,2048]{1,0:T(8,128)(2,1)S(1)}, u32[]{:S(2)}, u32[]{:S(2)}) collective-permute-start(bf16[32,2048]{1,0:T(8,128)(2,1)S(1)} %step.12.refs_9_), channel_id=1, source_target_pairs={{0,4},{1,5},{2,6},{3,7},{4,0},{5,1},{6,2},{7,3},{8,12},{9,13},{10,... | collective-permute-start | bytes 393224 | tf_op jit(solution)/shard_map/ppermute | solution.py:317
  105.8 9.4 %collective-permute-start.14 = (bf16[32,2048]{1,0:T(8,128)(2,1)S(1)}, bf16[32,2048]{1,0:T(8,128)(2,1)S(1)}, u32[]{:S(2)}, u32[]{:S(2)}) collective-permute-start(bf16[32,2048]{1,0:T(8,128)(2,1)S(1)} %get-tuple-element.73.refs_10_), channel_id=1, source_target_pairs={{0,4},{1,5},{2,6},{3,7},{4,0},{5,1},{6,2},{7,3},{8,12},{9,13},{10,... | collective-permute-start | bytes 393224 | tf_op jit(solution)/shard_map/ppermute | solution.py:317
  115.0 5.9 %collective-permute-start.15 = (bf16[32,2048]{1,0:T(8,128)(2,1)S(1)}, bf16[32,2048]{1,0:T(8,128)(2,1)S(1)}, u32[]{:S(2)}, u32[]{:S(2)}) collective-permute-start(bf16[32,2048]{1,0:T(8,128)(2,1)S(1)} %get-tuple-element.74.refs_12_), channel_id=1, source_target_pairs={{0,4},{1,5},{2,6},{3,7},{4,0},{5,1},{6,2},{7,3},{8,12},{9,13},{10,... | collective-permute-start | bytes 393224 | tf_op jit(solution)/shard_map/ppermute | solution.py:317
  150.3 6.3 %collective-permute-start.16 = (f32[128,128]{1,0:T(8,128)S(1)}, f32[128,128]{1,0:T(8,128)S(1)}, u32[]{:S(2)}, u32[]{:S(2)}) collective-permute-start(f32[128,128]{1,0:T(8,128)S(1)} %gram.4.part_ref), channel_id=1, source_target_pairs={{0,4},{1,5},{2,6},{3,7},{4,0},{5,1},{6,2},{7,3},{8,12},{9,13},{10,... | collective-permute-start | bytes 196616 | tf_op jit(solution)/shard_map/ppermute | solution.py:317
  165.4 11.0 %collective-permute-start.17 = (bf16[32,2048]{1,0:T(8,128)(2,1)S(1)}, bf16[32,2048]{1,0:T(8,128)(2,1)S(1)}, u32[]{:S(2)}, u32[]{:S(2)}) collective-permute-start(bf16[32,2048]{1,0:T(8,128)(2,1)S(1)} %step.15.refs_9_), channel_id=1, source_target_pairs={{0,4},{1,5},{2,6},{3,7},{4,0},{5,1},{6,2},{7,3},{8,12},{9,13},{10,... | collective-permute-start | bytes 393224 | tf_op jit(solution)/shard_map/ppermute | solution.py:317
  169.7 12.9 %collective-permute-start.18 = (bf16[32,2048]{1,0:T(8,128)(2,1)S(1)}, bf16[32,2048]{1,0:T(8,128)(2,1)S(1)}, u32[]{:S(2)}, u32[]{:S(2)}) collective-permute-start(bf16[32,2048]{1,0:T(8,128)(2,1)S(1)} %step.17.refs_9_), channel_id=1, source_target_pairs={{0,4},{1,5},{2,6},{3,7},{4,0},{5,1},{6,2},{7,3},{8,12},{9,13},{10,... | collective-permute-start | bytes 393224 | tf_op jit(solution)/shard_map/ppermute | solution.py:317
  182.5 9.2 %collective-permute-start.19 = (bf16[32,2048]{1,0:T(8,128)(2,1)S(1)}, bf16[32,2048]{1,0:T(8,128)(2,1)S(1)}, u32[]{:S(2)}, u32[]{:S(2)}) collective-permute-start(bf16[32,2048]{1,0:T(8,128)(2,1)S(1)} %get-tuple-element.81.refs_10_), channel_id=1, source_target_pairs={{0,4},{1,5},{2,6},{3,7},{4,0},{5,1},{6,2},{7,3},{8,12},{9,13},{10,... | collective-permute-start | bytes 393224 | tf_op jit(solution)/shard_map/ppermute | solution.py:317
  201.5 10.0 %all-to-all-start.3 = ((bf16[8,64,256]{2,1,0:T(8,128)(2,1)}), bf16[8,64,256]{2,1,0:T(8,128)(2,1)S(1)}, u32[]{:S(2)}, u32[]{:S(2)}) async-start(bf16[8,64,256]{2,1,0:T(8,128)(2,1)} %get-tuple-element.83), calls=%async_computation.3 | async-start | bytes 524288 | tf_op jit(solution)/shard_map/all_to_all | solution.py:496
  212.4 13.7 %all-to-all-start.4 = ((bf16[16,64,256]{2,1,0:T(8,128)(2,1)}), bf16[16,64,256]{2,1,0:T(8,128)(2,1)S(1)}, u32[]{:S(2)}, u32[]{:S(2)}) async-start(bf16[16,64,256]{2,1,0:T(8,128)(2,1)} %fan.3), calls=%async_computation.4 | async-start | bytes 1048576 | tf_op jit(solution)/shard_map/all_to_all | solution.py:497
  216.0 10.0 %collective-permute-start.23 = (f32[64,256]{1,0:T(8,128)S(1)}, f32[64,256]{1,0:T(8,128)S(1)}, u32[]{:S(2)}, u32[]{:S(2)}) collective-permute-start(f32[64,256]{1,0:T(8,128)S(1)} %pad_maximum_fusion.3), channel_id=1, source_target_pairs={{0,1},{1,0},{2,9},{3,8},{4,5},{5,4},{6,13},{7,12},{8,3},{9,2},{10,... | collective-permute-start | bytes 196616 | tf_op jit(solution)/shard_map/ppermute | solution.py:317
  217.9 8.1 %collective-permute-start.24 = (f32[64,256]{1,0:T(8,128)S(1)}, f32[64,256]{1,0:T(8,128)S(1)}, u32[]{:S(2)}, u32[]{:S(2)}) collective-permute-start(f32[64,256]{1,0:T(8,128)S(1)} %pad_maximum_fusion.4), channel_id=1, source_target_pairs={{0,2},{1,3},{2,10},{3,11},{4,6},{5,7},{6,14},{7,15},{8,0},{9,1},{1... | collective-permute-start | bytes 196616 | tf_op jit(solution)/shard_map/ppermute | solution.py:317
  219.1 6.9 %collective-permute-start.25 = (f32[64,256]{1,0:T(8,128)S(1)}, f32[64,256]{1,0:T(8,128)S(1)}, u32[]{:S(2)}, u32[]{:S(2)}) collective-permute-start(f32[64,256]{1,0:T(8,128)S(1)} %pad_maximum_fusion.5), channel_id=1, source_target_pairs={{0,3},{1,2},{2,11},{3,10},{4,7},{5,6},{6,15},{7,14},{8,1},{9,0},{1... | collective-permute-start | bytes 196616 | tf_op jit(solution)/shard_map/ppermute | solution.py:317
  219.2 6.8 %collective-permute-start.22 = (f32[64,256]{1,0:T(8,128)S(1)}, f32[64,256]{1,0:T(8,128)S(1)}, u32[]{:S(2)}, u32[]{:S(2)}) collective-permute-start(f32[64,256]{1,0:T(8,128)S(1)} %pad_maximum_fusion.2), channel_id=1, source_target_pairs={{0,0},{1,1},{2,8},{3,9},{4,4},{5,5},{6,12},{7,13},{8,2},{9,3},{10,... | collective-permute-start | bytes 196616 | tf_op jit(solution)/shard_map/ppermute | solution.py:317
  (10 other events, 50.8 us)
